TPU v7x, 256 devices: a whole 4x4x8 slice. The times are simulated.
256 devices in a mesh: slab: 8 (over z_lo, core), brick: 32 (over x, y, z_hi).
Axes of the slice: x: 4, y: 4, z: 8 (z_hi: 2, z_lo: 4; z = z_hi * 4 + z_lo), core: 2. Of those that a mesh axis runs over, the one named last changes fastest.
Arguments:
- features: float32 [64, 65536], P(None, ('slab', 'brick')), may hold values from -6 to 6
- cotangent: float32 [64, 65536], P(None, ('slab', 'brick')), may hold values from -6 to 6
- positions: float32 [3, 65536], P(None, ('slab', 'brick')), may hold values from 0 to 1, as said below
- edge_length: float32 [32, 65536], P(None, ('slab', 'brick')), may hold values from 1 to 6
- neighbors: int32 [32, 65536], P(None, ('slab', 'brick')), may hold values from 0 to 383
- send_map: int32 [4, 4096], P(None, ('slab', 'brick')), may hold values from 0 to 127
- atom_count: int32 [256], P(('slab', 'brick')), may hold values from 128 to 256, as said below
- short_weight: float32 [64, 64], replicated, may hold values from -0.75 to 0.75
- charge_weight: float32 [64, 64], replicated, may hold values from -0.75 to 0.75
- radial_weight: float32 [64, 8], replicated, may hold values from -2 to 2
Outputs:
- feature_grad: float32 [64, 65536], P(None, ('slab', 'brick'))
- short_grad: float32 [64, 64], replicated
- charge_grad: float32 [64, 64], replicated
- radial_grad: float32 [64, 8], replicated
Inputs may be any that keep to these rules, and one draw needn't show every extreme that they name: `neighbors`: Entries may repeat. `send_map`: row 2p + q, columns d * 16 to (d + 1) * 16 - 1 list the atoms of brick d in its boundary group (p, q), as indices within the brick; they may repeat. `atom_count`: some brick has exactly 256 live atoms and some exactly 128. `positions`: an atom of brick d = s * 32 + b has its first coordinate in [b / 32, (b + 1) / 32] and its third in [s / 8, (s + 1) / 8].
All inputs are finite; a program needn't handle non-finite values.
Results may differ from a plain program's by a relative error of at most 0.0003.
Values sent between devices are 32-bit elements; how exact they have to be, the bound alone decides.
No kernel may reach another device: no remote copies, remote signals or barrier semaphores. Data moves between devices by JAX's collectives and lax.ppermute only.
A program may use at most 64 MiB of HBM per device.

v0:
```python
import math

import jax
import jax.numpy as jnp
from jax import lax
from jax.sharding import PartitionSpec as P

KX = 8
KY = 16
KZ = 8


CUTOFF = 6.0
TWO_PI = 2.0 * math.pi
FULL_PRECISION = lax.Precision.HIGHEST


def padded_2(shard, sides, width):
    edges = {}
    for axis, dim in sides:
        size, length = (lax.axis_size(axis), shard.shape[dim])
        up = [(i, (i + 1) % size) for i in range(size)]
        last = lax.slice_in_dim(shard, length - width, length, axis=dim)
        first = lax.slice_in_dim(shard, 0, width, axis=dim)
        edges[dim] = (
            lax.ppermute(last, axis, up),
            lax.ppermute(first, axis, [(b, a) for a, b in up]),
        )
    done = []
    for _, dim in sides:
        low, high = edges[dim]
        around = [(width, width) if d in done else (0, 0) for d in range(shard.ndim)]
        shard = jnp.concatenate([jnp.pad(low, around), shard, jnp.pad(high, around)], axis=dim)
        done.append(dim)
    return shard


def extended_2(block, sides, width):
    for axis, dim in sides:
        count = lax.axis_size(axis)
        forward = [(i, i + 1) for i in range(count - 1)]
        forward.append((count - 1, 0))
        backward = [(target, source) for source, target in forward]
        low = lax.ppermute(
            lax.slice_in_dim(block, block.shape[dim] - width, None, axis=dim), axis, forward
        )
        high = lax.ppermute(lax.slice_in_dim(block, 0, width, axis=dim), axis, backward)
        block = jnp.concatenate([low, block, high], axis=dim)
    return block


def radial_terms(lengths, count):
    orders = jnp.arange(1, count + 1, dtype=jnp.int32).astype(jnp.float32)
    scaled_r = lengths / CUTOFF
    envelope = (1.0 - scaled_r * scaled_r) ** 2
    wave_terms = jnp.sin(orders[:, None, None] * (jnp.pi * scaled_r)[None])
    return math.sqrt(2.0 / CUTOFF) * wave_terms * (envelope / lengths)[None]


def mode_tables():
    counter = jnp.arange(KX * KY * KZ, dtype=jnp.int32)
    mode_one = (counter // (KY * KZ) - KX // 2).astype(jnp.float32)
    mode_two = (counter // KZ % KY - KY // 2).astype(jnp.float32)
    mode_three = (counter % KZ - KZ // 2).astype(jnp.float32)
    squared = mode_one * mode_one + mode_two * mode_two + mode_three * mode_three
    filter_values = jnp.where(
        squared > 0.0, jnp.exp(-squared / 16.0) / jnp.maximum(squared, 1.0), 0.0
    )
    return (mode_one, mode_two, mode_three, filter_values)


def phase_parts(modes, fraction):
    angle_values = TWO_PI * (
        modes[0][:, None] * fraction[0][None, :]
        + modes[1][:, None] * fraction[1][None, :]
        + modes[2][:, None] * fraction[2][None, :]
    )
    return (jnp.cos(angle_values), jnp.sin(angle_values))


def contract_last(left, right):
    return lax.dot_general(left, right, (((1,), (1,)), ((), ())), precision=FULL_PRECISION)


def contract_first(left, right):
    return lax.dot_general(left, right, (((0,), (0,)), ((), ())), precision=FULL_PRECISION)


def edge_terms(
    gathered, lengths, targets, keep_mask, tangent, radial_weight, own_count, live_count
):
    radial_values = radial_terms(lengths, radial_weight.shape[1])
    filter_edge = jnp.einsum("cm,meb->ceb", radial_weight, radial_values, precision=FULL_PRECISION)
    reach_mask = (
        jnp.logical_or(targets >= own_count, targets < live_count).astype(jnp.float32)
        * keep_mask[None, :]
    )
    weight = filter_edge * reach_mask[None]
    short_sum = jnp.sum(weight * gathered, axis=1)
    sigmoid_v = jax.nn.sigmoid(short_sum)
    upstream = tangent * sigmoid_v * (1.0 + short_sum * (1.0 - sigmoid_v)) * keep_mask[None, :]
    spread = weight * upstream[:, None, :]
    radial_part = jnp.einsum(
        "ceb,meb->cm",
        upstream[:, None, :] * gathered * reach_mask[None],
        radial_values,
        precision=FULL_PRECISION,
    )
    return (spread, radial_part)


def on_device(
    features,
    cotangent,
    positions,
    edge_length,
    neighbors,
    send_map,
    atom_count,
    short_weight,
    charge_weight,
    radial_weight,
):
    channels, atoms_dev = features.shape
    group_size = send_map.shape[1]
    atom_total = atoms_dev * lax.axis_size("slab") * lax.axis_size("brick")
    grad_scale = 1.0 / math.sqrt(atom_total)
    block_len = min(512, atoms_dev)
    block_count = atoms_dev // block_len
    live_count = atom_count[0]
    live_mask = (jnp.arange(atoms_dev, dtype=jnp.int32) < live_count).astype(jnp.float32)
    column_count = atoms_dev + 8 * group_size
    slot_count = neighbors.shape[0]
    outgoing = features[:, send_map].reshape(channels, 2, 2, group_size)
    padded = padded_2(outgoing, (("slab", 1), ("brick", 2)), 1)
    ghosts = jnp.concatenate(
        [padded[:, 0, 1:3], padded[:, 3, 1:3], padded[:, 1:3, 0], padded[:, 1:3, 3]], axis=1
    )
    extended = jnp.concatenate([features, ghosts.reshape(channels, 8 * group_size)], axis=1)
    projected = jnp.dot(short_weight, extended, precision=FULL_PRECISION)
    column_ids = jnp.arange(column_count, dtype=jnp.int32)

    def edge_step(step_index, running):
        grads_ext, radial_acc = running
        selector = (column_ids[:, None] == neighbors.reshape(-1)[None, :]).astype(jnp.float32)
        gathered = jnp.dot(projected, selector, precision=FULL_PRECISION).reshape(
            channels, slot_count, block_len
        )
        spread, radial_part = edge_terms(
            gathered,
            edge_length,
            neighbors,
            live_mask,
            cotangent,
            radial_weight,
            atoms_dev,
            live_count,
        )
        grads_ext = grads_ext + contract_last(spread.reshape(channels, -1), selector)
        return (grads_ext, radial_acc + radial_part)

    start_state = (
        jnp.zeros((channels, column_count), jnp.float32),
        jnp.zeros((channels, radial_weight.shape[1]), jnp.float32),
    )
    grads_ext, radial_acc = lax.fori_loop(0, block_count, edge_step, start_state)
    ghost_grads = grads_ext[:, atoms_dev:].reshape(channels, 8, group_size)
    slab_pad = extended_2(
        ghost_grads[:, 0:4].reshape(channels, 2, 2, group_size), (("slab", 1),), 1
    )
    brick_pad = extended_2(
        ghost_grads[:, 4:8].reshape(channels, 2, 2, group_size), (("brick", 1),), 1
    )
    returned = jnp.stack(
        [
            slab_pad[:, 0, 0] + brick_pad[:, 0, 0],
            slab_pad[:, 0, 1] + brick_pad[:, 3, 0],
            slab_pad[:, 3, 0] + brick_pad[:, 0, 1],
            slab_pad[:, 3, 1] + brick_pad[:, 3, 1],
        ],
        axis=1,
    )
    owned_grad = (
        grads_ext[:, :atoms_dev]
        .at[:, send_map.reshape(-1)]
        .add(returned.reshape(channels, 4 * group_size))
    )
    short_part = grad_scale * contract_last(owned_grad, features)
    radial_part = grad_scale * radial_acc
    modes = mode_tables()
    gated = cotangent * live_mask[None, :]
    masked_features = features * live_mask[None, :]
    wave_count = KX * KY * KZ

    def wave_step(step_index, running):
        cos_part, sin_part = phase_parts(modes, positions)
        updated = (
            running[0] + contract_last(cos_part, gated),
            running[1] + contract_last(sin_part, gated),
        )
        updated = updated + (
            running[2] + contract_last(cos_part, masked_features),
            running[3] + contract_last(sin_part, masked_features),
        )
        return updated

    zero_waves = jnp.zeros((wave_count, channels), jnp.float32)
    initial = (zero_waves,) * 4
    pieces = lax.fori_loop(0, block_count, wave_step, initial) + (short_part, radial_part)
    flat_all = jnp.concatenate([piece.reshape(-1) for piece in pieces])
    flat_sum = lax.psum(flat_all, ("slab", "brick"))
    summed = []
    position_now = 0
    for piece in pieces:
        summed.append(flat_sum[position_now : position_now + piece.size].reshape(piece.shape))
        position_now = position_now + piece.size
    weighted_real = summed[0] * (modes[3] * grad_scale)[:, None]
    weighted_imag = summed[1] * (modes[3] * grad_scale)[:, None]

    def charge_step(step_index, field):
        cos_part, sin_part = phase_parts(modes, positions)
        values = (
            contract_first(weighted_real, cos_part) + contract_first(weighted_imag, sin_part)
        ) * live_mask[None, :]
        return values

    charge_field = lax.fori_loop(
        0, block_count, charge_step, jnp.zeros((channels, atoms_dev), jnp.float32)
    )
    feature_grad = contract_first(short_weight, owned_grad) + contract_first(
        charge_weight, charge_field
    )
    charge_grad = grad_scale * (
        contract_first(weighted_real, summed[2]) + contract_first(weighted_imag, summed[3])
    )
    short_grad = summed[4]
    radial_grad = summed[5]
    return (feature_grad, short_grad, charge_grad, radial_grad)


def solution(mesh):
    placed = (
        P(None, ("slab", "brick")),
        P(None, ("slab", "brick")),
        P(None, ("slab", "brick")),
        P(None, ("slab", "brick")),
        P(None, ("slab", "brick")),
        P(None, ("slab", "brick")),
        P(("slab", "brick")),
        P(),
        P(),
        P(),
    )
    return jax.shard_map(
        on_device,
        mesh=mesh,
        in_specs=placed,
        out_specs=(P(None, ("slab", "brick")), P(), P(), P()),
        check_vma=False,
    )
```

profile of v0, /device:TPU:1, one launch (start us, length us, event | category | flops | bytes accessed | tf_op | source)
XLA Modules:
  0.0 366.6 jit_solution(1560045469015067074)
XLA Ops:
  7.2 0.7 compare_select_fusion
  8.0 0.9 copy.37
  9.0 0.6 gather_fusion
  9.6 3.1 collective-permute-start
  12.7 0.3 collective-permute-start.1
  13.0 5.7 %collective-permute-start.2 = (f32[64,2,1,16]{0,3,1,2:T(8,128)S(1)}, f32[64,2,1,16]{0,3,1,2:T(8,128)S(1)}, u32[]{:S(2)}, u32[]{:S(2)}) collective-permute-start(f32[64,2,1,16]{0,3,1,2:T(8,128)S(1)} %get-tuple-element.107), channel_id=1, source_target_pairs={{0,1},{1,2},{2,3},{3,4},{4,5},{5,6},{6,7},{7,8},{8,9},{9,10},{10,1... | collective-permute-start | bytes 24584 | tf_op jit(solution)/shard_map/ppermute | solution.py:26
  18.7 4.9 %collective-permute-start.3 = (f32[64,2,1,16]{0,3,2,1:T(8,128)S(1)}, f32[64,2,1,16]{0,3,2,1:T(8,128)S(1)}, u32[]{:S(2)}, u32[]{:S(2)}) collective-permute-start(f32[64,2,1,16]{0,3,2,1:T(8,128)S(1)} %get-tuple-element.108), channel_id=1, source_target_pairs={{1,0},{2,1},{3,2},{4,3},{5,4},{6,5},{7,6},{8,7},{9,8},{10,9},{11,1... | collective-permute-start | bytes 24584 | tf_op jit(solution)/shard_map/ppermute | solution.py:27
  23.6 0.8 reshape.325
  25.1 0.8 fusion.136
  25.9 5.4 %fusion.24 = f32[1024,64]{1,0:T(8,128)S(1)} fusion(f32[256]{0:T(256)S(1)} %bitcast.102, f32[1024]{0:T(1024)S(1)} %fusion.118, f32[256]{0:T(256)S(1)} %bitcast.108, f32[1024]{0:T(1024)S(1)} %get-tuple-element.131, f32[256]{0:T(256)S(1)} %bitcast.96, f32[1024]{0:T(1024)S(1)} %get-tuple-element.130, f32[64,256]{1,0:T(8,128)} %param.10, ...), kind=kOutput, calls=%fused_computation.29 | convolution fusion | flops 202915840 | bytes 344064 | tf_op jit(solution)/shard_map/while/body/eval_jaxpr/dot_general | solution.py:82
  31.3 4.7 %fusion.29 = f32[1024,64]{1,0:T(8,128)S(1)} fusion(f32[256]{0:T(256)S(1)} %bitcast.103, f32[1024]{0:T(1024)S(1)} %fusion.118, f32[256]{0:T(256)S(1)} %bitcast.109, f32[1024]{0:T(1024)S(1)} %get-tuple-element.131, f32[256]{0:T(256)S(1)} %bitcast.97, f32[1024]{0:T(1024)S(1)} %get-tuple-element.130, f32[64,256]{1,0:T(8,128)S(1)} %copy-done.2, ...), kind=kOutput, calls=%fused_computation.31 | convolution fusion | flops 202915840 | bytes 344064 | tf_op jit(solution)/shard_map/while/body/eval_jaxpr/dot_general | solution.py:82
  36.0 5.1 %fusion.31 = f32[1024,64]{1,0:T(8,128)S(1)} fusion(f32[256]{0:T(256)S(1)} %bitcast.104, f32[1024]{0:T(1024)S(1)} %fusion.118, f32[256]{0:T(256)S(1)} %bitcast.110, f32[1024]{0:T(1024)S(1)} %get-tuple-element.131, f32[256]{0:T(256)S(1)} %bitcast.98, f32[1024]{0:T(1024)S(1)} %get-tuple-element.130, f32[64,256]{1,0:T(8,128)S(1)} %copy-done.6, ...), kind=kOutput, calls=%fused_computation.32 | convolution fusion | flops 202915840 | bytes 344064 | tf_op jit(solution)/shard_map/while/body/eval_jaxpr/dot_general | solution.py:82
  41.1 4.6 %fusion.26 = f32[1024,64]{1,0:T(8,128)S(1)} fusion(f32[256]{0:T(256)S(1)} %bitcast.105, f32[1024]{0:T(1024)S(1)} %fusion.118, f32[256]{0:T(256)S(1)} %bitcast.111, f32[1024]{0:T(1024)S(1)} %get-tuple-element.131, f32[256]{0:T(256)S(1)} %bitcast.99, f32[1024]{0:T(1024)S(1)} %get-tuple-element.130, f32[64,256]{1,0:T(8,128)S(1)} %copy-done.6, ...), kind=kOutput, calls=%fused_computation.30 | convolution fusion | flops 202915840 | bytes 344064 | tf_op jit(solution)/shard_map/while/body/eval_jaxpr/dot_general | solution.py:82
  45.7 0.5 fusion.123
  46.4 0.1 reshape.333
  46.9 0.2 copy-done.3
  47.4 0.2 fusion.92
  47.6 5.0 %fusion.1 = f32[64,8192]{1,0:T(8,128)S(1)} fusion(f32[384,64]{0,1:T(8,128)S(1)} %fusion.92, s32[8192]{0:T(1024)S(1)} %bitcast.90), kind=kOutput, calls=%fused_computation.4 | convolution fusion | flops 2419064832 | bytes 2228224 | tf_op jit(solution)/shard_map/while/body/eval_jaxpr/dot_general | solution.py:146
  52.6 2.7 fusion.4
  55.4 0.3 fusion.8
  55.7 0.2 copy.57
  55.9 6.4 %fusion = f32[64,384]{1,0:T(8,128)S(1)} fusion(f32[64,8192]{1,0:T(8,128)S(1)} %bitcast.81, s32[8192]{0:T(1024)S(1)} %bitcast.91), kind=kOutput, calls=%fused_computation.3 | convolution fusion | flops 2419064832 | bytes 2228224 | tf_op jit(solution)/shard_map/while/body/eval_jaxpr/dot_general | solution.py:82
  62.4 0.6 copy-done.4
  63.2 0.6 fusion.133
  63.8 1.9 collective-permute-start.4
  65.7 1.2 collective-permute-start.7
  66.9 1.0 collective-permute-start.5
  67.9 8.6 %collective-permute-start.6 = (f32[64,1,2,16]{0,3,2,1:T(8,128)S(1)}, f32[64,1,2,16]{0,3,2,1:T(8,128)S(1)}, u32[]{:S(2)}, u32[]{:S(2)}) collective-permute-start(f32[64,1,2,16]{0,3,2,1:T(8,128)S(1)} %get-tuple-element.95), channel_id=1, source_target_pairs={{1,0},{2,1},{3,2},{4,3},{5,4},{6,5},{7,6},{8,7},{9,8},{10,9},{11,1... | collective-permute-start | bytes 24584 | tf_op jit(solution)/shard_map/ppermute | solution.py:47
  76.5 3.3 fusion.16
  80.2 1.3 scatter_fusion
  81.5 0.4 convolution_multiply_fusion
  82.0 1.0 copy-done.1
  83.0 0.3 fusion.137
  83.3 258.1 %all-reduce.2.cloned.1.call-done = f32[266752]{0:T(1024)} async-done(((f32[266752]{0:T(1024)}), f32[266752]{0:T(1024)}) %all-reduce.2.cloned.1.call-update) | async-done | bytes 1067024 | tf_op jit(solution)/shard_map/psum | solution.py:211
  341.4 0.7 slice.207
  342.1 0.7 reshape.338
  342.8 0.7 slice.210
  343.6 0.7 copy.50
  344.2 1.3 fusion.131
  345.6 0.1 reshape.340
  345.7 0.1 reshape.337
  345.9 0.1 reshape.336
  346.0 0.1 reshape.339
  346.2 4.7 %fusion.22 = f32[64,256]{1,0:T(8,128)S(1)} fusion(f32[256]{0:T(256)S(1)} %bitcast.106, f32[1024]{0:T(1024)S(1)} %fusion.118, f32[256]{0:T(256)S(1)} %bitcast.112, f32[1024]{0:T(1024)S(1)} %copy-done.12, f32[256]{0:T(256)S(1)} %bitcast.100, f32[1024]{0:T(1024)S(1)} %copy-done.10, f32[1024,64]{1,0:T(8,128)S(1)} %reshape.336, f32[1024]{0:T(1024)S(1)} %select_multiply_fusion), kind=kOutput, calls=%fused_computation.28 | convolution fusion | flops 202964992 | bytes 347136 | tf_op jit(solution)/shard_map/while/body/eval_jaxpr/dot_general | solution.py:86
  350.9 1.2 fusion.78
  352.1 4.7 %fusion.11 = f32[64,256]{1,0:T(8,128)S(1)} fusion(f32[64,256]{1,0:T(8,128)S(1)} %fusion.22, f32[256]{0:T(256)S(1)} %bitcast.107, f32[1024]{0:T(1024)S(1)} %fusion.118, f32[256]{0:T(256)S(1)} %bitcast.113, f32[1024]{0:T(1024)S(1)} %copy-done.12, f32[256]{0:T(256)S(1)} %bitcast.101, f32[1024]{0:T(1024)S(1)} %copy-done.10, f32[1024,64]{1,0:T(8,128)S(1)} %reshape.337, ...), kind=kOutput, calls=%fused_computation.18 | convolution fusion | flops 202997760 | bytes 413696 | tf_op jit(solution)/shard_map/while/body/eval_jaxpr/dot_general | solution.py:86
  356.8 1.8 fusion.12
  358.6 0.9 fusion.10
  (84 shorter events, 1.6 us)
Async XLA Ops:
  7.2 40.2 %copy-start = (f32[64,64]{1,0:T(8,128)S(1)}, f32[64,64]{1,0:T(8,128)}, u32[]{:S(2)}) copy-start(f32[64,64]{1,0:T(8,128)} %param.17) | copy-start | bytes 49156
  7.2 24.2 %copy-start.2 = (f32[64,256]{1,0:T(8,128)S(1)}, f32[64,256]{1,0:T(8,128)}, u32[]{:S(2)}) copy-start(f32[64,256]{1,0:T(8,128)} %param.10) | copy-start | bytes 196612
  7.2 334.2 %all-reduce.2.cloned.1.call-start = ((), (), s32[]{:S(2)}) async-start(), calls=%async_computation | async-start | bytes 2138112 | tf_op jit(solution)/shard_map/psum | solution.py:211
  9.6 26.4 %copy-start.6 = (f32[64,256]{1,0:T(8,128)S(1)}, f32[64,256]{1,0:T(8,128)}, u32[]{:S(2)}) copy-start(f32[64,256]{1,0:T(8,128)} %param.11) | copy-start | bytes 196612
  9.6 37.7 %collective-permute-start = (f32[64,1,2,16]{0,3,2,1:T(8,128)S(1)}, f32[64,1,2,16]{0,3,2,1:T(8,128)S(1)}, u32[]{:S(2)}, u32[]{:S(2)}) collective-permute-start(f32[64,1,2,16]{0,3,2,1:T(8,128)S(1)} %get-tuple-element.96), channel_id=1, source_target_pairs={{0,32},{32,64},{64,96},{96,128},{128,160},{160,192},{192,224},{224... | collective-permute-start | bytes 24584 | tf_op jit(solution)/shard_map/ppermute | solution.py:26
  12.7 34.6 %collective-permute-start.1 = (f32[64,1,2,16]{0,3,2,1:T(8,128)S(1)}, f32[64,1,2,16]{0,3,2,1:T(8,128)S(1)}, u32[]{:S(2)}, u32[]{:S(2)}) collective-permute-start(f32[64,1,2,16]{0,3,2,1:T(8,128)S(1)} %get-tuple-element.106), channel_id=1, source_target_pairs={{32,0},{64,32},{96,64},{128,96},{160,128},{192,160},{224,192},{0,2... | collective-permute-start | bytes 24584 | tf_op jit(solution)/shard_map/ppermute | solution.py:27
  13.0 34.3 %collective-permute-start.2 = (f32[64,2,1,16]{0,3,1,2:T(8,128)S(1)}, f32[64,2,1,16]{0,3,1,2:T(8,128)S(1)}, u32[]{:S(2)}, u32[]{:S(2)}) collective-permute-start(f32[64,2,1,16]{0,3,1,2:T(8,128)S(1)} %get-tuple-element.107), channel_id=1, source_target_pairs={{0,1},{1,2},{2,3},{3,4},{4,5},{5,6},{6,7},{7,8},{8,9},{9,10},{10,1... | collective-permute-start | bytes 24584 | tf_op jit(solution)/shard_map/ppermute | solution.py:26
  18.7 28.6 %collective-permute-start.3 = (f32[64,2,1,16]{0,3,2,1:T(8,128)S(1)}, f32[64,2,1,16]{0,3,2,1:T(8,128)S(1)}, u32[]{:S(2)}, u32[]{:S(2)}) collective-permute-start(f32[64,2,1,16]{0,3,2,1:T(8,128)S(1)} %get-tuple-element.108), channel_id=1, source_target_pairs={{1,0},{2,1},{3,2},{4,3},{5,4},{6,5},{7,6},{8,7},{9,8},{10,9},{11,1... | collective-permute-start | bytes 24584 | tf_op jit(solution)/shard_map/ppermute | solution.py:27
  24.4 16.7 %copy-start.9 = (f32[1024]{0:T(1024)}, f32[1024]{0:T(1024)S(1)}, u32[]{:S(2)}) copy-start(f32[1024]{0:T(1024)S(1)} %get-tuple-element.130) | copy-start | bytes 12292
  24.4 16.7 %copy-start.11 = (f32[1024]{0:T(1024)}, f32[1024]{0:T(1024)S(1)}, u32[]{:S(2)}) copy-start(f32[1024]{0:T(1024)S(1)} %get-tuple-element.131) | copy-start | bytes 12292
  25.9 15.2 %copy-start.15 = (f32[1,256]{1,0:T(1,128)}, f32[1,256]{1,0:T(1,128)S(1)}, u32[]{:S(2)}) copy-start(f32[1,256]{1,0:T(1,128)S(1)} %get-tuple-element.124) | copy-start | bytes 3076
  25.9 15.2 %copy-start.17 = (f32[1,256]{1,0:T(1,128)}, f32[1,256]{1,0:T(1,128)S(1)}, u32[]{:S(2)}) copy-start(f32[1,256]{1,0:T(1,128)S(1)} %get-tuple-element.125) | copy-start | bytes 3076
  25.9 15.2 %copy-start.19 = (f32[1,256]{1,0:T(1,128)}, f32[1,256]{1,0:T(1,128)S(1)}, u32[]{:S(2)}) copy-start(f32[1,256]{1,0:T(1,128)S(1)} %get-tuple-element.126) | copy-start | bytes 3076
  46.4 0.8 copy-start.3
  46.4 0.8 copy-start.7
  47.2 8.5 %copy-start.14 = (f32[8]{0:T(128)}, f32[8]{0:T(128)S(1)}, u32[]{:S(2)}) copy-start(f32[8]{0:T(128)S(1)} %add_convert_fusion) | copy-start | bytes 100
  47.4 5.2 %copy-start.13 = (f32[64,8]{0,1:T(8,128)S(1)}, f32[64,8]{0,1:T(8,128)}, u32[]{:S(2)}) copy-start(f32[64,8]{0,1:T(8,128)} %param.19) | copy-start | bytes 6148
  62.4 0.6 copy-start.4
  63.1 16.7 %copy-start.5 = (f32[64,384]{1,0:T(8,128)S(1)}, f32[64,384]{1,0:T(8,128)}, u32[]{:S(2)}) copy-start(f32[64,384]{1,0:T(8,128)} %copy-done.4) | copy-start | bytes 294916
  63.8 16.4 %collective-permute-start.4 = (f32[64,1,2,16]{0,3,2,1:T(8,128)}, f32[64,1,2,16]{0,3,2,1:T(8,128)S(1)}, u32[]{:S(2)}, u32[]{:S(2)}) collective-permute-start(f32[64,1,2,16]{0,3,2,1:T(8,128)} %get-tuple-element.92), channel_id=1, source_target_pairs={{0,32},{32,64},{64,96},{96,128},{128,160},{160,192},{192,224},{224... | collective-permute-start | bytes 24584 | tf_op jit(solution)/shard_map/ppermute | solution.py:44
  65.7 14.5 %collective-permute-start.7 = (f32[64,1,2,16]{0,3,2,1:T(8,128)S(1)}, f32[64,1,2,16]{0,3,2,1:T(8,128)S(1)}, u32[]{:S(2)}, u32[]{:S(2)}) collective-permute-start(f32[64,1,2,16]{0,3,2,1:T(8,128)S(1)} %get-tuple-element.93), channel_id=1, source_target_pairs={{32,0},{64,32},{96,64},{128,96},{160,128},{192,160},{224,192},{0,2... | collective-permute-start | bytes 24584 | tf_op jit(solution)/shard_map/ppermute | solution.py:47
  66.9 13.2 %collective-permute-start.5 = (f32[64,1,2,16]{0,3,2,1:T(8,128)S(1)}, f32[64,1,2,16]{0,3,2,1:T(8,128)S(1)}, u32[]{:S(2)}, u32[]{:S(2)}) collective-permute-start(f32[64,1,2,16]{0,3,2,1:T(8,128)S(1)} %get-tuple-element.94), channel_id=1, source_target_pairs={{0,1},{1,2},{2,3},{3,4},{4,5},{5,6},{6,7},{7,8},{8,9},{9,10},{10,1... | collective-permute-start | bytes 24584 | tf_op jit(solution)/shard_map/ppermute | solution.py:44
  67.9 12.3 %collective-permute-start.6 = (f32[64,1,2,16]{0,3,2,1:T(8,128)S(1)}, f32[64,1,2,16]{0,3,2,1:T(8,128)S(1)}, u32[]{:S(2)}, u32[]{:S(2)}) collective-permute-start(f32[64,1,2,16]{0,3,2,1:T(8,128)S(1)} %get-tuple-element.95), channel_id=1, source_target_pairs={{1,0},{2,1},{3,2},{4,3},{5,4},{6,5},{7,6},{8,7},{9,8},{10,9},{11,1... | collective-permute-start | bytes 24584 | tf_op jit(solution)/shard_map/ppermute | solution.py:47
  82.0 1.0 copy-start.1
  345.5 0.7 copy-start.10
  345.5 0.7 copy-start.12
  345.5 0.7 copy-start.16
  345.5 0.7 copy-start.18
  345.6 0.7 copy-start.20
  350.9 7.7 %copy-start.8 = (f32[64,64]{1,0:T(8,128)S(1)}, f32[64,64]{1,0:T(8,128)}, u32[]{:S(2)}) copy-start(f32[64,64]{1,0:T(8,128)} %param.18) | copy-start | bytes 49156
Sparse Core Ops, SparseCore 0:
  83.1 258.2 all-reduce.1
where the time goes:
time: 370 us; the launch traced here: 367 us
  waiting for transfers between devices  258 us (70%)
  matrix products  51.4 us (14%)
  starting transfers between devices  26.8 us (7%)
  between operations  15.5 us (4%)
  local copies, waits for them, and re-layouts  11.8 us (3%)
    psum x1, waiting for transfers between devices, on_device(): flat_sum = lax.psum(flat_all, ('slab', 'brick'))  258 us
    dot_general x6, matrix products, contract_last(): lax.dot_general(left, right, (((1,), (1,)), ((), ())), precision=FULL_PRE...  26.6 us
    dot_general x6, matrix products, contract_first(): lax.dot_general(left, right, (((0,), (0,)), ((), ())), precision=FULL_PRE...  13.5 us
    ppermute x2, starting transfers between devices, extended_2(): lax.ppermute(lax.slice_in_dim(block, 0, width, axis=dim), axis, backward)  9.86 us
    ppermute x2, starting transfers between devices, padded_2(): lax.ppermute(last, axis, up)  8.81 us
  transfers between devices with their start and end apart: 9, of which 1 were waited for; matrix products, arithmetic and copies ran while one was open for 7% of the time, Pallas kernels for 0%

commit v1 on v0

v1 whole, which is shorter than its diff:
```python
import math

import jax
import jax.numpy as jnp
import numpy as np
from jax import lax
from jax.experimental import pallas as pl
from jax.experimental.pallas import tpu as pltpu
from jax.sharding import PartitionSpec as P

KX = 8
KY = 16
KZ = 8
CUTOFF = 6.0
HALF_ROWS = 64
CHUNKS = 11
F32 = jnp.float32
BF16 = jnp.bfloat16
FULL_PRECISION = lax.Precision.HIGHEST
BOTH = ("slab", "brick")


def slot_modes(chunk, i, j):
    if chunk < 8:
        return (chunk - 4, j - 8, i - 4)
    if chunk == 8:
        return (4, j - 8, i - 3)
    if chunk == 9:
        return (i - 3, j - 8, 4)
    return (i - 4, 0, j - 4)


def weight_table(scale):
    where = {}
    for chunk in range(CHUNKS):
        for i in range(8):
            for j in range(8):
                where.setdefault(slot_modes(chunk, i, j), (chunk, i * 8 + j))
    table = np.zeros((CHUNKS, HALF_ROWS), np.float64)
    for k in range(KX * KY * KZ):
        n = (k // (KY * KZ) - KX // 2, k // KZ % KY - KY // 2, k % KZ - KZ // 2)
        squared = float(n[0] ** 2 + n[1] ** 2 + n[2] ** 2)
        if squared == 0.0:
            continue
        slot = where.get(n)
        if slot is None or n[1] > 0:
            slot = where[(-n[0], -n[1], -n[2])]
        table[slot] += math.exp(-squared / 16.0) / squared
    wide = np.ones((CHUNKS * HALF_ROWS, 128), np.float32)
    wide[:, :64] = (table.reshape(-1, 1) * scale).astype(np.float32)
    return wide


def split(value):
    high = value.astype(BF16)
    return high, (value - high.astype(F32)).astype(BF16)


def dot(left, right, contract=((1,), (0,))):
    return lax.dot_general(left, right, (contract, ((), ())), preferred_element_type=F32)


def dot_full(left, right, contract=((1,), (0,))):
    return lax.dot_general(
        left, right, (contract, ((), ())), precision=FULL_PRECISION, preferred_element_type=F32
    )


def sin_turns(turns):
    turns = turns - jnp.floor(turns + 0.5)
    folded = jnp.where(turns > 0.25, 0.5 - turns, jnp.where(turns < -0.25, -0.5 - turns, turns))
    angle = folded * (2.0 * math.pi)
    square = angle * angle
    poly = -1.0 / 39916800.0
    for divisor in (362880.0, -5040.0, 120.0, -6.0):
        poly = poly * square + 1.0 / divisor
    return angle + angle * square * poly


def wave_factors(turns, first):
    order = lax.broadcasted_iota(jnp.int32, (8, turns.shape[1]), 0) + first
    phase = order.astype(F32) * turns
    phase = phase - jnp.floor(phase + 0.5)
    return sin_turns(phase + 0.25), sin_turns(phase)


def complex_product(left, right):
    return (
        left[0] * right[0] - left[1] * right[1],
        left[0] * right[1] + left[1] * right[0],
    )


def chunk_waves(positions):
    one = wave_factors(positions[0:1], -4)
    one_up = wave_factors(positions[0:1], -3)
    two = wave_factors(positions[1:2], -8)
    three = wave_factors(positions[2:3], -4)
    three_up = wave_factors(positions[2:3], -3)

    def row(pair, index):
        return pair[0][index : index + 1], pair[1][index : index + 1]

    def chunk(number):
        if number < 8:
            outer, inner = complex_product(row(one, number), three), two
        elif number == 8:
            outer, inner = complex_product(row(one_up, 7), three_up), two
        elif number == 9:
            outer, inner = complex_product(row(three_up, 7), one_up), two
        else:
            outer, inner = one, three
        cos_part, sin_part = complex_product(
            (outer[0][:, None, :], outer[1][:, None, :]),
            (inner[0][None, :, :], inner[1][None, :, :]),
        )
        atoms = positions.shape[1]
        return jnp.concatenate(
            [cos_part.reshape(HALF_ROWS, atoms), sin_part.reshape(HALF_ROWS, atoms)], axis=0
        )

    return chunk


def live_row(count_ref, atoms):
    index = lax.broadcasted_iota(jnp.int32, (1, atoms), 1)
    return (index < count_ref[0]).astype(F32)


def send_selector(send_map, atoms, transposed=False):
    size = send_map.shape[1]
    spread = (
        lax.broadcasted_iota(jnp.int32, (size, 128), 1) % size
        == lax.broadcasted_iota(jnp.int32, (size, 128), 0)
    ).astype(F32)
    tiled = dot_full(send_map.astype(F32), spread)
    place = lax.broadcasted_iota(jnp.int32, (1, 128), 1) // size
    wanted = jnp.zeros((1, 128), F32)
    for slot, group in enumerate((2, 3, 0, 1, 1, 3, 0, 2)):
        wanted = jnp.where(place == slot, tiled[group : group + 1], wanted)
    atom = lax.broadcasted_iota(jnp.int32, (atoms, 128), 0).astype(F32)
    return (atom == jnp.round(wanted)).astype(F32).astype(BF16)


def pick_lanes(refs):
    place = lax.broadcasted_iota(jnp.int32, (64, 128), 1) // 32
    value = refs[3][...]
    for slot in range(3):
        value = jnp.where(place == slot, refs[slot][...], value)
    return value


def send_kernel(features_ref, map_ref, out_ref):
    features = features_ref[...]
    selector = send_selector(map_ref[...], features.shape[1])
    high, rest = split(features)
    middle, low = split(features - high.astype(F32))
    out_ref[...] = dot(high, selector) + (dot(middle, selector) + dot(low, selector))


def wave_kernel(count_ref, positions_ref, cotangent_ref, features_ref, table_ref, out_ref):
    chunk = chunk_waves(positions_ref[...])
    live = live_row(count_ref, positions_ref.shape[1])
    both = jnp.concatenate([cotangent_ref[...] * live, features_ref[...] * live], axis=0)
    high, low = split(both)
    stacked = jnp.concatenate([high, low], axis=0)
    for number in range(CHUNKS):
        wave_high, wave_low = split(chunk(number))
        part = dot(wave_high, stacked, ((1,), (1,)))
        part = part[:, :128] + part[:, 128:] + dot(wave_low, high, ((1,), (1,)))
        weight = table_ref[number * HALF_ROWS : (number + 1) * HALF_ROWS, :]
        base = number * 2 * HALF_ROWS
        out_ref[base : base + HALF_ROWS, :] = part[:HALF_ROWS] * weight
        out_ref[base + HALF_ROWS : base + 2 * HALF_ROWS, :] = part[HALF_ROWS:] * weight
    done = CHUNKS * 2 * HALF_ROWS
    out_ref[done:, :] = jnp.zeros((out_ref.shape[0] - done, 128), F32)


def edge_kernel(
    count_ref,
    features_ref,
    up_ref,
    down_ref,
    right_ref,
    left_ref,
    cotangent_ref,
    length_ref,
    neighbor_ref,
    short_ref,
    radial_ref,
    own_ref,
    ghost_ref,
    small_ref,
    basis_ref,
    selector_ref,
    gathered_ref,
    weight_ref,
):
    channels, atoms = features_ref.shape
    slots = length_ref.shape[0]
    columns = atoms + 128
    scale = small_ref.shape[0]
    extended = jnp.concatenate(
        [features_ref[...], pick_lanes((up_ref, down_ref, right_ref, left_ref))], axis=1
    )
    projected = jnp.concatenate(split(dot_full(short_ref[...], extended)), axis=0)
    live = live_row(count_ref, atoms)

    lengths = length_ref[...]
    targets = neighbor_ref[...]
    reach = jnp.where(jnp.logical_or(targets >= atoms, targets < count_ref[0]), live, 0.0)
    ratio = lengths * (1.0 / CUTOFF)
    envelope = 1.0 - ratio * ratio
    envelope = math.sqrt(2.0 / CUTOFF) * envelope * envelope / lengths * reach
    order = lax.broadcasted_iota(jnp.int32, (slots, 8, atoms), 1).astype(F32) + 1.0
    basis = sin_turns(order * (0.5 * ratio)[:, None, :]) * envelope[:, None, :]
    basis_ref[...] = basis.reshape(slots * 8, atoms)

    radial_high, radial_low = split(radial_ref[...])
    radial_wide = jnp.concatenate([radial_high, radial_high, radial_low], axis=1)
    column = lax.broadcasted_iota(jnp.int32, (columns, atoms), 0)

    def basis_of(slot):
        return split(basis_ref[pl.ds(pl.multiple_of(slot * 8, 8), 8), :])

    def forward(slot, total):
        selector = (column == neighbor_ref[pl.ds(slot, 1), :]).astype(F32).astype(BF16)
        selector_ref[slot] = selector
        found = dot(projected, selector)
        gathered = found[:channels] + found[channels:]
        basis_high, basis_low = basis_of(slot)
        weight = dot(radial_wide, jnp.concatenate([basis_high, basis_low, basis_high], axis=0))
        gathered_ref[slot] = gathered
        weight_ref[slot] = weight
        return total + weight * gathered

    short_sum = lax.fori_loop(0, slots, forward, jnp.zeros((channels, atoms), F32), unroll=2)
    gate = jax.nn.sigmoid(short_sum)
    upstream = cotangent_ref[...] * gate * (1.0 + short_sum * (1.0 - gate)) * live

    def backward(slot, running):
        grads, radial = running
        spread = jnp.concatenate(split(weight_ref[slot] * upstream), axis=0)
        grads = grads + dot(spread, selector_ref[slot], ((1,), (1,)))
        pulled = jnp.concatenate(split(gathered_ref[slot] * upstream), axis=0)
        pair = jnp.concatenate(basis_of(slot), axis=0)
        return grads, radial + dot(pulled, pair, ((1,), (1,)))

    grads, radial = lax.fori_loop(
        0,
        slots,
        backward,
        (jnp.zeros((2 * channels, columns), F32), jnp.zeros((2 * channels, 16), F32)),
        unroll=2,
    )
    grads = grads[:channels] + grads[channels:]
    radial = radial[:channels] + radial[channels:]
    radial = radial[:, :8] + radial[:, 8:]
    own_ref[...] = grads[:, :atoms]
    ghost_ref[...] = grads[:, atoms:]
    factor = 1.0 / math.sqrt(atoms * scale)
    short_part = dot_full(grads, extended, ((1,), (1,))) * factor
    rows = small_ref.shape[0] // channels
    small_ref[...] = jnp.zeros(small_ref.shape, F32)
    packed = jnp.concatenate(
        [short_part, radial * factor, jnp.zeros((channels, 128 - channels - 8), F32)], axis=1
    )
    small_ref[pl.ds(0, channels, stride=rows), :] = packed


def return_kernel(up_ref, down_ref, right_ref, left_ref, own_ref, map_ref, short_ref, out_ref):
    back = pick_lanes((up_ref, down_ref, right_ref, left_ref))
    selector = send_selector(map_ref[...], own_ref.shape[1])
    high, low = split(back)
    owned = own_ref[...] + (
        dot(high, selector, ((1,), (1,))) + dot(low, selector, ((1,), (1,)))
    )
    out_ref[...] = dot_full(short_ref[...], owned, ((0,), (0,)))


def charge_kernel(
    count_ref, positions_ref, waves_ref, partial_ref, charge_ref, grad_ref, out_ref, *, factor
):
    chunk = chunk_waves(positions_ref[...])
    channels, atoms = partial_ref.shape
    field = jnp.zeros((2 * channels, atoms), F32)
    grad = jnp.zeros((2 * channels, 128), F32)
    for number in range(CHUNKS):
        base = number * 2 * HALF_ROWS
        block = waves_ref[base : base + 2 * HALF_ROWS, :]
        turned = block.T[:channels]
        turned_high, turned_low = split(turned)
        turned = jnp.concatenate([turned_high, turned_low], axis=0)
        block_high, block_low = split(block)
        wave_high, wave_low = split(chunk(number))
        field = field + dot(turned, wave_high)
        grad = grad + dot(turned, block_high)
        extra = dot(turned_high, jnp.concatenate([wave_low, block_low], axis=1))
        field = field + jnp.concatenate([extra[:, :atoms], jnp.zeros((channels, atoms), F32)], axis=0)
        grad = grad + jnp.concatenate([extra[:, atoms:], jnp.zeros((channels, 128), F32)], axis=0)
    field = (field[:channels] + field[channels:]) * live_row(count_ref, atoms)
    grad = grad[:channels] + grad[channels:]
    grad_ref[...] = grad[:, channels : 2 * channels] * factor
    out_ref[...] = partial_ref[...] + dot_full(charge_ref[...], field, ((0,), (0,)))


def vmem(count):
    return [pl.BlockSpec(memory_space=pltpu.VMEM)] * count


def scalar_first(count):
    return [pl.BlockSpec(memory_space=pltpu.SMEM)] + vmem(count)


def shape(*dims):
    return jax.ShapeDtypeStruct(dims, F32)


def shifted(value, axis, step):
    size = lax.axis_size(axis)
    return lax.ppermute(value, axis, [(i, (i + step) % size) for i in range(size)])


def exchange(value):
    return lax.all_to_all(value, BOTH, 0, 0, tiled=True)


def on_device(
    features,
    cotangent,
    positions,
    edge_length,
    neighbors,
    send_map,
    atom_count,
    short_weight,
    charge_weight,
    radial_weight,
):
    channels, atoms = features.shape
    slots = neighbors.shape[0]
    devices = lax.axis_size("slab") * lax.axis_size("brick")
    factor = 1.0 / math.sqrt(atoms * devices)
    wave_rows = -(-CHUNKS * 2 * HALF_ROWS // devices)
    total_rows = wave_rows * devices

    outgoing = pl.pallas_call(
        send_kernel, out_shape=shape(channels, 128), in_specs=vmem(2), out_specs=vmem(1)[0]
    )(features, send_map)
    arrived = (
        shifted(outgoing, "slab", 1),
        shifted(outgoing, "slab", -1),
        shifted(outgoing, "brick", 1),
        shifted(outgoing, "brick", -1),
    )
    waves = pl.pallas_call(
        wave_kernel,
        out_shape=shape(total_rows, 128),
        in_specs=scalar_first(4),
        out_specs=vmem(1)[0],
    )(atom_count, positions, cotangent, features, jnp.asarray(weight_table(factor)))
    pieces = exchange(waves.reshape(devices, wave_rows, 128))
    mine = jnp.sum(pieces, axis=0)
    everyone = exchange(jnp.broadcast_to(mine[None], (devices, wave_rows, 128)))

    own, ghost, small = pl.pallas_call(
        edge_kernel,
        out_shape=(shape(channels, atoms), shape(channels, 128), shape(devices, 128)),
        in_specs=scalar_first(10),
        out_specs=tuple(vmem(3)),
        scratch_shapes=[
            pltpu.VMEM((slots * 8, atoms), F32),
            pltpu.VMEM((slots, atoms + 128, atoms), BF16),
            pltpu.VMEM((slots, channels, atoms), F32),
            pltpu.VMEM((slots, channels, atoms), F32),
        ],
    )(
        atom_count,
        features,
        *arrived,
        cotangent,
        edge_length,
        neighbors,
        short_weight,
        radial_weight,
    )
    small_sum = jnp.sum(exchange(small[:, None, :]), axis=0)
    small_all = exchange(jnp.broadcast_to(small_sum[None], (devices, 1, 128)))
    back = (
        shifted(ghost, "slab", -1),
        shifted(ghost, "slab", 1),
        shifted(ghost, "brick", -1),
        shifted(ghost, "brick", 1),
    )
    partial = pl.pallas_call(
        return_kernel, out_shape=shape(channels, atoms), in_specs=vmem(7), out_specs=vmem(1)[0]
    )(*back, own, send_map, short_weight)
    charge_grad, feature_grad = pl.pallas_call(
        lambda *refs: charge_kernel(*refs, factor=factor),
        out_shape=(shape(channels, channels), shape(channels, atoms)),
        in_specs=scalar_first(4),
        out_specs=tuple(vmem(2)),
    )(atom_count, positions, everyone.reshape(total_rows, 128), partial, charge_weight)
    small_rows = small_all.reshape(channels, devices // channels, 128)[:, 0]
    return (
        feature_grad,
        small_rows[:, :channels],
        charge_grad,
        small_rows[:, channels : channels + radial_weight.shape[1]],
    )


def solution(mesh):
    split_all = P(None, BOTH)
    placed = (split_all,) * 6 + (P(BOTH), P(), P(), P())
    return jax.shard_map(
        on_device,
        mesh=mesh,
        in_specs=placed,
        out_specs=(split_all, P(), P(), P()),
        check_vma=False,
    )
```

time: 370 us -> 167 us (0.45)
  waiting for transfers between devices: 258 us -> 74.8 us
  matrix products: 51.4 us -> 0 us
  starting transfers between devices: 26.8 us -> 60 us
  Pallas kernels: 0 us -> 21.2 us
  between operations: 15.5 us -> 1.39 us
    psum x1 -> x0, waiting for transfers between devices: 258 us -> none  [on_device(): flat_sum = lax.psum(flat_all, ('slab', 'brick'))]
    dot_general x16 -> x0, matrix products: 51.4 us -> none  [the longest x6 26.6 us: contract_last(): lax.dot_general(left, right, (((1,), (1,)), ((), ())), precision=FULL_PRE...]
    all_to_all x0 -> x4, waiting for transfers between devices: none -> 50.7 us  [exchange(): return lax.all_to_all(value, BOTH, 0, 0, tiled=True)]
    all_to_all x0 -> x4, starting transfers between devices: none -> 33.7 us  [exchange(): return lax.all_to_all(value, BOTH, 0, 0, tiled=True)]
    ppermute x8, waiting for transfers between devices: 0.02 us -> 24.1 us  [shifted(): lax.ppermute(value, axis, [(i, (i + step) % size) for i in range(size)])]
    pallas_call x0 -> x5, Pallas kernels: none -> 21.2 us  [the longest x1 11.7 us: on_device(): pl.pallas_call(edge_kernel, out_shape=(shape(channels, atoms), shape(chan...]
    slice x12 -> x2, local copies, waits for them, and re-layouts: 4.29 us -> 0.1 us  [the longest x1 0.07 us: on_device(): small_rows[:, channels:channels + radial_weight.shape[1]]]
  transfers between devices with their start and end apart: 9 -> 12, of which waited for: 1 -> 8; matrix products, arithmetic and copies ran while one was open for 7% -> 3% of each run, Pallas kernels for 0% -> 3%
where the time goes in v1:
time: 167 us; the launch traced here: 166 us
  waiting for transfers between devices  74.8 us (45%)
  starting transfers between devices  60 us (36%)
  Pallas kernels  21.2 us (13%)
  local copies, waits for them, and re-layouts  8.43 us (5%)
    all_to_all x4, waiting for transfers between devices, exchange(): return lax.all_to_all(value, BOTH, 0, 0, tiled=True)  50.7 us
    all_to_all x4, starting transfers between devices, exchange(): return lax.all_to_all(value, BOTH, 0, 0, tiled=True)  33.7 us
    ppermute x8, starting transfers between devices, shifted(): lax.ppermute(value, axis, [(i, (i + step) % size) for i in range(size)])  26.3 us
    ppermute x8, waiting for transfers between devices, shifted(): lax.ppermute(value, axis, [(i, (i + step) % size) for i in range(size)])  24.1 us
    pallas_call x1, Pallas kernels, on_device(): pl.pallas_call(edge_kernel, out_shape=(shape(channels, atoms), shape(chan...  11.7 us
    unnamed x24, local copies, waits for them, and re-layouts  3.35 us
  transfers between devices with their start and end apart: 12, of which 8 were waited for; matrix products, arithmetic and copies ran while one was open for 3% of the time, Pallas kernels for 3%

profile of v1, /device:TPU:1, one launch (start us, length us, event | category | flops | bytes accessed | tf_op | source)
XLA Modules:
  0.0 166.5 jit_solution(2568475472901334515)
XLA Ops:
  0.6 0.0 copy-start.9
  0.6 1.8 %shard_map.139 = f32[64,128]{1,0:T(8,128)} custom-call(f32[64,256]{1,0:T(8,128)} %features_ref.5, s32[4,16]{1,0:T(4,128)} %map_ref.3), custom_call_target="tpu_custom_call" | custom-call | tf_op jit(solution)/shard_map/pallas_call | solution.py:347
  2.4 3.0 %collective-permute-start = (f32[64,128]{1,0:T(8,128)}, f32[64,128]{1,0:T(8,128)S(1)}, u32[]{:S(2)}, u32[]{:S(2)}) collective-permute-start(f32[64,128]{1,0:T(8,128)} %shard_map.139), channel_id=1, source_target_pairs={{0,32},{32,64},{64,96},{96,128},{128,160},{160,192},{192,224},{224... | collective-permute-start | bytes 98312 | tf_op jit(solution)/shard_map/ppermute | solution.py:321
  5.5 0.2 collective-permute-start.1
  5.7 5.8 %collective-permute-start.2 = (f32[64,128]{1,0:T(8,128)}, f32[64,128]{1,0:T(8,128)S(1)}, u32[]{:S(2)}, u32[]{:S(2)}) collective-permute-start(f32[64,128]{1,0:T(8,128)} %shard_map.139), channel_id=1, source_target_pairs={{0,1},{1,2},{2,3},{3,4},{4,5},{5,6},{6,7},{7,8},{8,9},{9,10},{10,1... | collective-permute-start | bytes 98312 | tf_op jit(solution)/shard_map/ppermute | solution.py:321
  11.5 4.6 %collective-permute-start.3 = (f32[64,128]{1,0:T(8,128)}, f32[64,128]{1,0:T(8,128)S(1)}, u32[]{:S(2)}, u32[]{:S(2)}) collective-permute-start(f32[64,128]{1,0:T(8,128)} %shard_map.139), channel_id=1, source_target_pairs={{0,31},{1,0},{2,1},{3,2},{4,3},{5,4},{6,5},{7,6},{8,7},{9,8},{10,9... | collective-permute-start | bytes 98312 | tf_op jit(solution)/shard_map/ppermute | solution.py:321
  16.8 0.0 copy-done.9
  16.8 0.7 copy.19.radial_ref
  17.5 0.0 collective-permute-done.up_ref
  17.5 0.0 collective-permute-done.1.down_ref
  17.5 0.5 collective-permute-done.2.right_ref
  18.0 0.4 collective-permute-done.3.left_ref
  18.4 0.0 copy-done.1
  18.4 0.2 copy-done.4
  18.6 0.6 copy-done.6
  19.2 11.7 %shard_map.140 = (f32[64,256]{1,0:T(8,128)}, f32[64,128]{1,0:T(8,128)}, f32[256,128]{1,0:T(8,128)}) custom-call(s32[1]{0:T(128)S(6)} %copy.22.count_ref.refs_0_, f32[64,256]{1,0:T(8,128)} %features_ref.5, f32[64,128]{1,0:T(8,128)} %copy-done.1, f32[64,128]{1,0:T(8,128)} %copy-done.2, f32[64,128]{1,0:T(8,128)} %copy-done.4, f32[64,128]{1,0:T(8,128)} %copy-done.6, ...), custom_call_target="tpu_custom_call" | custom-call | tf_op jit(solution)/shard_map/pallas_call | solution.py:366
  30.9 14.9 %all-to-all-start.2 = ((f32[256,1,128]{2,1,0:T(1,128)}), f32[256,1,128]{2,1,0:T(1,128)S(1)}, u32[]{:S(2)}, u32[]{:S(2)}) async-start(f32[256,1,128]{2,1,0:T(1,128)} %bitcast.7), calls=%async_computation.2 | async-start | bytes 262144 | tf_op jit(solution)/shard_map/all_to_all | solution.py:325
  45.8 2.8 %shard_map.138 = f32[1536,128]{1,0:T(8,128)} custom-call(s32[1]{0:T(128)S(6)} %copy.22.count_ref.refs_0_, f32[3,256]{1,0:T(4,128)} %refs_1_.1, f32[64,256]{1,0:T(8,128)} %cotangent_ref.3, f32[64,256]{1,0:T(8,128)} %features_ref.5, f32[704,128]{1,0:T(8,128)} %constant.4.clone.table_ref), custom_call_target="tpu_custom_call" | custom-call | tf_op jit(solution)/shard_map/pallas_call | solution.py:356
  48.6 2.2 %reshape.23 = f32[256,6,128]{2,1,0:T(8,128)} reshape(f32[1536,128]{1,0:T(8,128)} %shard_map.138) | data formatting | bytes 1572864 | tf_op jit(solution)/shard_map/reshape | solution.py:362
  50.9 8.0 %all-to-all-done.2 = f32[256,1,128]{2,1,0:T(1,128)S(1)} async-done(((f32[256,1,128]{2,1,0:T(1,128)}), f32[256,1,128]{2,1,0:T(1,128)S(1)}, u32[]{:S(2)}, u32[]{:S(2)}) %all-to-all-start.2) | async-done | bytes 131104 | tf_op jit(solution)/shard_map/all_to_all | solution.py:325
  58.9 5.7 %all-to-all-start = ((f32[256,6,128]{2,1,0:T(8,128)}), f32[256,6,128]{2,1,0:T(8,128)S(1)}, u32[]{:S(2)}, u32[]{:S(2)}) async-start(f32[256,6,128]{2,1,0:T(8,128)} %reshape.23), calls=%async_computation | async-start | bytes 2097152 | tf_op jit(solution)/shard_map/all_to_all | solution.py:325
  64.6 0.3 reduce_sum.19
  64.9 30.0 %all-to-all-done = f32[256,6,128]{2,1,0:T(8,128)S(1)} async-done(((f32[256,6,128]{2,1,0:T(8,128)}), f32[256,6,128]{2,1,0:T(8,128)S(1)}, u32[]{:S(2)}, u32[]{:S(2)}) %all-to-all-start) | async-done | bytes 786464 | tf_op jit(solution)/shard_map/all_to_all | solution.py:325
  94.9 0.7 broadcast_in_dim.8
  95.6 7.3 %all-to-all-start.3 = ((f32[256,1,128]{2,1,0:T(1,128)}), f32[256,1,128]{2,1,0:T(1,128)S(1)}, u32[]{:S(2)}, u32[]{:S(2)}) async-start(f32[256,1,128]{2,1,0:T(1,128)} %broadcast_in_dim.8), calls=%async_computation.3 | async-start | bytes 262144 | tf_op jit(solution)/shard_map/all_to_all | solution.py:325
  102.9 0.3 reduce_sum.18
  103.2 12.7 %all-to-all-done.3 = f32[256,1,128]{2,1,0:T(1,128)S(1)} async-done(((f32[256,1,128]{2,1,0:T(1,128)}), f32[256,1,128]{2,1,0:T(1,128)S(1)}, u32[]{:S(2)}, u32[]{:S(2)}) %all-to-all-start.3) | async-done | bytes 131104 | tf_op jit(solution)/shard_map/all_to_all | solution.py:325
  115.9 1.1 broadcast_in_dim.6
  117.0 5.8 %all-to-all-start.1 = ((f32[256,6,128]{2,1,0:T(8,128)}), f32[256,6,128]{2,1,0:T(8,128)S(1)}, u32[]{:S(2)}, u32[]{:S(2)}) async-start(f32[256,6,128]{2,1,0:T(8,128)} %broadcast_in_dim.6), calls=%async_computation.1 | async-start | bytes 2097152 | tf_op jit(solution)/shard_map/all_to_all | solution.py:325
  122.7 0.0 copy-done.10
  122.8 2.4 %collective-permute-start.4 = (f32[64,128]{1,0:T(8,128)S(1)}, f32[64,128]{1,0:T(8,128)S(1)}, u32[]{:S(2)}, u32[]{:S(2)}) collective-permute-start(f32[64,128]{1,0:T(8,128)S(1)} %copy-done.10), channel_id=1, source_target_pairs={{0,224},{32,0},{64,32},{96,64},{128,96},{160,128},{192,160},{224,1... | collective-permute-start | bytes 98312 | tf_op jit(solution)/shard_map/ppermute | solution.py:321
  125.1 0.0 collective-permute-start.5
  125.1 10.3 %collective-permute-start.6 = (f32[64,128]{1,0:T(8,128)S(1)}, f32[64,128]{1,0:T(8,128)S(1)}, u32[]{:S(2)}, u32[]{:S(2)}) collective-permute-start(f32[64,128]{1,0:T(8,128)S(1)} %copy-done.10), channel_id=1, source_target_pairs={{0,31},{1,0},{2,1},{3,2},{4,3},{5,4},{6,5},{7,6},{8,7},{9,8},{10,9... | collective-permute-start | bytes 98312 | tf_op jit(solution)/shard_map/ppermute | solution.py:321
  135.4 0.0 collective-permute-start.7
  135.4 12.8 %collective-permute-done.4.up_ref = f32[64,128]{1,0:T(8,128)S(1)} collective-permute-done((f32[64,128]{1,0:T(8,128)S(1)}, f32[64,128]{1,0:T(8,128)S(1)}, u32[]{:S(2)}, u32[]{:S(2)}) %collective-permute-start.4) | collective-permute-done | bytes 32800 | tf_op jit(solution)/shard_map/ppermute | solution.py:321
  148.2 0.0 collective-permute-done.5.down_ref
  148.2 3.9 %collective-permute-done.6.right_ref = f32[64,128]{1,0:T(8,128)S(1)} collective-permute-done((f32[64,128]{1,0:T(8,128)S(1)}, f32[64,128]{1,0:T(8,128)S(1)}, u32[]{:S(2)}, u32[]{:S(2)}) %collective-permute-start.6) | collective-permute-done | bytes 32800 | tf_op jit(solution)/shard_map/ppermute | solution.py:321
  152.1 6.6 %collective-permute-done.7.left_ref = f32[64,128]{1,0:T(8,128)S(1)} collective-permute-done((f32[64,128]{1,0:T(8,128)S(1)}, f32[64,128]{1,0:T(8,128)S(1)}, u32[]{:S(2)}, u32[]{:S(2)}) %collective-permute-start.7) | collective-permute-done | bytes 32800 | tf_op jit(solution)/shard_map/ppermute | solution.py:321
  158.7 0.0 copy-done.3
  158.7 0.6 copy-done.8
  159.3 2.1 %shard_map.141.refs_3_ = f32[64,256]{1,0:T(8,128)} custom-call(f32[64,128]{1,0:T(8,128)} %copy-done.3, f32[64,128]{1,0:T(8,128)} %copy-done.5, f32[64,128]{1,0:T(8,128)} %copy-done.7, f32[64,128]{1,0:T(8,128)} %copy-done.8, f32[64,256]{1,0:T(8,128)} %get-tuple-element.10.own_ref, s32[4,16]{1,0:T(4,128)} %map_ref.3, f32[64,64]{1,0:T(8,128)} %short_ref.3), custom_call_target="tpu_custom_call" | custom-call | tf_op jit(solution)/shard_map/pallas_call | solution.py:395
  161.4 0.0 copy-start
  161.4 0.1 slice.14
  161.5 0.5 copy-done
  162.0 0.7 copy.21
  162.7 0.0 all-to-all-done.1
  162.7 1.0 reshape.24.refs_2_
  163.7 2.8 %shard_map.142 = (f32[64,64]{1,0:T(8,128)}, f32[64,256]{1,0:T(8,128)}) custom-call(s32[1]{0:T(128)S(6)} %copy.22.count_ref.refs_0_, f32[3,256]{1,0:T(4,128)} %refs_1_.1, f32[1536,128]{1,0:T(8,128)} %reshape.24.refs_2_, f32[64,256]{1,0:T(8,128)} %shard_map.141.refs_3_, f32[64,64]{1,0:T(8,128)} %refs_4_.1), custom_call_target="tpu_custom_call" | custom-call | tf_op jit(solution)/shard_map/pallas_call | solution.py:398
  (13 shorter events, 0.0 us)
Async XLA Ops:
  0.6 16.1 %copy-start.9 = (f32[64,8]{0,1:T(8,128)S(1)}, f32[64,8]{0,1:T(8,128)}, u32[]{:S(2)}) copy-start(f32[64,8]{0,1:T(8,128)} %param.20) | copy-start | bytes 6148
  2.4 15.0 %collective-permute-start = (f32[64,128]{1,0:T(8,128)}, f32[64,128]{1,0:T(8,128)S(1)}, u32[]{:S(2)}, u32[]{:S(2)}) collective-permute-start(f32[64,128]{1,0:T(8,128)} %shard_map.139), channel_id=1, source_target_pairs={{0,32},{32,64},{64,96},{96,128},{128,160},{160,192},{192,224},{224... | collective-permute-start | bytes 98312 | tf_op jit(solution)/shard_map/ppermute | solution.py:321
  5.5 12.0 %collective-permute-start.1 = (f32[64,128]{1,0:T(8,128)}, f32[64,128]{1,0:T(8,128)S(1)}, u32[]{:S(2)}, u32[]{:S(2)}) collective-permute-start(f32[64,128]{1,0:T(8,128)} %shard_map.139), channel_id=1, source_target_pairs={{0,224},{32,0},{64,32},{96,64},{128,96},{160,128},{192,160},{224,1... | collective-permute-start | bytes 98312 | tf_op jit(solution)/shard_map/ppermute | solution.py:321
  5.7 12.3 %collective-permute-start.2 = (f32[64,128]{1,0:T(8,128)}, f32[64,128]{1,0:T(8,128)S(1)}, u32[]{:S(2)}, u32[]{:S(2)}) collective-permute-start(f32[64,128]{1,0:T(8,128)} %shard_map.139), channel_id=1, source_target_pairs={{0,1},{1,2},{2,3},{3,4},{4,5},{5,6},{6,7},{7,8},{8,9},{9,10},{10,1... | collective-permute-start | bytes 98312 | tf_op jit(solution)/shard_map/ppermute | solution.py:321
  11.5 6.9 %collective-permute-start.3 = (f32[64,128]{1,0:T(8,128)}, f32[64,128]{1,0:T(8,128)S(1)}, u32[]{:S(2)}, u32[]{:S(2)}) collective-permute-start(f32[64,128]{1,0:T(8,128)} %shard_map.139), channel_id=1, source_target_pairs={{0,31},{1,0},{2,1},{3,2},{4,3},{5,4},{6,5},{7,6},{8,7},{9,8},{10,9... | collective-permute-start | bytes 98312 | tf_op jit(solution)/shard_map/ppermute | solution.py:321
  17.5 0.9 copy-start.1
  17.5 0.9 copy-start.2
  18.0 0.6 copy-start.4
  18.6 0.6 copy-start.6
  30.9 28.0 %all-to-all-start.2 = ((f32[256,1,128]{2,1,0:T(1,128)}), f32[256,1,128]{2,1,0:T(1,128)S(1)}, u32[]{:S(2)}, u32[]{:S(2)}) async-start(f32[256,1,128]{2,1,0:T(1,128)} %bitcast.7), calls=%async_computation.2 | async-start | bytes 262144 | tf_op jit(solution)/shard_map/all_to_all | solution.py:325
  58.9 36.0 %all-to-all-start = ((f32[256,6,128]{2,1,0:T(8,128)}), f32[256,6,128]{2,1,0:T(8,128)S(1)}, u32[]{:S(2)}, u32[]{:S(2)}) async-start(f32[256,6,128]{2,1,0:T(8,128)} %reshape.23), calls=%async_computation | async-start | bytes 2097152 | tf_op jit(solution)/shard_map/all_to_all | solution.py:325
  95.6 20.3 %all-to-all-start.3 = ((f32[256,1,128]{2,1,0:T(1,128)}), f32[256,1,128]{2,1,0:T(1,128)S(1)}, u32[]{:S(2)}, u32[]{:S(2)}) async-start(f32[256,1,128]{2,1,0:T(1,128)} %broadcast_in_dim.8), calls=%async_computation.3 | async-start | bytes 262144 | tf_op jit(solution)/shard_map/all_to_all | solution.py:325
  117.0 5.8 %copy-start.10 = (f32[64,128]{1,0:T(8,128)S(1)}, f32[64,128]{1,0:T(8,128)}, u32[]{:S(2)}) copy-start(f32[64,128]{1,0:T(8,128)} %get-tuple-element.9) | copy-start | bytes 98308
  117.0 45.7 %all-to-all-start.1 = ((f32[256,6,128]{2,1,0:T(8,128)}), f32[256,6,128]{2,1,0:T(8,128)S(1)}, u32[]{:S(2)}, u32[]{:S(2)}) async-start(f32[256,6,128]{2,1,0:T(8,128)} %broadcast_in_dim.6), calls=%async_computation.1 | async-start | bytes 2097152 | tf_op jit(solution)/shard_map/all_to_all | solution.py:325
  122.8 25.4 %collective-permute-start.4 = (f32[64,128]{1,0:T(8,128)S(1)}, f32[64,128]{1,0:T(8,128)S(1)}, u32[]{:S(2)}, u32[]{:S(2)}) collective-permute-start(f32[64,128]{1,0:T(8,128)S(1)} %copy-done.10), channel_id=1, source_target_pairs={{0,224},{32,0},{64,32},{96,64},{128,96},{160,128},{192,160},{224,1... | collective-permute-start | bytes 98312 | tf_op jit(solution)/shard_map/ppermute | solution.py:321
  125.1 23.1 %collective-permute-start.5 = (f32[64,128]{1,0:T(8,128)S(1)}, f32[64,128]{1,0:T(8,128)S(1)}, u32[]{:S(2)}, u32[]{:S(2)}) collective-permute-start(f32[64,128]{1,0:T(8,128)S(1)} %copy-done.10), channel_id=1, source_target_pairs={{0,32},{32,64},{64,96},{96,128},{128,160},{160,192},{192,224},{224... | collective-permute-start | bytes 98312 | tf_op jit(solution)/shard_map/ppermute | solution.py:321
  125.1 26.9 %collective-permute-start.6 = (f32[64,128]{1,0:T(8,128)S(1)}, f32[64,128]{1,0:T(8,128)S(1)}, u32[]{:S(2)}, u32[]{:S(2)}) collective-permute-start(f32[64,128]{1,0:T(8,128)S(1)} %copy-done.10), channel_id=1, source_target_pairs={{0,31},{1,0},{2,1},{3,2},{4,3},{5,4},{6,5},{7,6},{8,7},{9,8},{10,9... | collective-permute-start | bytes 98312 | tf_op jit(solution)/shard_map/ppermute | solution.py:321
  135.4 23.2 %collective-permute-start.7 = (f32[64,128]{1,0:T(8,128)S(1)}, f32[64,128]{1,0:T(8,128)S(1)}, u32[]{:S(2)}, u32[]{:S(2)}) collective-permute-start(f32[64,128]{1,0:T(8,128)S(1)} %copy-done.10), channel_id=1, source_target_pairs={{0,1},{1,2},{2,3},{3,4},{4,5},{5,6},{6,7},{7,8},{8,9},{9,10},{10,1... | collective-permute-start | bytes 98312 | tf_op jit(solution)/shard_map/ppermute | solution.py:321
  148.2 10.5 %copy-start.3 = (f32[64,128]{1,0:T(8,128)}, f32[64,128]{1,0:T(8,128)S(1)}, u32[]{:S(2)}) copy-start(f32[64,128]{1,0:T(8,128)S(1)} %collective-permute-done.4.up_ref) | copy-start | bytes 98308
  148.2 10.5 %copy-start.5 = (f32[64,128]{1,0:T(8,128)}, f32[64,128]{1,0:T(8,128)S(1)}, u32[]{:S(2)}) copy-start(f32[64,128]{1,0:T(8,128)S(1)} %collective-permute-done.5.down_ref) | copy-start | bytes 98308
  152.1 6.6 %copy-start.7 = (f32[64,128]{1,0:T(8,128)}, f32[64,128]{1,0:T(8,128)S(1)}, u32[]{:S(2)}) copy-start(f32[64,128]{1,0:T(8,128)S(1)} %collective-permute-done.6.right_ref) | copy-start | bytes 98308
  158.7 0.6 copy-start.8
  161.4 0.6 copy-start

commit v2 on v1

--- a/solution.py
+++ b/solution.py
@@ -6,6 +6,7 @@
 from jax import lax
 from jax.experimental import pallas as pl
 from jax.experimental.pallas import tpu as pltpu
+from jax.sharding import Mesh
 from jax.sharding import PartitionSpec as P
 
 KX = 8
@@ -17,7 +18,9 @@
 F32 = jnp.float32
 BF16 = jnp.bfloat16
 FULL_PRECISION = lax.Precision.HIGHEST
-BOTH = ("slab", "brick")
+SLAB = ("chip", "core")
+CHIPS = ("chip", "brick")
+ALL = ("chip", "core", "brick")
 
 
 def slot_modes(chunk, i, j):
@@ -150,30 +153,51 @@
     return value
 
 
-def send_kernel(features_ref, map_ref, out_ref):
+def front_kernel(
+    scalar_ref,
+    positions_ref,
+    cotangent_ref,
+    features_ref,
+    table_ref,
+    map_ref,
+    keep_ref,
+    give_ref,
+    outgoing_ref,
+):
     features = features_ref[...]
     selector = send_selector(map_ref[...], features.shape[1])
-    high, rest = split(features)
-    middle, low = split(features - high.astype(F32))
-    out_ref[...] = dot(high, selector) + (dot(middle, selector) + dot(low, selector))
-
-
-def wave_kernel(count_ref, positions_ref, cotangent_ref, features_ref, table_ref, out_ref):
+    top, rest = split(features)
+    middle, bottom = split(features - top.astype(F32))
+    outgoing_ref[...] = dot(top, selector) + (dot(middle, selector) + dot(bottom, selector))
+
     chunk = chunk_waves(positions_ref[...])
-    live = live_row(count_ref, positions_ref.shape[1])
-    both = jnp.concatenate([cotangent_ref[...] * live, features_ref[...] * live], axis=0)
+    live = live_row(scalar_ref, positions_ref.shape[1])
+    both = jnp.concatenate([cotangent_ref[...] * live, features * live], axis=0)
     high, low = split(both)
     stacked = jnp.concatenate([high, low], axis=0)
+    first = scalar_ref[1] == 0
+    half = keep_ref.shape[0] // (2 * HALF_ROWS)
+
+    def store(number, value):
+        base = number % half * 2 * HALF_ROWS
+        mine = first if number < half else jnp.logical_not(first)
+
+        @pl.when(mine)
+        def _():
+            keep_ref[base : base + 2 * HALF_ROWS, :] = value
+
+        @pl.when(jnp.logical_not(mine))
+        def _():
+            give_ref[base : base + 2 * HALF_ROWS, :] = value
+
     for number in range(CHUNKS):
         wave_high, wave_low = split(chunk(number))
         part = dot(wave_high, stacked, ((1,), (1,)))
         part = part[:, :128] + part[:, 128:] + dot(wave_low, high, ((1,), (1,)))
         weight = table_ref[number * HALF_ROWS : (number + 1) * HALF_ROWS, :]
-        base = number * 2 * HALF_ROWS
-        out_ref[base : base + HALF_ROWS, :] = part[:HALF_ROWS] * weight
-        out_ref[base + HALF_ROWS : base + 2 * HALF_ROWS, :] = part[HALF_ROWS:] * weight
-    done = CHUNKS * 2 * HALF_ROWS
-    out_ref[done:, :] = jnp.zeros((out_ref.shape[0] - done, 128), F32)
+        store(number, part * jnp.concatenate([weight, weight], axis=0))
+    for number in range(CHUNKS, 2 * half):
+        store(number, jnp.zeros((2 * HALF_ROWS, 128), F32))
 
 
 def edge_kernel(
@@ -279,15 +303,28 @@
 
 
 def charge_kernel(
-    count_ref, positions_ref, waves_ref, partial_ref, charge_ref, grad_ref, out_ref, *, factor
+    scalar_ref,
+    positions_ref,
+    mine_ref,
+    other_ref,
+    partial_ref,
+    charge_ref,
+    grad_ref,
+    out_ref,
+    *,
+    factor,
 ):
+    first = scalar_ref[1] == 0
+    half = mine_ref.shape[0] // (2 * HALF_ROWS)
     chunk = chunk_waves(positions_ref[...])
     channels, atoms = partial_ref.shape
     field = jnp.zeros((2 * channels, atoms), F32)
     grad = jnp.zeros((2 * channels, 128), F32)
     for number in range(CHUNKS):
-        base = number * 2 * HALF_ROWS
-        block = waves_ref[base : base + 2 * HALF_ROWS, :]
+        base = number % half * 2 * HALF_ROWS
+        mine = first if number < half else jnp.logical_not(first)
+        rows = pl.ds(base, 2 * HALF_ROWS)
+        block = jnp.where(mine, mine_ref[rows, :], other_ref[rows, :])
         turned = block.T[:channels]
         turned_high, turned_low = split(turned)
         turned = jnp.concatenate([turned_high, turned_low], axis=0)
@@ -298,7 +335,7 @@
         extra = dot(turned_high, jnp.concatenate([wave_low, block_low], axis=1))
         field = field + jnp.concatenate([extra[:, :atoms], jnp.zeros((channels, atoms), F32)], axis=0)
         grad = grad + jnp.concatenate([extra[:, atoms:], jnp.zeros((channels, 128), F32)], axis=0)
-    field = (field[:channels] + field[channels:]) * live_row(count_ref, atoms)
+    field = (field[:channels] + field[channels:]) * live_row(scalar_ref, atoms)
     grad = grad[:channels] + grad[channels:]
     grad_ref[...] = grad[:, channels : 2 * channels] * factor
     out_ref[...] = partial_ref[...] + dot_full(charge_ref[...], field, ((0,), (0,)))
@@ -312,6 +349,12 @@
     return [pl.BlockSpec(memory_space=pltpu.SMEM)] + vmem(count)
 
 
+def work(micros):
+    return pl.CostEstimate(
+        flops=int(micros * 1e9), transcendentals=0, bytes_accessed=int(micros * 3e6)
+    )
+
+
 def shape(*dims):
     return jax.ShapeDtypeStruct(dims, F32)
 
@@ -321,8 +364,17 @@
     return lax.ppermute(value, axis, [(i, (i + step) % size) for i in range(size)])
 
 
-def exchange(value):
-    return lax.all_to_all(value, BOTH, 0, 0, tiled=True)
+def swapped(value):
+    return lax.ppermute(value, "core", [(0, 1), (1, 0)])
+
+
+def exchange(value, axes):
+    return lax.all_to_all(value, axes, 0, 0, tiled=True)
+
+
+def everywhere(value, axes):
+    size = lax.axis_size(axes)
+    return exchange(jnp.broadcast_to(value[None], (size,) + value.shape), axes)
 
 
 def on_device(
@@ -339,29 +391,30 @@
 ):
     channels, atoms = features.shape
     slots = neighbors.shape[0]
-    devices = lax.axis_size("slab") * lax.axis_size("brick")
+    devices = lax.axis_size(ALL)
+    chips = lax.axis_size(CHIPS)
     factor = 1.0 / math.sqrt(atoms * devices)
     wave_rows = -(-CHUNKS * 2 * HALF_ROWS // devices)
-    total_rows = wave_rows * devices
-
-    outgoing = pl.pallas_call(
-        send_kernel, out_shape=shape(channels, 128), in_specs=vmem(2), out_specs=vmem(1)[0]
-    )(features, send_map)
+    half_rows = wave_rows * chips
+    scalars = jnp.concatenate([atom_count, lax.axis_index("core").reshape(1)])
+
+    keep, give, outgoing = pl.pallas_call(
+        front_kernel,
+        out_shape=(shape(half_rows, 128), shape(half_rows, 128), shape(channels, 128)),
+        in_specs=scalar_first(5),
+        out_specs=tuple(vmem(3)),
+        cost_estimate=work(3.0),
+    )(scalars, positions, cotangent, features, jnp.asarray(weight_table(factor)), send_map)
+    pair = keep + swapped(give)
+    pieces = exchange(pair.reshape(chips, 1, wave_rows * 128), CHIPS)
     arrived = (
-        shifted(outgoing, "slab", 1),
-        shifted(outgoing, "slab", -1),
+        shifted(outgoing, SLAB, 1),
+        shifted(outgoing, SLAB, -1),
         shifted(outgoing, "brick", 1),
         shifted(outgoing, "brick", -1),
     )
-    waves = pl.pallas_call(
-        wave_kernel,
-        out_shape=shape(total_rows, 128),
-        in_specs=scalar_first(4),
-        out_specs=vmem(1)[0],
-    )(atom_count, positions, cotangent, features, jnp.asarray(weight_table(factor)))
-    pieces = exchange(waves.reshape(devices, wave_rows, 128))
-    mine = jnp.sum(pieces, axis=0)
-    everyone = exchange(jnp.broadcast_to(mine[None], (devices, wave_rows, 128)))
+    mine = everywhere(jnp.sum(pieces, axis=0), CHIPS).reshape(half_rows, 128)
+    other = swapped(mine)
 
     own, ghost, small = pl.pallas_call(
         edge_kernel,
@@ -374,8 +427,9 @@
             pltpu.VMEM((slots, channels, atoms), F32),
             pltpu.VMEM((slots, channels, atoms), F32),
         ],
+        cost_estimate=work(10.0),
     )(
-        atom_count,
+        scalars,
         features,
         *arrived,
         cotangent,
@@ -384,23 +438,27 @@
         short_weight,
         radial_weight,
     )
-    small_sum = jnp.sum(exchange(small[:, None, :]), axis=0)
-    small_all = exchange(jnp.broadcast_to(small_sum[None], (devices, 1, 128)))
+    small_all = everywhere(jnp.sum(exchange(small[:, None, :], ALL), axis=0), ALL)
     back = (
-        shifted(ghost, "slab", -1),
-        shifted(ghost, "slab", 1),
+        shifted(ghost, SLAB, -1),
+        shifted(ghost, SLAB, 1),
         shifted(ghost, "brick", -1),
         shifted(ghost, "brick", 1),
     )
     partial = pl.pallas_call(
-        return_kernel, out_shape=shape(channels, atoms), in_specs=vmem(7), out_specs=vmem(1)[0]
+        return_kernel,
+        out_shape=shape(channels, atoms),
+        in_specs=vmem(7),
+        out_specs=vmem(1)[0],
+        cost_estimate=work(2.0),
     )(*back, own, send_map, short_weight)
     charge_grad, feature_grad = pl.pallas_call(
         lambda *refs: charge_kernel(*refs, factor=factor),
         out_shape=(shape(channels, channels), shape(channels, atoms)),
-        in_specs=scalar_first(4),
+        in_specs=scalar_first(5),
         out_specs=tuple(vmem(2)),
-    )(atom_count, positions, everyone.reshape(total_rows, 128), partial, charge_weight)
+        cost_estimate=work(3.0),
+    )(scalars, positions, mine, other, partial, charge_weight)
     small_rows = small_all.reshape(channels, devices // channels, 128)[:, 0]
     return (
         feature_grad,
@@ -411,11 +469,13 @@
 
 
 def solution(mesh):
-    split_all = P(None, BOTH)
-    placed = (split_all,) * 6 + (P(BOTH), P(), P(), P())
+    slabs, bricks = mesh.devices.shape
+    fine = Mesh(mesh.devices.reshape(slabs // 2, 2, bricks), ALL)
+    split_all = P(None, ALL)
+    placed = (split_all,) * 6 + (P(ALL), P(), P(), P())
     return jax.shard_map(
         on_device,
-        mesh=mesh,
+        mesh=fine,
         in_specs=placed,
         out_specs=(split_all, P(), P(), P()),
         check_vma=False,

time: 167 us -> 130 us (0.78)
  waiting for transfers between devices: 74.8 us -> 27 us
  starting transfers between devices: 60 us -> 70.3 us
  other arithmetic: 0.56 us -> 3.02 us
  local copies, waits for them, and re-layouts: 8.43 us -> 6.23 us
    all_to_all x4, waiting for transfers between devices: 50.7 us -> 14.6 us  [exchange(): return lax.all_to_all(value, axes, 0, 0, tiled=True)]
    ppermute x8, waiting for transfers between devices: 24.1 us -> 10.9 us  [shifted(): lax.ppermute(value, axis, [(i, (i + step) % size) for i in range(size)])]
    all_to_all x4, starting transfers between devices: 33.7 us -> 41 us  [exchange(): return lax.all_to_all(value, axes, 0, 0, tiled=True)]
    ppermute x0 -> x2, starting transfers between devices: none -> 5.47 us  [swapped(): return lax.ppermute(value, 'core', [(0, 1), (1, 0)])]
    reshape x2 -> x0, local copies, waits for them, and re-layouts: 3.21 us -> none  [the longest x1 2.23 us: on_device(): pieces = exchange(waves.reshape(devices, wave_rows, 128))]
    ppermute x8, starting transfers between devices: 26.3 us -> 23.8 us  [shifted(): lax.ppermute(value, axis, [(i, (i + step) % size) for i in range(size)])]
    add x0 -> x1, other arithmetic: none -> 1.8 us  [on_device(): pair = keep + swapped(give)]
    unnamed x24 -> x30, local copies, waits for them, and re-layouts: 3.35 us -> 4.45 us
  transfers between devices with their start and end apart: 12 -> 14, of which waited for: 8 -> 6; matrix products, arithmetic and copies ran while one was open for 3% -> 3% of each run, Pallas kernels for 3% -> 11%
where the time goes in v2:
time: 130 us; the launch traced here: 129 us
  starting transfers between devices  70.3 us (54%)
  waiting for transfers between devices  27 us (21%)
  Pallas kernels  21.3 us (16%)
  local copies, waits for them, and re-layouts  6.23 us (5%)
  other arithmetic  3.02 us (2%)
  between operations  1.44 us (1%)
    all_to_all x4, starting transfers between devices, exchange(): return lax.all_to_all(value, axes, 0, 0, tiled=True)  41 us
    ppermute x8, starting transfers between devices, shifted(): lax.ppermute(value, axis, [(i, (i + step) % size) for i in range(size)])  23.8 us
    all_to_all x4, waiting for transfers between devices, exchange(): return lax.all_to_all(value, axes, 0, 0, tiled=True)  14.6 us
    pallas_call x1, Pallas kernels, on_device(): pl.pallas_call(edge_kernel, out_shape=(shape(channels, atoms), shape(chan...  11.7 us
    ppermute x8, waiting for transfers between devices, shifted(): lax.ppermute(value, axis, [(i, (i + step) % size) for i in range(size)])  10.9 us
    ppermute x2, starting transfers between devices, swapped(): return lax.ppermute(value, 'core', [(0, 1), (1, 0)])  5.47 us
    pallas_call x1, Pallas kernels, on_device(): pl.pallas_call(front_kernel, out_shape=(shape(half_rows, 128), shape(half...  4.56 us
    unnamed x30, local copies, waits for them, and re-layouts  4.45 us
  transfers between devices with their start and end apart: 14, of which 6 were waited for; matrix products, arithmetic and copies ran while one was open for 3% of the time, Pallas kernels for 11%

profile of v2, /device:TPU:1, one launch (start us, length us, event | category | flops | bytes accessed | tf_op | source)
XLA Modules:
  0.0 129.3 jit_solution(12310279773790639179)
XLA Ops:
  1.3 0.7 pad_add_fusion.scalar_ref.count_ref.refs_0_
  1.9 4.6 %shard_map.138 = (f32[768,128]{1,0:T(8,128)}, f32[768,128]{1,0:T(8,128)}, f32[64,128]{1,0:T(8,128)}) custom-call(s32[2]{0:T(128)} %pad_add_fusion.scalar_ref.count_ref.refs_0_, f32[3,256]{1,0:T(4,128)} %refs_1_.1, f32[64,256]{1,0:T(8,128)} %cotangent_ref.3, f32[64,256]{1,0:T(8,128)} %features_ref.3, f32[704,128]{1,0:T(8,128)} %constant.10.clone.table_ref, ...), custom_call_target="tpu_custom_call" | custom-call | flops 3000000000 | bytes 9000000 | tf_op jit(solution)/shard_map/pallas_call | solution.py:401
  6.5 3.2 %collective-permute-start = (f32[768,128]{1,0:T(8,128)}, f32[768,128]{1,0:T(8,128)S(1)}, u32[]{:S(2)}, u32[]{:S(2)}) collective-permute-start(f32[768,128]{1,0:T(8,128)} %get-tuple-element.13), channel_id=1, source_target_pairs={{0,32},{32,0},{1,33},{33,1},{2,34},{34,2},{3,35},{35,3},{4,36},{36... | collective-permute-start | bytes 1179656 | tf_op jit(solution)/shard_map/ppermute | solution.py:368
  9.7 1.6 %collective-permute-done = f32[768,128]{1,0:T(8,128)S(1)} collective-permute-done((f32[768,128]{1,0:T(8,128)}, f32[768,128]{1,0:T(8,128)S(1)}, u32[]{:S(2)}, u32[]{:S(2)}) %collective-permute-start) | collective-permute-done | bytes 393248 | tf_op jit(solution)/shard_map/ppermute | solution.py:368
  11.3 1.8 %add.3 = f32[768,128]{1,0:T(8,128)} add(f32[768,128]{1,0:T(8,128)} %get-tuple-element.12, f32[768,128]{1,0:T(8,128)S(1)} %collective-permute-done) | non-fusion elementwise | flops 98304 | bytes 1179648 | tf_op jit(solution)/shard_map/add | solution.py:408
  13.1 13.9 %all-to-all-start = ((f32[128,1,768]{2,1,0:T(1,128)}), f32[128,1,768]{2,1,0:T(1,128)S(1)}, u32[]{:S(2)}, u32[]{:S(2)}) async-start(f32[128,1,768]{2,1,0:T(1,128)} %bitcast.1), calls=%async_computation | async-start | bytes 786432 | tf_op jit(solution)/shard_map/all_to_all | solution.py:372
  27.0 1.6 %collective-permute-start.2 = (f32[64,128]{1,0:T(8,128)S(1)}, f32[64,128]{1,0:T(8,128)S(1)}, u32[]{:S(2)}, u32[]{:S(2)}) collective-permute-start(f32[64,128]{1,0:T(8,128)S(1)} %copy-done.5), channel_id=1, source_target_pairs={{0,32},{32,64},{64,96},{96,128},{128,160},{160,192},{192,224},{224... | collective-permute-start | bytes 98312 | tf_op jit(solution)/shard_map/ppermute | solution.py:364
  28.6 0.0 collective-permute-start.3
  28.6 4.2 %collective-permute-start.4 = (f32[64,128]{1,0:T(8,128)S(1)}, f32[64,128]{1,0:T(8,128)S(1)}, u32[]{:S(2)}, u32[]{:S(2)}) collective-permute-start(f32[64,128]{1,0:T(8,128)S(1)} %copy-done.5), channel_id=1, source_target_pairs={{0,1},{1,2},{2,3},{3,4},{4,5},{5,6},{6,7},{7,8},{8,9},{9,10},{10,1... | collective-permute-start | bytes 98312 | tf_op jit(solution)/shard_map/ppermute | solution.py:364
  32.8 5.4 %collective-permute-start.5 = (f32[64,128]{1,0:T(8,128)S(1)}, f32[64,128]{1,0:T(8,128)S(1)}, u32[]{:S(2)}, u32[]{:S(2)}) collective-permute-start(f32[64,128]{1,0:T(8,128)S(1)} %copy-done.5), channel_id=1, source_target_pairs={{0,31},{1,0},{2,1},{3,2},{4,3},{5,4},{6,5},{7,6},{8,7},{9,8},{10,9... | collective-permute-start | bytes 98312 | tf_op jit(solution)/shard_map/ppermute | solution.py:364
  38.2 0.7 copy.20.radial_ref
  38.9 3.6 %all-to-all-done = f32[128,1,768]{2,1,0:T(1,128)S(1)} async-done(((f32[128,1,768]{2,1,0:T(1,128)}), f32[128,1,768]{2,1,0:T(1,128)S(1)}, u32[]{:S(2)}, u32[]{:S(2)}) %all-to-all-start) | async-done | bytes 393248 | tf_op jit(solution)/shard_map/all_to_all | solution.py:372
  42.4 0.3 reduce_sum.18
  42.7 1.0 broadcast_in_dim.6
  43.7 7.6 %all-to-all-start.1 = ((f32[128,1,768]{2,1,0:T(1,128)}), f32[128,1,768]{2,1,0:T(1,128)S(1)}, u32[]{:S(2)}, u32[]{:S(2)}) async-start(f32[128,1,768]{2,1,0:T(1,128)} %broadcast_in_dim.6), calls=%async_computation.1 | async-start | bytes 786432 | tf_op jit(solution)/shard_map/all_to_all | solution.py:372
  51.3 0.0 copy-start.6
  51.3 0.0 collective-permute-done.3.down_ref
  51.3 0.0 copy-start.7
  51.4 0.0 collective-permute-done.5.left_ref
  51.4 0.6 copy-done.6
  51.9 0.0 copy-done.7
  52.0 0.0 copy-done.8
  52.0 0.6 copy-done.9
  52.6 11.7 %shard_map.139 = (f32[64,256]{1,0:T(8,128)}, f32[64,128]{1,0:T(8,128)}, f32[256,128]{1,0:T(8,128)}) custom-call(s32[2]{0:T(128)} %pad_add_fusion.scalar_ref.count_ref.refs_0_, f32[64,256]{1,0:T(8,128)} %features_ref.3, f32[64,128]{1,0:T(8,128)} %copy-done.6, f32[64,128]{1,0:T(8,128)} %copy-done.7, f32[64,128]{1,0:T(8,128)} %copy-done.8, ...), custom_call_target="tpu_custom_call" | custom-call | flops 10000000000 | bytes 30000000 | tf_op jit(solution)/shard_map/pallas_call | solution.py:419
  64.3 0.2 all-to-all-done.1
  64.5 13.8 %all-to-all-start.2 = ((f32[256,1,128]{2,1,0:T(1,128)}), f32[256,1,128]{2,1,0:T(1,128)S(1)}, u32[]{:S(2)}, u32[]{:S(2)}) async-start(f32[256,1,128]{2,1,0:T(1,128)} %bitcast.12), calls=%async_computation.2 | async-start | bytes 262144 | tf_op jit(solution)/shard_map/all_to_all | solution.py:372
  78.3 2.2 %collective-permute-start.1 = (f32[768,128]{1,0:T(8,128)S(1)}, f32[768,128]{1,0:T(8,128)S(1)}, u32[]{:S(2)}, u32[]{:S(2)}) collective-permute-start(f32[768,128]{1,0:T(8,128)S(1)} %bitcast.9), channel_id=1, source_target_pairs={{0,32},{32,0},{1,33},{33,1},{2,34},{34,2},{3,35},{35,3},{4,36},{36... | collective-permute-start | bytes 1179656 | tf_op jit(solution)/shard_map/ppermute | solution.py:368
  80.6 10.8 %all-to-all-done.2 = f32[256,1,128]{2,1,0:T(1,128)S(1)} async-done(((f32[256,1,128]{2,1,0:T(1,128)}), f32[256,1,128]{2,1,0:T(1,128)S(1)}, u32[]{:S(2)}, u32[]{:S(2)}) %all-to-all-start.2) | async-done | bytes 131104 | tf_op jit(solution)/shard_map/all_to_all | solution.py:372
  91.4 0.3 reduce_sum.19
  91.6 0.7 broadcast_in_dim.8
  92.4 5.7 %all-to-all-start.3 = ((f32[256,1,128]{2,1,0:T(1,128)}), f32[256,1,128]{2,1,0:T(1,128)S(1)}, u32[]{:S(2)}, u32[]{:S(2)}) async-start(f32[256,1,128]{2,1,0:T(1,128)} %broadcast_in_dim.8), calls=%async_computation.3 | async-start | bytes 262144 | tf_op jit(solution)/shard_map/all_to_all | solution.py:372
  98.1 2.4 %collective-permute-start.6 = (f32[64,128]{1,0:T(8,128)S(1)}, f32[64,128]{1,0:T(8,128)S(1)}, u32[]{:S(2)}, u32[]{:S(2)}) collective-permute-start(f32[64,128]{1,0:T(8,128)S(1)} %copy-done.4), channel_id=1, source_target_pairs={{0,224},{32,0},{64,32},{96,64},{128,96},{160,128},{192,160},{224,1... | collective-permute-start | bytes 98312 | tf_op jit(solution)/shard_map/ppermute | solution.py:364
  100.5 0.0 collective-permute-start.7
  100.5 10.3 %collective-permute-start.8 = (f32[64,128]{1,0:T(8,128)S(1)}, f32[64,128]{1,0:T(8,128)S(1)}, u32[]{:S(2)}, u32[]{:S(2)}) collective-permute-start(f32[64,128]{1,0:T(8,128)S(1)} %copy-done.4), channel_id=1, source_target_pairs={{0,31},{1,0},{2,1},{3,2},{4,3},{5,4},{6,5},{7,6},{8,7},{9,8},{10,9... | collective-permute-start | bytes 98312 | tf_op jit(solution)/shard_map/ppermute | solution.py:364
  110.7 0.0 collective-permute-start.9
  110.8 0.0 collective-permute-done.6.up_ref
  110.8 0.0 collective-permute-done.7.down_ref
  110.8 0.0 copy-start.11
  110.8 1.0 collective-permute-done.8.right_ref
  111.8 9.9 %collective-permute-done.9.left_ref = f32[64,128]{1,0:T(8,128)S(1)} collective-permute-done((f32[64,128]{1,0:T(8,128)S(1)}, f32[64,128]{1,0:T(8,128)S(1)}, u32[]{:S(2)}, u32[]{:S(2)}) %collective-permute-start.9) | collective-permute-done | bytes 32800 | tf_op jit(solution)/shard_map/ppermute | solution.py:364
  121.7 0.6 copy-done.13
  122.2 2.1 %shard_map.140.refs_4_ = f32[64,256]{1,0:T(8,128)} custom-call(f32[64,128]{1,0:T(8,128)} %copy-done.10, f32[64,128]{1,0:T(8,128)} %copy-done.11, f32[64,128]{1,0:T(8,128)} %copy-done.12, f32[64,128]{1,0:T(8,128)} %copy-done.13, f32[64,256]{1,0:T(8,128)} %get-tuple-element.16.own_ref, s32[4,16]{1,0:T(4,128)} %map_ref.3, f32[64,64]{1,0:T(8,128)} %short_ref.3), custom_call_target="tpu_custom_call" | custom-call | flops 2000000000 | bytes 6000000 | tf_op jit(solution)/shard_map/pallas_call | solution.py:448
  124.4 0.0 copy-start.1
  124.4 0.1 slice.14
  124.5 0.5 copy-done.1
  125.0 0.7 copy.22
  125.7 0.7 copy-done.3
  126.4 2.9 %shard_map.141 = (f32[64,64]{1,0:T(8,128)}, f32[64,256]{1,0:T(8,128)}) custom-call(s32[2]{0:T(128)} %pad_add_fusion.scalar_ref.count_ref.refs_0_, f32[3,256]{1,0:T(4,128)} %refs_1_.1, f32[768,128]{1,0:T(8,128)} %bitcast.10, f32[768,128]{1,0:T(8,128)} %copy-done.3, f32[64,256]{1,0:T(8,128)} %shard_map.140.refs_4_, f32[64,64]{1,0:T(8,128)} %refs_5_.1), custom_call_target="tpu_custom_call" | custom-call | flops 3000000000 | bytes 9000000 | tf_op jit(solution)/shard_map/pallas_call | solution.py:455
  (22 shorter events, 0.1 us)
Async XLA Ops:
  6.5 4.8 %collective-permute-start = (f32[768,128]{1,0:T(8,128)}, f32[768,128]{1,0:T(8,128)S(1)}, u32[]{:S(2)}, u32[]{:S(2)}) collective-permute-start(f32[768,128]{1,0:T(8,128)} %get-tuple-element.13), channel_id=1, source_target_pairs={{0,32},{32,0},{1,33},{33,1},{2,34},{34,2},{3,35},{35,3},{4,36},{36... | collective-permute-start | bytes 1179656 | tf_op jit(solution)/shard_map/ppermute | solution.py:368
  13.1 13.9 %copy-start.5 = (f32[64,128]{1,0:T(8,128)S(1)}, f32[64,128]{1,0:T(8,128)}, u32[]{:S(2)}) copy-start(f32[64,128]{1,0:T(8,128)} %get-tuple-element.14) | copy-start | bytes 98308
  13.1 25.1 %copy-start.2 = (f32[64,8]{0,1:T(8,128)S(1)}, f32[64,8]{0,1:T(8,128)}, u32[]{:S(2)}) copy-start(f32[64,8]{0,1:T(8,128)} %param.20) | copy-start | bytes 6148
  13.1 29.3 %all-to-all-start = ((f32[128,1,768]{2,1,0:T(1,128)}), f32[128,1,768]{2,1,0:T(1,128)S(1)}, u32[]{:S(2)}, u32[]{:S(2)}) async-start(f32[128,1,768]{2,1,0:T(1,128)} %bitcast.1), calls=%async_computation | async-start | bytes 786432 | tf_op jit(solution)/shard_map/all_to_all | solution.py:372
  27.0 24.3 %collective-permute-start.2 = (f32[64,128]{1,0:T(8,128)S(1)}, f32[64,128]{1,0:T(8,128)S(1)}, u32[]{:S(2)}, u32[]{:S(2)}) collective-permute-start(f32[64,128]{1,0:T(8,128)S(1)} %copy-done.5), channel_id=1, source_target_pairs={{0,32},{32,64},{64,96},{96,128},{128,160},{160,192},{192,224},{224... | collective-permute-start | bytes 98312 | tf_op jit(solution)/shard_map/ppermute | solution.py:364
  28.6 22.7 %collective-permute-start.3 = (f32[64,128]{1,0:T(8,128)S(1)}, f32[64,128]{1,0:T(8,128)S(1)}, u32[]{:S(2)}, u32[]{:S(2)}) collective-permute-start(f32[64,128]{1,0:T(8,128)S(1)} %copy-done.5), channel_id=1, source_target_pairs={{0,224},{32,0},{64,32},{96,64},{128,96},{160,128},{192,160},{224,1... | collective-permute-start | bytes 98312 | tf_op jit(solution)/shard_map/ppermute | solution.py:364
  28.6 22.8 %collective-permute-start.4 = (f32[64,128]{1,0:T(8,128)S(1)}, f32[64,128]{1,0:T(8,128)S(1)}, u32[]{:S(2)}, u32[]{:S(2)}) collective-permute-start(f32[64,128]{1,0:T(8,128)S(1)} %copy-done.5), channel_id=1, source_target_pairs={{0,1},{1,2},{2,3},{3,4},{4,5},{5,6},{6,7},{7,8},{8,9},{9,10},{10,1... | collective-permute-start | bytes 98312 | tf_op jit(solution)/shard_map/ppermute | solution.py:364
  32.8 18.6 %collective-permute-start.5 = (f32[64,128]{1,0:T(8,128)S(1)}, f32[64,128]{1,0:T(8,128)S(1)}, u32[]{:S(2)}, u32[]{:S(2)}) collective-permute-start(f32[64,128]{1,0:T(8,128)S(1)} %copy-done.5), channel_id=1, source_target_pairs={{0,31},{1,0},{2,1},{3,2},{4,3},{5,4},{6,5},{7,6},{8,7},{9,8},{10,9... | collective-permute-start | bytes 98312 | tf_op jit(solution)/shard_map/ppermute | solution.py:364
  43.7 20.8 %all-to-all-start.1 = ((f32[128,1,768]{2,1,0:T(1,128)}), f32[128,1,768]{2,1,0:T(1,128)S(1)}, u32[]{:S(2)}, u32[]{:S(2)}) async-start(f32[128,1,768]{2,1,0:T(1,128)} %broadcast_in_dim.6), calls=%async_computation.1 | async-start | bytes 786432 | tf_op jit(solution)/shard_map/all_to_all | solution.py:372
  51.3 0.6 copy-start.6
  51.3 0.6 copy-start.7
  51.4 0.6 copy-start.8
  52.0 0.6 copy-start.9
  64.5 27.9 %copy-start = (f32[128,1,768]{2,1,0:T(1,128)}, f32[128,1,768]{2,1,0:T(1,128)S(1)}, u32[]{:S(2)}) copy-start(f32[128,1,768]{2,1,0:T(1,128)S(1)} %all-to-all-done.1) | copy-start | bytes 1179652
  64.5 26.8 %all-to-all-start.2 = ((f32[256,1,128]{2,1,0:T(1,128)}), f32[256,1,128]{2,1,0:T(1,128)S(1)}, u32[]{:S(2)}, u32[]{:S(2)}) async-start(f32[256,1,128]{2,1,0:T(1,128)} %bitcast.12), calls=%async_computation.2 | async-start | bytes 262144 | tf_op jit(solution)/shard_map/all_to_all | solution.py:372
  78.3 47.4 %collective-permute-start.1 = (f32[768,128]{1,0:T(8,128)S(1)}, f32[768,128]{1,0:T(8,128)S(1)}, u32[]{:S(2)}, u32[]{:S(2)}) collective-permute-start(f32[768,128]{1,0:T(8,128)S(1)} %bitcast.9), channel_id=1, source_target_pairs={{0,32},{32,0},{1,33},{33,1},{2,34},{34,2},{3,35},{35,3},{4,36},{36... | collective-permute-start | bytes 1179656 | tf_op jit(solution)/shard_map/ppermute | solution.py:368
  92.4 5.7 %copy-start.4 = (f32[64,128]{1,0:T(8,128)S(1)}, f32[64,128]{1,0:T(8,128)}, u32[]{:S(2)}) copy-start(f32[64,128]{1,0:T(8,128)} %get-tuple-element.15) | copy-start | bytes 98308
  92.4 32.0 %all-to-all-start.3 = ((f32[256,1,128]{2,1,0:T(1,128)}), f32[256,1,128]{2,1,0:T(1,128)S(1)}, u32[]{:S(2)}, u32[]{:S(2)}) async-start(f32[256,1,128]{2,1,0:T(1,128)} %broadcast_in_dim.8), calls=%async_computation.3 | async-start | bytes 262144 | tf_op jit(solution)/shard_map/all_to_all | solution.py:372
  98.1 12.7 %collective-permute-start.6 = (f32[64,128]{1,0:T(8,128)S(1)}, f32[64,128]{1,0:T(8,128)S(1)}, u32[]{:S(2)}, u32[]{:S(2)}) collective-permute-start(f32[64,128]{1,0:T(8,128)S(1)} %copy-done.4), channel_id=1, source_target_pairs={{0,224},{32,0},{64,32},{96,64},{128,96},{160,128},{192,160},{224,1... | collective-permute-start | bytes 98312 | tf_op jit(solution)/shard_map/ppermute | solution.py:364
  100.5 10.3 %collective-permute-start.7 = (f32[64,128]{1,0:T(8,128)S(1)}, f32[64,128]{1,0:T(8,128)S(1)}, u32[]{:S(2)}, u32[]{:S(2)}) collective-permute-start(f32[64,128]{1,0:T(8,128)S(1)} %copy-done.4), channel_id=1, source_target_pairs={{0,32},{32,64},{64,96},{96,128},{128,160},{160,192},{192,224},{224... | collective-permute-start | bytes 98312 | tf_op jit(solution)/shard_map/ppermute | solution.py:364
  100.5 11.3 %collective-permute-start.8 = (f32[64,128]{1,0:T(8,128)S(1)}, f32[64,128]{1,0:T(8,128)S(1)}, u32[]{:S(2)}, u32[]{:S(2)}) collective-permute-start(f32[64,128]{1,0:T(8,128)S(1)} %copy-done.4), channel_id=1, source_target_pairs={{0,31},{1,0},{2,1},{3,2},{4,3},{5,4},{6,5},{7,6},{8,7},{9,8},{10,9... | collective-permute-start | bytes 98312 | tf_op jit(solution)/shard_map/ppermute | solution.py:364
  110.7 10.9 %collective-permute-start.9 = (f32[64,128]{1,0:T(8,128)S(1)}, f32[64,128]{1,0:T(8,128)S(1)}, u32[]{:S(2)}, u32[]{:S(2)}) collective-permute-start(f32[64,128]{1,0:T(8,128)S(1)} %copy-done.4), channel_id=1, source_target_pairs={{0,1},{1,2},{2,3},{3,4},{4,5},{5,6},{6,7},{7,8},{8,9},{9,10},{10,1... | collective-permute-start | bytes 98312 | tf_op jit(solution)/shard_map/ppermute | solution.py:364
  110.8 10.9 %copy-start.10 = (f32[64,128]{1,0:T(8,128)}, f32[64,128]{1,0:T(8,128)S(1)}, u32[]{:S(2)}) copy-start(f32[64,128]{1,0:T(8,128)S(1)} %collective-permute-done.6.up_ref) | copy-start | bytes 98308
  110.8 10.9 %copy-start.11 = (f32[64,128]{1,0:T(8,128)}, f32[64,128]{1,0:T(8,128)S(1)}, u32[]{:S(2)}) copy-start(f32[64,128]{1,0:T(8,128)S(1)} %collective-permute-done.7.down_ref) | copy-start | bytes 98308
  111.8 9.9 %copy-start.12 = (f32[64,128]{1,0:T(8,128)}, f32[64,128]{1,0:T(8,128)S(1)}, u32[]{:S(2)}) copy-start(f32[64,128]{1,0:T(8,128)S(1)} %collective-permute-done.8.right_ref) | copy-start | bytes 98308
  121.6 0.6 copy-start.13
  124.4 0.6 copy-start.1
  125.7 0.8 copy-start.3

commit v3 on v2

--- a/solution.py
+++ b/solution.py
@@ -1,3 +1,4 @@
+import functools
 import math
 
 import jax
@@ -153,8 +154,8 @@
     return value
 
 
-def front_kernel(
-    scalar_ref,
+def wave_kernel(
+    count_ref,
     positions_ref,
     cotangent_ref,
     features_ref,
@@ -169,61 +170,65 @@
     top, rest = split(features)
     middle, bottom = split(features - top.astype(F32))
     outgoing_ref[...] = dot(top, selector) + (dot(middle, selector) + dot(bottom, selector))
-
     chunk = chunk_waves(positions_ref[...])
-    live = live_row(scalar_ref, positions_ref.shape[1])
+    live = live_row(count_ref, positions_ref.shape[1])
     both = jnp.concatenate([cotangent_ref[...] * live, features * live], axis=0)
     high, low = split(both)
     stacked = jnp.concatenate([high, low], axis=0)
-    first = scalar_ref[1] == 0
-    half = keep_ref.shape[0] // (2 * HALF_ROWS)
-
-    def store(number, value):
-        base = number % half * 2 * HALF_ROWS
-        mine = first if number < half else jnp.logical_not(first)
+    first = lax.axis_index("core") == 0
+
+    def store(unit, value):
+        rows = pl.ds(unit % CHUNKS * HALF_ROWS, HALF_ROWS)
+        mine = first if unit < CHUNKS else jnp.logical_not(first)
 
         @pl.when(mine)
         def _():
-            keep_ref[base : base + 2 * HALF_ROWS, :] = value
+            keep_ref[rows, :] = value
 
         @pl.when(jnp.logical_not(mine))
         def _():
-            give_ref[base : base + 2 * HALF_ROWS, :] = value
+            give_ref[rows, :] = value
 
     for number in range(CHUNKS):
         wave_high, wave_low = split(chunk(number))
         part = dot(wave_high, stacked, ((1,), (1,)))
         part = part[:, :128] + part[:, 128:] + dot(wave_low, high, ((1,), (1,)))
         weight = table_ref[number * HALF_ROWS : (number + 1) * HALF_ROWS, :]
-        store(number, part * jnp.concatenate([weight, weight], axis=0))
-    for number in range(CHUNKS, 2 * half):
-        store(number, jnp.zeros((2 * HALF_ROWS, 128), F32))
+        store(2 * number, part[:HALF_ROWS] * weight)
+        store(2 * number + 1, part[HALF_ROWS:] * weight)
 
 
 def edge_kernel(
     count_ref,
     features_ref,
+    right_ref,
+    left_ref,
     up_ref,
     down_ref,
-    right_ref,
-    left_ref,
     cotangent_ref,
     length_ref,
     neighbor_ref,
     short_ref,
     radial_ref,
+    keep_ref,
+    taken_ref,
     own_ref,
     ghost_ref,
-    small_ref,
+    payload_ref,
     basis_ref,
     selector_ref,
     gathered_ref,
     weight_ref,
+    *,
+    factor,
 ):
     channels, atoms = features_ref.shape
     slots = length_ref.shape[0]
     columns = atoms + 128
-    scale = small_ref.shape[0]
+    group = 4
+    wide = group * atoms
+    waves = keep_ref.shape[0]
+    payload_ref[:waves, :] = keep_ref[...] + taken_ref[...]
     extended = jnp.concatenate(
         [features_ref[...], pick_lanes((up_ref, down_ref, right_ref, left_ref))], axis=1
     )
@@ -241,58 +246,69 @@
     basis_ref[...] = basis.reshape(slots * 8, atoms)
 
     radial_high, radial_low = split(radial_ref[...])
-    radial_wide = jnp.concatenate([radial_high, radial_high, radial_low], axis=1)
-    column = lax.broadcasted_iota(jnp.int32, (columns, atoms), 0)
-
-    def basis_of(slot):
-        return split(basis_ref[pl.ds(pl.multiple_of(slot * 8, 8), 8), :])
-
-    def forward(slot, total):
-        selector = (column == neighbor_ref[pl.ds(slot, 1), :]).astype(F32).astype(BF16)
-        selector_ref[slot] = selector
+    radial_wide = jnp.concatenate([radial_high, radial_high, radial_low], axis=0)
+    column = lax.broadcasted_iota(jnp.int32, (columns, wide), 0)
+
+    def side_by_side(pieces):
+        return jnp.concatenate(pieces, axis=1)
+
+    def basis_of(turn):
+        base = turn * group * 8
+        return split(
+            side_by_side(
+                [basis_ref[pl.ds(pl.multiple_of(base + 8 * i, 8), 8), :] for i in range(group)]
+            )
+        )
+
+    def forward(turn, total):
+        picks = side_by_side([neighbor_ref[pl.ds(turn * group + i, 1), :] for i in range(group)])
+        selector = (column == picks).astype(F32).astype(BF16)
+        selector_ref[turn] = selector
         found = dot(projected, selector)
         gathered = found[:channels] + found[channels:]
-        basis_high, basis_low = basis_of(slot)
-        weight = dot(radial_wide, jnp.concatenate([basis_high, basis_low, basis_high], axis=0))
-        gathered_ref[slot] = gathered
-        weight_ref[slot] = weight
-        return total + weight * gathered
-
-    short_sum = lax.fori_loop(0, slots, forward, jnp.zeros((channels, atoms), F32), unroll=2)
+        basis_high, basis_low = basis_of(turn)
+        weight = dot(
+            radial_wide, jnp.concatenate([basis_high, basis_low, basis_high], axis=0), ((0,), (0,))
+        )
+        gathered_ref[turn] = gathered
+        weight_ref[turn] = weight
+        product = weight * gathered
+        for i in range(group):
+            total = total + product[:, i * atoms : (i + 1) * atoms]
+        return total
+
+    turns = slots // group
+    short_sum = lax.fori_loop(0, turns, forward, jnp.zeros((channels, atoms), F32))
     gate = jax.nn.sigmoid(short_sum)
     upstream = cotangent_ref[...] * gate * (1.0 + short_sum * (1.0 - gate)) * live
-
-    def backward(slot, running):
+    upstream = side_by_side([upstream] * group)
+
+    def backward(turn, running):
         grads, radial = running
-        spread = jnp.concatenate(split(weight_ref[slot] * upstream), axis=0)
-        grads = grads + dot(spread, selector_ref[slot], ((1,), (1,)))
-        pulled = jnp.concatenate(split(gathered_ref[slot] * upstream), axis=0)
-        pair = jnp.concatenate(basis_of(slot), axis=0)
+        spread = jnp.concatenate(split(weight_ref[turn] * upstream), axis=0)
+        grads = grads + dot(spread, selector_ref[turn], ((1,), (1,)))
+        pulled = jnp.concatenate(split(gathered_ref[turn] * upstream), axis=0)
+        pair = jnp.concatenate(basis_of(turn), axis=0)
         return grads, radial + dot(pulled, pair, ((1,), (1,)))
 
     grads, radial = lax.fori_loop(
         0,
-        slots,
+        turns,
         backward,
         (jnp.zeros((2 * channels, columns), F32), jnp.zeros((2 * channels, 16), F32)),
-        unroll=2,
     )
     grads = grads[:channels] + grads[channels:]
     radial = radial[:channels] + radial[channels:]
     radial = radial[:, :8] + radial[:, 8:]
     own_ref[...] = grads[:, :atoms]
     ghost_ref[...] = grads[:, atoms:]
-    factor = 1.0 / math.sqrt(atoms * scale)
     short_part = dot_full(grads, extended, ((1,), (1,))) * factor
-    rows = small_ref.shape[0] // channels
-    small_ref[...] = jnp.zeros(small_ref.shape, F32)
-    packed = jnp.concatenate(
+    payload_ref[waves:, :] = jnp.concatenate(
         [short_part, radial * factor, jnp.zeros((channels, 128 - channels - 8), F32)], axis=1
     )
-    small_ref[pl.ds(0, channels, stride=rows), :] = packed
-
-
-def return_kernel(up_ref, down_ref, right_ref, left_ref, own_ref, map_ref, short_ref, out_ref):
+
+
+def return_kernel(right_ref, left_ref, up_ref, down_ref, own_ref, map_ref, short_ref, out_ref):
     back = pick_lanes((up_ref, down_ref, right_ref, left_ref))
     selector = send_selector(map_ref[...], own_ref.shape[1])
     high, low = split(back)
@@ -303,7 +319,7 @@
 
 
 def charge_kernel(
-    scalar_ref,
+    count_ref,
     positions_ref,
     mine_ref,
     other_ref,
@@ -311,20 +327,28 @@
     charge_ref,
     grad_ref,
     out_ref,
+    short_ref,
+    radial_ref,
     *,
     factor,
 ):
-    first = scalar_ref[1] == 0
-    half = mine_ref.shape[0] // (2 * HALF_ROWS)
+    first = lax.axis_index("core") == 0
+    waves = CHUNKS * HALF_ROWS
+    small = mine_ref[waves:, :] + other_ref[waves:, :]
+    channels, atoms = partial_ref.shape
+    short_ref[...] = small[:, :channels]
+    radial_ref[...] = small.T[channels : channels + 8, :]
+
+    def unit(number):
+        rows = pl.ds(number % CHUNKS * HALF_ROWS, HALF_ROWS)
+        mine = first if number < CHUNKS else jnp.logical_not(first)
+        return jnp.where(mine, mine_ref[rows, :], other_ref[rows, :])
+
     chunk = chunk_waves(positions_ref[...])
-    channels, atoms = partial_ref.shape
     field = jnp.zeros((2 * channels, atoms), F32)
     grad = jnp.zeros((2 * channels, 128), F32)
     for number in range(CHUNKS):
-        base = number % half * 2 * HALF_ROWS
-        mine = first if number < half else jnp.logical_not(first)
-        rows = pl.ds(base, 2 * HALF_ROWS)
-        block = jnp.where(mine, mine_ref[rows, :], other_ref[rows, :])
+        block = jnp.concatenate([unit(2 * number), unit(2 * number + 1)], axis=0)
         turned = block.T[:channels]
         turned_high, turned_low = split(turned)
         turned = jnp.concatenate([turned_high, turned_low], axis=0)
@@ -335,7 +359,7 @@
         extra = dot(turned_high, jnp.concatenate([wave_low, block_low], axis=1))
         field = field + jnp.concatenate([extra[:, :atoms], jnp.zeros((channels, atoms), F32)], axis=0)
         grad = grad + jnp.concatenate([extra[:, atoms:], jnp.zeros((channels, 128), F32)], axis=0)
-    field = (field[:channels] + field[channels:]) * live_row(scalar_ref, atoms)
+    field = (field[:channels] + field[channels:]) * live_row(count_ref, atoms)
     grad = grad[:channels] + grad[channels:]
     grad_ref[...] = grad[:, channels : 2 * channels] * factor
     out_ref[...] = partial_ref[...] + dot_full(charge_ref[...], field, ((0,), (0,)))
@@ -394,56 +418,56 @@
     devices = lax.axis_size(ALL)
     chips = lax.axis_size(CHIPS)
     factor = 1.0 / math.sqrt(atoms * devices)
-    wave_rows = -(-CHUNKS * 2 * HALF_ROWS // devices)
-    half_rows = wave_rows * chips
-    scalars = jnp.concatenate([atom_count, lax.axis_index("core").reshape(1)])
+    half = CHUNKS * HALF_ROWS
+    rows = half + channels
+    width = rows // chips * 128
 
     keep, give, outgoing = pl.pallas_call(
-        front_kernel,
-        out_shape=(shape(half_rows, 128), shape(half_rows, 128), shape(channels, 128)),
+        wave_kernel,
+        out_shape=(shape(half, 128), shape(half, 128), shape(channels, 128)),
         in_specs=scalar_first(5),
         out_specs=tuple(vmem(3)),
-        cost_estimate=work(3.0),
-    )(scalars, positions, cotangent, features, jnp.asarray(weight_table(factor)), send_map)
-    pair = keep + swapped(give)
-    pieces = exchange(pair.reshape(chips, 1, wave_rows * 128), CHIPS)
-    arrived = (
-        shifted(outgoing, SLAB, 1),
-        shifted(outgoing, SLAB, -1),
-        shifted(outgoing, "brick", 1),
-        shifted(outgoing, "brick", -1),
-    )
-    mine = everywhere(jnp.sum(pieces, axis=0), CHIPS).reshape(half_rows, 128)
-    other = swapped(mine)
-
-    own, ghost, small = pl.pallas_call(
-        edge_kernel,
-        out_shape=(shape(channels, atoms), shape(channels, 128), shape(devices, 128)),
-        in_specs=scalar_first(10),
+        cost_estimate=work(4.0),
+    )(atom_count, positions, cotangent, features, jnp.asarray(weight_table(factor)), send_map)
+    right = shifted(outgoing, "brick", 1)
+    left = shifted(outgoing, "brick", -1)
+    up = shifted(outgoing, SLAB, 1)
+    down = shifted(outgoing, SLAB, -1)
+    taken = swapped(give)
+
+    own, ghost, payload = pl.pallas_call(
+        functools.partial(edge_kernel, factor=factor),
+        out_shape=(shape(channels, atoms), shape(channels, 128), shape(rows, 128)),
+        in_specs=scalar_first(12),
         out_specs=tuple(vmem(3)),
         scratch_shapes=[
             pltpu.VMEM((slots * 8, atoms), F32),
-            pltpu.VMEM((slots, atoms + 128, atoms), BF16),
-            pltpu.VMEM((slots, channels, atoms), F32),
-            pltpu.VMEM((slots, channels, atoms), F32),
+            pltpu.VMEM((slots // 4, atoms + 128, 4 * atoms), BF16),
+            pltpu.VMEM((slots // 4, channels, 4 * atoms), F32),
+            pltpu.VMEM((slots // 4, channels, 4 * atoms), F32),
         ],
         cost_estimate=work(10.0),
     )(
-        scalars,
+        atom_count,
         features,
-        *arrived,
+        right,
+        left,
+        up,
+        down,
         cotangent,
         edge_length,
         neighbors,
         short_weight,
-        radial_weight,
-    )
-    small_all = everywhere(jnp.sum(exchange(small[:, None, :], ALL), axis=0), ALL)
+        radial_weight.T,
+        keep,
+        taken,
+    )
+    pieces = exchange(payload.reshape(chips, 1, width), CHIPS)
     back = (
+        shifted(ghost, "brick", -1),
+        shifted(ghost, "brick", 1),
         shifted(ghost, SLAB, -1),
         shifted(ghost, SLAB, 1),
-        shifted(ghost, "brick", -1),
-        shifted(ghost, "brick", 1),
     )
     partial = pl.pallas_call(
         return_kernel,
@@ -452,20 +476,22 @@
         out_specs=vmem(1)[0],
         cost_estimate=work(2.0),
     )(*back, own, send_map, short_weight)
-    charge_grad, feature_grad = pl.pallas_call(
-        lambda *refs: charge_kernel(*refs, factor=factor),
-        out_shape=(shape(channels, channels), shape(channels, atoms)),
+    summed, partial = lax.optimization_barrier((jnp.sum(pieces, axis=0), partial))
+    mine = everywhere(summed, CHIPS).reshape(rows, 128)
+    other = swapped(mine)
+    charge_grad, feature_grad, short_grad, radial_grad = pl.pallas_call(
+        functools.partial(charge_kernel, factor=factor),
+        out_shape=(
+            shape(channels, channels),
+            shape(channels, atoms),
+            shape(channels, channels),
+            shape(radial_weight.shape[1], channels),
+        ),
         in_specs=scalar_first(5),
-        out_specs=tuple(vmem(2)),
+        out_specs=tuple(vmem(4)),
         cost_estimate=work(3.0),
-    )(scalars, positions, mine, other, partial, charge_weight)
-    small_rows = small_all.reshape(channels, devices // channels, 128)[:, 0]
-    return (
-        feature_grad,
-        small_rows[:, :channels],
-        charge_grad,
-        small_rows[:, channels : channels + radial_weight.shape[1]],
-    )
+    )(atom_count, positions, mine, other, partial, charge_weight)
+    return feature_grad, short_grad, charge_grad, radial_grad.T
 
 
 def solution(mesh):

time: 130 us -> 103 us (0.79)
  starting transfers between devices: 70.3 us -> 38.8 us
  blocking collectives: 0 us -> 21.6 us
  waiting for transfers between devices: 27 us -> 18.3 us
  local copies, waits for them, and re-layouts: 6.23 us -> 2.3 us
  other arithmetic: 3.02 us -> 0.3 us
  Pallas kernels: 21.3 us -> 19.9 us
    all_to_all x4 -> x1, starting transfers between devices: 41 us -> 7.08 us  [exchange(): return lax.all_to_all(value, axes, 0, 0, tiled=True)]
    all_to_all x0 -> x1, blocking collectives: none -> 21.6 us  [exchange(): return lax.all_to_all(value, axes, 0, 0, tiled=True)]
    all_to_all x4 -> x1, waiting for transfers between devices: 14.6 us -> 0.01 us  [exchange(): return lax.all_to_all(value, axes, 0, 0, tiled=True)]
    ppermute x8, waiting for transfers between devices: 10.9 us -> 16.9 us  [shifted(): lax.ppermute(value, axis, [(i, (i + step) % size) for i in range(size)])]
    ppermute x2, starting transfers between devices: 5.47 us -> 8.72 us  [swapped(): return lax.ppermute(value, 'core', [(0, 1), (1, 0)])]
    unnamed x30 -> x24, local copies, waits for them, and re-layouts: 4.45 us -> 2.09 us
    add x1 -> x0, other arithmetic: 1.8 us -> none  [on_device(): pair = keep + swapped(give)]
    broadcast_in_dim x2 -> x1, local copies, waits for them, and re-layouts: 1.68 us -> 0.2 us  [everywhere(): return exchange(jnp.broadcast_to(value[None], (size,) + value.shape), axes)]
  transfers between devices with their start and end apart: 14 -> 11, of which waited for: 6 -> 4; matrix products, arithmetic and copies ran while one was open for 3% -> 0% of each run, Pallas kernels for 11% -> 2%
where the time goes in v3:
time: 103 us
  starting transfers between devices  38.8 us (38%)
  blocking collectives  21.6 us (21%)
  Pallas kernels  19.9 us (19%)
  waiting for transfers between devices  18.3 us (18%)
  local copies, waits for them, and re-layouts  2.3 us (2%)
  between operations  1.39 us (1%)
    ppermute x8, starting transfers between devices, shifted(): lax.ppermute(value, axis, [(i, (i + step) % size) for i in range(size)])  23 us
    all_to_all x1, blocking collectives, exchange(): return lax.all_to_all(value, axes, 0, 0, tiled=True)  21.6 us
    ppermute x8, waiting for transfers between devices, shifted(): lax.ppermute(value, axis, [(i, (i + step) % size) for i in range(size)])  16.9 us
    pallas_call x1, Pallas kernels, on_device(): pl.pallas_call(functools.partial(edge_kernel, factor=factor), out_shape=(...  10.4 us
    ppermute x2, starting transfers between devices, swapped(): return lax.ppermute(value, 'core', [(0, 1), (1, 0)])  8.72 us
    all_to_all x1, starting transfers between devices, exchange(): return lax.all_to_all(value, axes, 0, 0, tiled=True)  7.08 us
    pallas_call x1, Pallas kernels, on_device(): pl.pallas_call(wave_kernel, out_shape=(shape(half, 128), shape(half, 128)...  4.52 us
    pallas_call x1, Pallas kernels, on_device(): pl.pallas_call(functools.partial(charge_kernel, factor=factor), out_shape...  2.9 us
  transfers between devices with their start and end apart: 11, of which 4 were waited for; matrix products, arithmetic and copies ran while one was open for 0% of the time, Pallas kernels for 2%

profile of v3, /device:TPU:1, one launch (start us, length us, event | category | flops | bytes accessed | tf_op | source)
XLA Modules:
  0.0 102.6 jit_solution(18092888585626371610)
XLA Ops:
  1.3 4.5 %shard_map.138 = (f32[704,128]{1,0:T(8,128)}, f32[704,128]{1,0:T(8,128)}, f32[64,128]{1,0:T(8,128)}) custom-call(s32[1]{0:T(128)S(6)} %copy.16.count_ref, f32[3,256]{1,0:T(4,128)} %positions_ref.3, f32[64,256]{1,0:T(8,128)} %cotangent_ref.3, f32[64,256]{1,0:T(8,128)} %features_ref.3, f32[704,128]{1,0:T(8,128)} %constant.4.clone.table_ref, s32[4,16]{1,0:T(4,128)} %map_ref.3), custom_call_target="tpu_custom_call" | custom-call | flops 4000000000 | bytes 12000000 | tf_op jit(solution)/shard_map/pallas_call | solution.py:425
  5.8 3.2 %collective-permute-start.4 = (f32[704,128]{1,0:T(8,128)}, f32[704,128]{1,0:T(8,128)S(1)}, u32[]{:S(2)}, u32[]{:S(2)}) collective-permute-start(f32[704,128]{1,0:T(8,128)} %get-tuple-element.18), channel_id=1, source_target_pairs={{0,32},{32,0},{1,33},{33,1},{2,34},{34,2},{3,35},{35,3},{4,36},{36... | collective-permute-start | bytes 1081352 | tf_op jit(solution)/shard_map/ppermute | solution.py:392
  9.0 0.0 collective-permute-start.3
  9.0 1.7 %collective-permute-start.2 = (f32[64,128]{1,0:T(8,128)}, f32[64,128]{1,0:T(8,128)S(1)}, u32[]{:S(2)}, u32[]{:S(2)}) collective-permute-start(f32[64,128]{1,0:T(8,128)} %get-tuple-element.16), channel_id=1, source_target_pairs={{0,32},{32,64},{64,96},{96,128},{128,160},{160,192},{192,224},{224... | collective-permute-start | bytes 98312 | tf_op jit(solution)/shard_map/ppermute | solution.py:388
  10.8 9.8 %collective-permute-start.1 = (f32[64,128]{1,0:T(8,128)}, f32[64,128]{1,0:T(8,128)S(1)}, u32[]{:S(2)}, u32[]{:S(2)}) collective-permute-start(f32[64,128]{1,0:T(8,128)} %get-tuple-element.16), channel_id=1, source_target_pairs={{0,31},{1,0},{2,1},{3,2},{4,3},{5,4},{6,5},{7,6},{8,7},{9,8},{10,9... | collective-permute-start | bytes 98312 | tf_op jit(solution)/shard_map/ppermute | solution.py:388
  20.6 0.0 collective-permute-start
  20.6 0.0 collective-permute-done.3.down_ref
  20.6 0.0 copy-start.4
  20.6 0.0 collective-permute-done.2.up_ref
  20.6 0.0 copy-start.5
  20.6 1.3 %collective-permute-done.1.left_ref = f32[64,128]{1,0:T(8,128)S(1)} collective-permute-done((f32[64,128]{1,0:T(8,128)}, f32[64,128]{1,0:T(8,128)S(1)}, u32[]{:S(2)}, u32[]{:S(2)}) %collective-permute-start.1) | collective-permute-done | bytes 32800 | tf_op jit(solution)/shard_map/ppermute | solution.py:388
  21.9 0.0 copy-start.6
  21.9 9.8 %collective-permute-done.right_ref = f32[64,128]{1,0:T(8,128)S(1)} collective-permute-done((f32[64,128]{1,0:T(8,128)}, f32[64,128]{1,0:T(8,128)S(1)}, u32[]{:S(2)}, u32[]{:S(2)}) %collective-permute-start) | collective-permute-done | bytes 32800 | tf_op jit(solution)/shard_map/ppermute | solution.py:388
  31.7 0.0 copy-start.8
  31.7 0.0 collective-permute-done.4.taken_ref
  31.7 0.0 copy-start.2
  31.7 0.0 copy-done.4
  31.7 0.0 copy-done.5
  31.7 0.0 copy-done.6
  31.7 0.6 copy-done.8
  32.3 0.1 copy-done.2
  32.5 10.4 %shard_map.139 = (f32[64,256]{1,0:T(8,128)}, f32[64,128]{1,0:T(8,128)}, f32[768,128]{1,0:T(8,128)}) custom-call(s32[1]{0:T(128)S(6)} %copy.16.count_ref, f32[64,256]{1,0:T(8,128)} %features_ref.3, f32[64,128]{1,0:T(8,128)} %copy-done.8, f32[64,128]{1,0:T(8,128)} %copy-done.6, f32[64,128]{1,0:T(8,128)} %copy-done.5, f32[64,128]{1,0:T(8,128)} %copy-done.4, ...), custom_call_target="tpu_custom_call" | custom-call | flops 10000000000 | bytes 30000000 | tf_op jit(solution)/shard_map/pallas_call | solution.py:438
  42.8 0.0 copy-start.3
  42.8 7.1 %all-to-all-start = ((f32[128,1,768]{2,1,0:T(1,128)}), f32[128,1,768]{2,1,0:T(1,128)S(1)}, u32[]{:S(2)}, u32[]{:S(2)}) async-start(f32[128,1,768]{2,1,0:T(1,128)} %bitcast.4), calls=%async_computation | async-start | bytes 786432 | tf_op jit(solution)/shard_map/all_to_all | solution.py:396
  49.9 0.0 copy-done.3
  49.9 1.9 %collective-permute-start.8 = (f32[64,128]{1,0:T(8,128)S(1)}, f32[64,128]{1,0:T(8,128)S(1)}, u32[]{:S(2)}, u32[]{:S(2)}) collective-permute-start(f32[64,128]{1,0:T(8,128)S(1)} %copy-done.3), channel_id=1, source_target_pairs={{0,32},{32,64},{64,96},{96,128},{128,160},{160,192},{192,224},{224... | collective-permute-start | bytes 98312 | tf_op jit(solution)/shard_map/ppermute | solution.py:388
  51.8 0.0 collective-permute-start.7
  51.8 4.2 %collective-permute-start.6 = (f32[64,128]{1,0:T(8,128)S(1)}, f32[64,128]{1,0:T(8,128)S(1)}, u32[]{:S(2)}, u32[]{:S(2)}) collective-permute-start(f32[64,128]{1,0:T(8,128)S(1)} %copy-done.3), channel_id=1, source_target_pairs={{0,1},{1,2},{2,3},{3,4},{4,5},{5,6},{6,7},{7,8},{8,9},{9,10},{10,1... | collective-permute-start | bytes 98312 | tf_op jit(solution)/shard_map/ppermute | solution.py:388
  56.0 5.4 %collective-permute-start.5 = (f32[64,128]{1,0:T(8,128)S(1)}, f32[64,128]{1,0:T(8,128)S(1)}, u32[]{:S(2)}, u32[]{:S(2)}) collective-permute-start(f32[64,128]{1,0:T(8,128)S(1)} %copy-done.3), channel_id=1, source_target_pairs={{0,31},{1,0},{2,1},{3,2},{4,3},{5,4},{6,5},{7,6},{8,7},{9,8},{10,9... | collective-permute-start | bytes 98312 | tf_op jit(solution)/shard_map/ppermute | solution.py:388
  61.4 0.0 collective-permute-done.8.down_ref
  61.4 0.0 collective-permute-done.7.up_ref
  61.4 0.0 copy-start.9
  61.4 5.8 %collective-permute-done.6.left_ref = f32[64,128]{1,0:T(8,128)S(1)} collective-permute-done((f32[64,128]{1,0:T(8,128)S(1)}, f32[64,128]{1,0:T(8,128)S(1)}, u32[]{:S(2)}, u32[]{:S(2)}) %collective-permute-start.6) | collective-permute-done | bytes 32800 | tf_op jit(solution)/shard_map/ppermute | solution.py:388
  67.2 0.0 collective-permute-done.5.right_ref
  67.2 0.0 copy-done.7
  67.2 0.0 copy-done.9
  67.2 0.6 copy-done.10
  67.8 0.0 copy-done.11
  67.8 2.1 %shard_map.140.partial_ref = f32[64,256]{1,0:T(8,128)} custom-call(f32[64,128]{1,0:T(8,128)} %copy-done.11, f32[64,128]{1,0:T(8,128)} %copy-done.10, f32[64,128]{1,0:T(8,128)} %copy-done.9, f32[64,128]{1,0:T(8,128)} %copy-done.7, f32[64,256]{1,0:T(8,128)} %get-tuple-element.21.own_ref, s32[4,16]{1,0:T(4,128)} %map_ref.3, f32[64,64]{1,0:T(8,128)} %short_ref.3), custom_call_target="tpu_custom_call" | custom-call | flops 2000000000 | bytes 6000000 | tf_op jit(solution)/shard_map/pallas_call | solution.py:472
  70.0 0.0 all-to-all-done
  70.0 0.3 reduce_sum.11
  70.3 0.2 broadcast_in_dim.9
  70.5 21.6 %all_to_all.10 = f32[128,1,768]{2,1,0:T(1,128)S(1)} all-to-all(f32[128,1,768]{2,1,0:T(1,128)S(1)} %broadcast_in_dim.9), channel_id=1, replica_groups=mesh['chip'=4,'core'=2,'brick'=32] {'chip','brick'}, dimensions={0} | all-to-all | bytes 786432 | tf_op jit(solution)/shard_map/all_to_all | solution.py:396
  92.2 5.5 %collective-permute-start.9 = (f32[768,128]{1,0:T(8,128)S(1)}, f32[768,128]{1,0:T(8,128)S(1)}, u32[]{:S(2)}, u32[]{:S(2)}) collective-permute-start(f32[768,128]{1,0:T(8,128)S(1)} %bitcast.5), channel_id=1, source_target_pairs={{0,32},{32,0},{1,33},{33,1},{2,34},{34,2},{3,35},{35,3},{4,36},{36... | collective-permute-start | bytes 1179656 | tf_op jit(solution)/shard_map/ppermute | solution.py:392
  97.6 1.3 %collective-permute-done.9.other_ref = f32[768,128]{1,0:T(8,128)S(1)} collective-permute-done((f32[768,128]{1,0:T(8,128)S(1)}, f32[768,128]{1,0:T(8,128)S(1)}, u32[]{:S(2)}, u32[]{:S(2)}) %collective-permute-start.9) | collective-permute-done | bytes 393248 | tf_op jit(solution)/shard_map/ppermute | solution.py:392
  99.0 0.0 copy-done
  99.0 0.7 copy-done.1
  99.7 2.9 %shard_map.141 = (f32[64,64]{1,0:T(8,128)}, f32[64,256]{1,0:T(8,128)}, f32[64,64]{1,0:T(8,128)}, f32[8,64]{1,0:T(8,128)}) custom-call(s32[1]{0:T(128)S(6)} %copy.16.count_ref, f32[3,256]{1,0:T(4,128)} %positions_ref.3, f32[768,128]{1,0:T(8,128)} %bitcast.6, f32[768,128]{1,0:T(8,128)} %copy-done.1, f32[64,256]{1,0:T(8,128)} %shard_map.140.partial_ref, ...), custom_call_target="tpu_custom_call" | custom-call | flops 3000000000 | bytes 9000000 | tf_op jit(solution)/shard_map/pallas_call | solution.py:482
  (7 shorter events, 0.0 us)
Async XLA Ops:
  5.8 25.9 %collective-permute-start.4 = (f32[704,128]{1,0:T(8,128)}, f32[704,128]{1,0:T(8,128)S(1)}, u32[]{:S(2)}, u32[]{:S(2)}) collective-permute-start(f32[704,128]{1,0:T(8,128)} %get-tuple-element.18), channel_id=1, source_target_pairs={{0,32},{32,0},{1,33},{33,1},{2,34},{34,2},{3,35},{35,3},{4,36},{36... | collective-permute-start | bytes 1081352 | tf_op jit(solution)/shard_map/ppermute | solution.py:392
  9.0 11.6 %collective-permute-start.3 = (f32[64,128]{1,0:T(8,128)}, f32[64,128]{1,0:T(8,128)S(1)}, u32[]{:S(2)}, u32[]{:S(2)}) collective-permute-start(f32[64,128]{1,0:T(8,128)} %get-tuple-element.16), channel_id=1, source_target_pairs={{0,224},{32,0},{64,32},{96,64},{128,96},{160,128},{192,160},{224,1... | collective-permute-start | bytes 98312 | tf_op jit(solution)/shard_map/ppermute | solution.py:388
  9.0 11.6 %collective-permute-start.2 = (f32[64,128]{1,0:T(8,128)}, f32[64,128]{1,0:T(8,128)S(1)}, u32[]{:S(2)}, u32[]{:S(2)}) collective-permute-start(f32[64,128]{1,0:T(8,128)} %get-tuple-element.16), channel_id=1, source_target_pairs={{0,32},{32,64},{64,96},{96,128},{128,160},{160,192},{192,224},{224... | collective-permute-start | bytes 98312 | tf_op jit(solution)/shard_map/ppermute | solution.py:388
  10.8 11.2 %collective-permute-start.1 = (f32[64,128]{1,0:T(8,128)}, f32[64,128]{1,0:T(8,128)S(1)}, u32[]{:S(2)}, u32[]{:S(2)}) collective-permute-start(f32[64,128]{1,0:T(8,128)} %get-tuple-element.16), channel_id=1, source_target_pairs={{0,31},{1,0},{2,1},{3,2},{4,3},{5,4},{6,5},{7,6},{8,7},{9,8},{10,9... | collective-permute-start | bytes 98312 | tf_op jit(solution)/shard_map/ppermute | solution.py:388
  20.6 11.1 %collective-permute-start = (f32[64,128]{1,0:T(8,128)}, f32[64,128]{1,0:T(8,128)S(1)}, u32[]{:S(2)}, u32[]{:S(2)}) collective-permute-start(f32[64,128]{1,0:T(8,128)} %get-tuple-element.16), channel_id=1, source_target_pairs={{0,1},{1,2},{2,3},{3,4},{4,5},{5,6},{6,7},{7,8},{8,9},{9,10},{10,1... | collective-permute-start | bytes 98312 | tf_op jit(solution)/shard_map/ppermute | solution.py:388
  20.6 11.1 %copy-start.4 = (f32[64,128]{1,0:T(8,128)}, f32[64,128]{1,0:T(8,128)S(1)}, u32[]{:S(2)}) copy-start(f32[64,128]{1,0:T(8,128)S(1)} %collective-permute-done.3.down_ref) | copy-start | bytes 98308
  20.6 11.1 %copy-start.5 = (f32[64,128]{1,0:T(8,128)}, f32[64,128]{1,0:T(8,128)S(1)}, u32[]{:S(2)}) copy-start(f32[64,128]{1,0:T(8,128)S(1)} %collective-permute-done.2.up_ref) | copy-start | bytes 98308
  21.9 9.8 %copy-start.6 = (f32[64,128]{1,0:T(8,128)}, f32[64,128]{1,0:T(8,128)S(1)}, u32[]{:S(2)}) copy-start(f32[64,128]{1,0:T(8,128)S(1)} %collective-permute-done.1.left_ref) | copy-start | bytes 98308
  31.7 0.6 copy-start.8
  31.7 0.7 copy-start.2
  42.8 7.1 %copy-start.3 = (f32[64,128]{1,0:T(8,128)S(1)}, f32[64,128]{1,0:T(8,128)}, u32[]{:S(2)}) copy-start(f32[64,128]{1,0:T(8,128)} %get-tuple-element.20) | copy-start | bytes 98308
  42.8 27.2 %all-to-all-start = ((f32[128,1,768]{2,1,0:T(1,128)}), f32[128,1,768]{2,1,0:T(1,128)S(1)}, u32[]{:S(2)}, u32[]{:S(2)}) async-start(f32[128,1,768]{2,1,0:T(1,128)} %bitcast.4), calls=%async_computation | async-start | bytes 786432 | tf_op jit(solution)/shard_map/all_to_all | solution.py:396
  49.9 11.5 %collective-permute-start.8 = (f32[64,128]{1,0:T(8,128)S(1)}, f32[64,128]{1,0:T(8,128)S(1)}, u32[]{:S(2)}, u32[]{:S(2)}) collective-permute-start(f32[64,128]{1,0:T(8,128)S(1)} %copy-done.3), channel_id=1, source_target_pairs={{0,32},{32,64},{64,96},{96,128},{128,160},{160,192},{192,224},{224... | collective-permute-start | bytes 98312 | tf_op jit(solution)/shard_map/ppermute | solution.py:388
  51.8 9.6 %collective-permute-start.7 = (f32[64,128]{1,0:T(8,128)S(1)}, f32[64,128]{1,0:T(8,128)S(1)}, u32[]{:S(2)}, u32[]{:S(2)}) collective-permute-start(f32[64,128]{1,0:T(8,128)S(1)} %copy-done.3), channel_id=1, source_target_pairs={{0,224},{32,0},{64,32},{96,64},{128,96},{160,128},{192,160},{224,1... | collective-permute-start | bytes 98312 | tf_op jit(solution)/shard_map/ppermute | solution.py:388
  51.8 15.4 %collective-permute-start.6 = (f32[64,128]{1,0:T(8,128)S(1)}, f32[64,128]{1,0:T(8,128)S(1)}, u32[]{:S(2)}, u32[]{:S(2)}) collective-permute-start(f32[64,128]{1,0:T(8,128)S(1)} %copy-done.3), channel_id=1, source_target_pairs={{0,1},{1,2},{2,3},{3,4},{4,5},{5,6},{6,7},{7,8},{8,9},{9,10},{10,1... | collective-permute-start | bytes 98312 | tf_op jit(solution)/shard_map/ppermute | solution.py:388
  56.0 11.2 %collective-permute-start.5 = (f32[64,128]{1,0:T(8,128)S(1)}, f32[64,128]{1,0:T(8,128)S(1)}, u32[]{:S(2)}, u32[]{:S(2)}) collective-permute-start(f32[64,128]{1,0:T(8,128)S(1)} %copy-done.3), channel_id=1, source_target_pairs={{0,31},{1,0},{2,1},{3,2},{4,3},{5,4},{6,5},{7,6},{8,7},{9,8},{10,9... | collective-permute-start | bytes 98312 | tf_op jit(solution)/shard_map/ppermute | solution.py:388
  61.4 5.9 %copy-start.7 = (f32[64,128]{1,0:T(8,128)}, f32[64,128]{1,0:T(8,128)S(1)}, u32[]{:S(2)}) copy-start(f32[64,128]{1,0:T(8,128)S(1)} %collective-permute-done.8.down_ref) | copy-start | bytes 98308
  61.4 5.8 %copy-start.9 = (f32[64,128]{1,0:T(8,128)}, f32[64,128]{1,0:T(8,128)S(1)}, u32[]{:S(2)}) copy-start(f32[64,128]{1,0:T(8,128)S(1)} %collective-permute-done.7.up_ref) | copy-start | bytes 98308
  67.2 0.6 copy-start.10
  67.2 0.6 copy-start.11
  92.1 6.8 %copy-start = (f32[128,1,768]{2,1,0:T(1,128)}, f32[128,1,768]{2,1,0:T(1,128)S(1)}, u32[]{:S(2)}) copy-start(f32[128,1,768]{2,1,0:T(1,128)S(1)} %all_to_all.10) | copy-start | bytes 1179652
  92.2 6.8 %collective-permute-start.9 = (f32[768,128]{1,0:T(8,128)S(1)}, f32[768,128]{1,0:T(8,128)S(1)}, u32[]{:S(2)}, u32[]{:S(2)}) collective-permute-start(f32[768,128]{1,0:T(8,128)S(1)} %bitcast.5), channel_id=1, source_target_pairs={{0,32},{32,0},{1,33},{33,1},{2,34},{34,2},{3,35},{35,3},{4,36},{36... | collective-permute-start | bytes 1179656 | tf_op jit(solution)/shard_map/ppermute | solution.py:392
  99.0 0.7 copy-start.1

commit v4 on v3

--- a/solution.py
+++ b/solution.py
@@ -201,10 +201,10 @@
 def edge_kernel(
     count_ref,
     features_ref,
+    left_ref,
     right_ref,
-    left_ref,
+    down_ref,
     up_ref,
-    down_ref,
     cotangent_ref,
     length_ref,
     neighbor_ref,
@@ -450,10 +450,10 @@
     )(
         atom_count,
         features,
+        left,
         right,
-        left,
+        down,
         up,
-        down,
         cotangent,
         edge_length,
         neighbors,
@@ -463,21 +463,22 @@
         taken,
     )
     pieces = exchange(payload.reshape(chips, 1, width), CHIPS)
-    back = (
-        shifted(ghost, "brick", -1),
-        shifted(ghost, "brick", 1),
-        shifted(ghost, SLAB, -1),
-        shifted(ghost, SLAB, 1),
-    )
+    back_left = shifted(ghost, "brick", -1)
+    back_right = shifted(ghost, "brick", 1)
+    back_down = shifted(ghost, SLAB, -1)
+    back_up = shifted(ghost, SLAB, 1)
+    summed, back_left, back_right = lax.optimization_barrier(
+        (jnp.sum(pieces, axis=0), back_left, back_right)
+    )
+    mine = everywhere(summed, CHIPS).reshape(rows, 128)
     partial = pl.pallas_call(
         return_kernel,
         out_shape=shape(channels, atoms),
         in_specs=vmem(7),
         out_specs=vmem(1)[0],
         cost_estimate=work(2.0),
-    )(*back, own, send_map, short_weight)
-    summed, partial = lax.optimization_barrier((jnp.sum(pieces, axis=0), partial))
-    mine = everywhere(summed, CHIPS).reshape(rows, 128)
+    )(back_left, back_right, back_down, back_up, own, send_map, short_weight)
+    mine, partial = lax.optimization_barrier((mine, partial))
     other = swapped(mine)
     charge_grad, feature_grad, short_grad, radial_grad = pl.pallas_call(
         functools.partial(charge_kernel, factor=factor),

time: 103 us -> 97 us (0.942)
  blocking collectives: 21.6 us -> 0 us
  starting transfers between devices: 38.8 us -> 59 us
  waiting for transfers between devices: 18.3 us -> 13 us
    all_to_all x1 -> x0, blocking collectives: 21.6 us -> none  [exchange(): return lax.all_to_all(value, axes, 0, 0, tiled=True)]
    all_to_all x1 -> x2, starting transfers between devices: 7.08 us -> 23.5 us  [exchange(): return lax.all_to_all(value, axes, 0, 0, tiled=True)]
    ppermute x8, waiting for transfers between devices: 16.9 us -> 8.62 us  [shifted(): lax.ppermute(value, axis, [(i, (i + step) % size) for i in range(size)])]
    ppermute x8, starting transfers between devices: 23 us -> 26.6 us  [shifted(): lax.ppermute(value, axis, [(i, (i + step) % size) for i in range(size)])]
    all_to_all x1 -> x2, waiting for transfers between devices: 0.01 us -> 3 us  [exchange(): return lax.all_to_all(value, axes, 0, 0, tiled=True)]
  transfers between devices with their start and end apart: 11 -> 12, of which waited for: 4 -> 7; matrix products, arithmetic and copies ran while one was open for 0% -> 0% of each run, Pallas kernels for 2% -> 2%
where the time goes in v4:
time: 97 us; the launch traced here: 96.6 us
  starting transfers between devices  59 us (61%)
  Pallas kernels  19.9 us (21%)
  waiting for transfers between devices  13 us (13%)
  local copies, waits for them, and re-layouts  3.06 us (3%)
  between operations  1.35 us (1%)
    ppermute x8, starting transfers between devices, shifted(): lax.ppermute(value, axis, [(i, (i + step) % size) for i in range(size)])  26.6 us
    all_to_all x2, starting transfers between devices, exchange(): return lax.all_to_all(value, axes, 0, 0, tiled=True)  23.5 us
    pallas_call x1, Pallas kernels, on_device(): pl.pallas_call(functools.partial(edge_kernel, factor=factor), out_shape=(...  10.4 us
    ppermute x2, starting transfers between devices, swapped(): return lax.ppermute(value, 'core', [(0, 1), (1, 0)])  8.82 us
    ppermute x8, waiting for transfers between devices, shifted(): lax.ppermute(value, axis, [(i, (i + step) % size) for i in range(size)])  8.62 us
    pallas_call x1, Pallas kernels, on_device(): pl.pallas_call(wave_kernel, out_shape=(shape(half, 128), shape(half, 128)...  4.51 us
    all_to_all x2, waiting for transfers between devices, exchange(): return lax.all_to_all(value, axes, 0, 0, tiled=True)  3 us
    pallas_call x1, Pallas kernels, on_device(): pl.pallas_call(functools.partial(charge_kernel, factor=factor), out_shape...  2.9 us
  transfers between devices with their start and end apart: 12, of which 7 were waited for; matrix products, arithmetic and copies ran while one was open for 0% of the time, Pallas kernels for 2%

profile of v4, /device:TPU:1, one launch (start us, length us, event | category | flops | bytes accessed | tf_op | source)
XLA Modules:
  0.0 96.6 jit_solution(9134334222738041740)
XLA Ops:
  1.3 4.5 %shard_map.138 = (f32[704,128]{1,0:T(8,128)}, f32[704,128]{1,0:T(8,128)}, f32[64,128]{1,0:T(8,128)}) custom-call(s32[1]{0:T(128)S(6)} %copy.16.count_ref, f32[3,256]{1,0:T(4,128)} %positions_ref.3, f32[64,256]{1,0:T(8,128)} %cotangent_ref.3, f32[64,256]{1,0:T(8,128)} %features_ref.3, f32[704,128]{1,0:T(8,128)} %constant.4.clone.table_ref, s32[4,16]{1,0:T(4,128)} %map_ref.3), custom_call_target="tpu_custom_call" | custom-call | flops 4000000000 | bytes 12000000 | tf_op jit(solution)/shard_map/pallas_call | solution.py:425
  5.8 3.2 %collective-permute-start.4 = (f32[704,128]{1,0:T(8,128)}, f32[704,128]{1,0:T(8,128)S(1)}, u32[]{:S(2)}, u32[]{:S(2)}) collective-permute-start(f32[704,128]{1,0:T(8,128)} %get-tuple-element.21), channel_id=1, source_target_pairs={{0,32},{32,0},{1,33},{33,1},{2,34},{34,2},{3,35},{35,3},{4,36},{36... | collective-permute-start | bytes 1081352 | tf_op jit(solution)/shard_map/ppermute | solution.py:392
  9.0 0.0 collective-permute-start.3
  9.0 0.5 collective-permute-start.2
  9.5 5.3 %collective-permute-start.1 = (f32[64,128]{1,0:T(8,128)}, f32[64,128]{1,0:T(8,128)S(1)}, u32[]{:S(2)}, u32[]{:S(2)}) collective-permute-start(f32[64,128]{1,0:T(8,128)} %get-tuple-element.19), channel_id=1, source_target_pairs={{0,1},{1,2},{2,3},{3,4},{4,5},{5,6},{6,7},{7,8},{8,9},{9,10},{10,1... | collective-permute-start | bytes 98312 | tf_op jit(solution)/shard_map/ppermute | solution.py:388
  14.8 4.6 %collective-permute-start = (f32[64,128]{1,0:T(8,128)}, f32[64,128]{1,0:T(8,128)S(1)}, u32[]{:S(2)}, u32[]{:S(2)}) collective-permute-start(f32[64,128]{1,0:T(8,128)} %get-tuple-element.19), channel_id=1, source_target_pairs={{0,31},{1,0},{2,1},{3,2},{4,3},{5,4},{6,5},{7,6},{8,7},{9,8},{10,9... | collective-permute-start | bytes 98312 | tf_op jit(solution)/shard_map/ppermute | solution.py:388
  19.5 0.0 collective-permute-done.3.up_ref
  19.5 0.0 copy-start.6
  19.5 0.0 collective-permute-done.2.down_ref
  19.5 0.0 copy-start.7
  19.5 1.8 %collective-permute-done.1.right_ref = f32[64,128]{1,0:T(8,128)S(1)} collective-permute-done((f32[64,128]{1,0:T(8,128)}, f32[64,128]{1,0:T(8,128)S(1)}, u32[]{:S(2)}, u32[]{:S(2)}) %collective-permute-start.1) | collective-permute-done | bytes 32800 | tf_op jit(solution)/shard_map/ppermute | solution.py:388
  21.4 0.0 copy-start.8
  21.4 0.4 collective-permute-done.left_ref
  21.7 0.0 copy-start.9
  21.7 0.0 collective-permute-done.4.taken_ref
  21.7 0.0 copy-start.2
  21.7 0.0 copy-done.6
  21.7 0.0 copy-done.7
  21.7 0.2 copy-done.8
  22.0 0.4 copy-done.9
  22.3 0.1 copy-done.2
  22.5 10.4 %shard_map.139 = (f32[64,256]{1,0:T(8,128)}, f32[64,128]{1,0:T(8,128)}, f32[768,128]{1,0:T(8,128)}) custom-call(s32[1]{0:T(128)S(6)} %copy.16.count_ref, f32[64,256]{1,0:T(8,128)} %features_ref.3, f32[64,128]{1,0:T(8,128)} %copy-done.9, f32[64,128]{1,0:T(8,128)} %copy-done.8, f32[64,128]{1,0:T(8,128)} %copy-done.7, f32[64,128]{1,0:T(8,128)} %copy-done.6, ...), custom_call_target="tpu_custom_call" | custom-call | flops 10000000000 | bytes 30000000 | tf_op jit(solution)/shard_map/pallas_call | solution.py:438
  32.9 12.7 %all-to-all-start = ((f32[128,1,768]{2,1,0:T(1,128)}), f32[128,1,768]{2,1,0:T(1,128)S(1)}, u32[]{:S(2)}, u32[]{:S(2)}) async-start(f32[128,1,768]{2,1,0:T(1,128)} %bitcast.6), calls=%async_computation | async-start | bytes 786432 | tf_op jit(solution)/shard_map/all_to_all | solution.py:396
  45.5 0.0 copy-done.3
  45.6 4.6 %collective-permute-start.6 = (f32[64,128]{1,0:T(8,128)S(1)}, f32[64,128]{1,0:T(8,128)S(1)}, u32[]{:S(2)}, u32[]{:S(2)}) collective-permute-start(f32[64,128]{1,0:T(8,128)S(1)} %copy-done.3), channel_id=1, source_target_pairs={{0,1},{1,2},{2,3},{3,4},{4,5},{5,6},{6,7},{7,8},{8,9},{9,10},{10,1... | collective-permute-start | bytes 98312 | tf_op jit(solution)/shard_map/ppermute | solution.py:388
  50.1 5.1 %collective-permute-start.5 = (f32[64,128]{1,0:T(8,128)S(1)}, f32[64,128]{1,0:T(8,128)S(1)}, u32[]{:S(2)}, u32[]{:S(2)}) collective-permute-start(f32[64,128]{1,0:T(8,128)S(1)} %copy-done.3), channel_id=1, source_target_pairs={{0,31},{1,0},{2,1},{3,2},{4,3},{5,4},{6,5},{7,6},{8,7},{9,8},{10,9... | collective-permute-start | bytes 98312 | tf_op jit(solution)/shard_map/ppermute | solution.py:388
  55.2 3.0 %all-to-all-done = f32[128,1,768]{2,1,0:T(1,128)S(1)} async-done(((f32[128,1,768]{2,1,0:T(1,128)}), f32[128,1,768]{2,1,0:T(1,128)S(1)}, u32[]{:S(2)}, u32[]{:S(2)}) %all-to-all-start) | async-done | bytes 393248 | tf_op jit(solution)/shard_map/all_to_all | solution.py:396
  58.2 0.3 reduce_sum.11
  58.5 1.0 collective-permute-done.6.left_ref
  59.5 0.0 copy-start.4
  59.5 0.0 collective-permute-done.5.right_ref
  59.5 1.0 broadcast_in_dim.9
  60.5 0.0 copy-done.4
  60.5 0.0 copy-done.5
  60.5 10.8 %all-to-all-start.1 = ((f32[128,1,768]{2,1,0:T(1,128)}), f32[128,1,768]{2,1,0:T(1,128)S(1)}, u32[]{:S(2)}, u32[]{:S(2)}) async-start(f32[128,1,768]{2,1,0:T(1,128)} %broadcast_in_dim.9), calls=%async_computation.1 | async-start | bytes 786432 | tf_op jit(solution)/shard_map/all_to_all | solution.py:396
  71.3 6.5 %collective-permute-start.8 = (f32[64,128]{1,0:T(8,128)S(1)}, f32[64,128]{1,0:T(8,128)S(1)}, u32[]{:S(2)}, u32[]{:S(2)}) collective-permute-start(f32[64,128]{1,0:T(8,128)S(1)} %copy-done.3), channel_id=1, source_target_pairs={{0,32},{32,64},{64,96},{96,128},{128,160},{160,192},{192,224},{224... | collective-permute-start | bytes 98312 | tf_op jit(solution)/shard_map/ppermute | solution.py:388
  77.8 0.0 collective-permute-start.7
  77.8 1.3 %collective-permute-done.8.down_ref = f32[64,128]{1,0:T(8,128)S(1)} collective-permute-done((f32[64,128]{1,0:T(8,128)S(1)}, f32[64,128]{1,0:T(8,128)S(1)}, u32[]{:S(2)}, u32[]{:S(2)}) %collective-permute-start.8) | collective-permute-done | bytes 32800 | tf_op jit(solution)/shard_map/ppermute | solution.py:388
  79.1 4.2 %collective-permute-done.7.up_ref = f32[64,128]{1,0:T(8,128)S(1)} collective-permute-done((f32[64,128]{1,0:T(8,128)S(1)}, f32[64,128]{1,0:T(8,128)S(1)}, u32[]{:S(2)}, u32[]{:S(2)}) %collective-permute-start.7) | collective-permute-done | bytes 32800 | tf_op jit(solution)/shard_map/ppermute | solution.py:388
  83.2 0.0 copy-done.10
  83.2 0.6 copy-done.11
  83.8 2.1 %shard_map.140.partial_ref = f32[64,256]{1,0:T(8,128)} custom-call(f32[64,128]{1,0:T(8,128)} %copy-done.5, f32[64,128]{1,0:T(8,128)} %copy-done.4, f32[64,128]{1,0:T(8,128)} %copy-done.11, f32[64,128]{1,0:T(8,128)} %copy-done.10, f32[64,256]{1,0:T(8,128)} %get-tuple-element.27.own_ref, s32[4,16]{1,0:T(4,128)} %map_ref.3, f32[64,64]{1,0:T(8,128)} %short_ref.3), custom_call_target="tpu_custom_call" | custom-call | flops 2000000000 | bytes 6000000 | tf_op jit(solution)/shard_map/pallas_call | solution.py:474
  86.0 0.0 all-to-all-done.1
  86.0 5.6 %collective-permute-start.9 = (f32[768,128]{1,0:T(8,128)S(1)}, f32[768,128]{1,0:T(8,128)S(1)}, u32[]{:S(2)}, u32[]{:S(2)}) collective-permute-start(f32[768,128]{1,0:T(8,128)S(1)} %bitcast.4), channel_id=1, source_target_pairs={{0,32},{32,0},{1,33},{33,1},{2,34},{34,2},{3,35},{35,3},{4,36},{36... | collective-permute-start | bytes 1179656 | tf_op jit(solution)/shard_map/ppermute | solution.py:392
  91.6 1.3 %collective-permute-done.9.other_ref = f32[768,128]{1,0:T(8,128)S(1)} collective-permute-done((f32[768,128]{1,0:T(8,128)S(1)}, f32[768,128]{1,0:T(8,128)S(1)}, u32[]{:S(2)}, u32[]{:S(2)}) %collective-permute-start.9) | collective-permute-done | bytes 393248 | tf_op jit(solution)/shard_map/ppermute | solution.py:392
  92.9 0.0 copy-done
  92.9 0.7 copy-done.1
  93.6 2.9 %shard_map.141 = (f32[64,64]{1,0:T(8,128)}, f32[64,256]{1,0:T(8,128)}, f32[64,64]{1,0:T(8,128)}, f32[8,64]{1,0:T(8,128)}) custom-call(s32[1]{0:T(128)S(6)} %copy.16.count_ref, f32[3,256]{1,0:T(4,128)} %positions_ref.3, f32[768,128]{1,0:T(8,128)} %bitcast.5, f32[768,128]{1,0:T(8,128)} %copy-done.1, f32[64,256]{1,0:T(8,128)} %shard_map.140.partial_ref, ...), custom_call_target="tpu_custom_call" | custom-call | flops 3000000000 | bytes 9000000 | tf_op jit(solution)/shard_map/pallas_call | solution.py:483
  (8 shorter events, 0.0 us)
Async XLA Ops:
  5.8 15.9 %collective-permute-start.4 = (f32[704,128]{1,0:T(8,128)}, f32[704,128]{1,0:T(8,128)S(1)}, u32[]{:S(2)}, u32[]{:S(2)}) collective-permute-start(f32[704,128]{1,0:T(8,128)} %get-tuple-element.21), channel_id=1, source_target_pairs={{0,32},{32,0},{1,33},{33,1},{2,34},{34,2},{3,35},{35,3},{4,36},{36... | collective-permute-start | bytes 1081352 | tf_op jit(solution)/shard_map/ppermute | solution.py:392
  9.0 10.5 %collective-permute-start.3 = (f32[64,128]{1,0:T(8,128)}, f32[64,128]{1,0:T(8,128)S(1)}, u32[]{:S(2)}, u32[]{:S(2)}) collective-permute-start(f32[64,128]{1,0:T(8,128)} %get-tuple-element.19), channel_id=1, source_target_pairs={{0,32},{32,64},{64,96},{96,128},{128,160},{160,192},{192,224},{224... | collective-permute-start | bytes 98312 | tf_op jit(solution)/shard_map/ppermute | solution.py:388
  9.0 10.5 %collective-permute-start.2 = (f32[64,128]{1,0:T(8,128)}, f32[64,128]{1,0:T(8,128)S(1)}, u32[]{:S(2)}, u32[]{:S(2)}) collective-permute-start(f32[64,128]{1,0:T(8,128)} %get-tuple-element.19), channel_id=1, source_target_pairs={{0,224},{32,0},{64,32},{96,64},{128,96},{160,128},{192,160},{224,1... | collective-permute-start | bytes 98312 | tf_op jit(solution)/shard_map/ppermute | solution.py:388
  9.5 11.8 %collective-permute-start.1 = (f32[64,128]{1,0:T(8,128)}, f32[64,128]{1,0:T(8,128)S(1)}, u32[]{:S(2)}, u32[]{:S(2)}) collective-permute-start(f32[64,128]{1,0:T(8,128)} %get-tuple-element.19), channel_id=1, source_target_pairs={{0,1},{1,2},{2,3},{3,4},{4,5},{5,6},{6,7},{7,8},{8,9},{9,10},{10,1... | collective-permute-start | bytes 98312 | tf_op jit(solution)/shard_map/ppermute | solution.py:388
  14.8 6.9 %collective-permute-start = (f32[64,128]{1,0:T(8,128)}, f32[64,128]{1,0:T(8,128)S(1)}, u32[]{:S(2)}, u32[]{:S(2)}) collective-permute-start(f32[64,128]{1,0:T(8,128)} %get-tuple-element.19), channel_id=1, source_target_pairs={{0,31},{1,0},{2,1},{3,2},{4,3},{5,4},{6,5},{7,6},{8,7},{9,8},{10,9... | collective-permute-start | bytes 98312 | tf_op jit(solution)/shard_map/ppermute | solution.py:388
  19.5 2.2 %copy-start.6 = (f32[64,128]{1,0:T(8,128)}, f32[64,128]{1,0:T(8,128)S(1)}, u32[]{:S(2)}) copy-start(f32[64,128]{1,0:T(8,128)S(1)} %collective-permute-done.3.up_ref) | copy-start | bytes 98308
  19.5 2.2 %copy-start.7 = (f32[64,128]{1,0:T(8,128)}, f32[64,128]{1,0:T(8,128)S(1)}, u32[]{:S(2)}) copy-start(f32[64,128]{1,0:T(8,128)S(1)} %collective-permute-done.2.down_ref) | copy-start | bytes 98308
  21.4 0.6 copy-start.8
  21.7 0.6 copy-start.9
  21.7 0.8 copy-start.2
  32.8 12.7 %copy-start.3 = (f32[64,128]{1,0:T(8,128)S(1)}, f32[64,128]{1,0:T(8,128)}, u32[]{:S(2)}) copy-start(f32[64,128]{1,0:T(8,128)} %get-tuple-element.23) | copy-start | bytes 98308
  32.9 25.4 %all-to-all-start = ((f32[128,1,768]{2,1,0:T(1,128)}), f32[128,1,768]{2,1,0:T(1,128)S(1)}, u32[]{:S(2)}, u32[]{:S(2)}) async-start(f32[128,1,768]{2,1,0:T(1,128)} %bitcast.6), calls=%async_computation | async-start | bytes 786432 | tf_op jit(solution)/shard_map/all_to_all | solution.py:396
  45.6 13.9 %collective-permute-start.6 = (f32[64,128]{1,0:T(8,128)S(1)}, f32[64,128]{1,0:T(8,128)S(1)}, u32[]{:S(2)}, u32[]{:S(2)}) collective-permute-start(f32[64,128]{1,0:T(8,128)S(1)} %copy-done.3), channel_id=1, source_target_pairs={{0,1},{1,2},{2,3},{3,4},{4,5},{5,6},{6,7},{7,8},{8,9},{9,10},{10,1... | collective-permute-start | bytes 98312 | tf_op jit(solution)/shard_map/ppermute | solution.py:388
  50.1 9.4 %collective-permute-start.5 = (f32[64,128]{1,0:T(8,128)S(1)}, f32[64,128]{1,0:T(8,128)S(1)}, u32[]{:S(2)}, u32[]{:S(2)}) collective-permute-start(f32[64,128]{1,0:T(8,128)S(1)} %copy-done.3), channel_id=1, source_target_pairs={{0,31},{1,0},{2,1},{3,2},{4,3},{5,4},{6,5},{7,6},{8,7},{9,8},{10,9... | collective-permute-start | bytes 98312 | tf_op jit(solution)/shard_map/ppermute | solution.py:388
  59.5 1.0 %copy-start.4 = (f32[64,128]{1,0:T(8,128)}, f32[64,128]{1,0:T(8,128)S(1)}, u32[]{:S(2)}) copy-start(f32[64,128]{1,0:T(8,128)S(1)} %collective-permute-done.6.left_ref) | copy-start | bytes 98308
  59.5 1.0 %copy-start.5 = (f32[64,128]{1,0:T(8,128)}, f32[64,128]{1,0:T(8,128)S(1)}, u32[]{:S(2)}) copy-start(f32[64,128]{1,0:T(8,128)S(1)} %collective-permute-done.5.right_ref) | copy-start | bytes 98308
  60.5 25.5 %all-to-all-start.1 = ((f32[128,1,768]{2,1,0:T(1,128)}), f32[128,1,768]{2,1,0:T(1,128)S(1)}, u32[]{:S(2)}, u32[]{:S(2)}) async-start(f32[128,1,768]{2,1,0:T(1,128)} %broadcast_in_dim.9), calls=%async_computation.1 | async-start | bytes 786432 | tf_op jit(solution)/shard_map/all_to_all | solution.py:396
  71.3 7.8 %collective-permute-start.8 = (f32[64,128]{1,0:T(8,128)S(1)}, f32[64,128]{1,0:T(8,128)S(1)}, u32[]{:S(2)}, u32[]{:S(2)}) collective-permute-start(f32[64,128]{1,0:T(8,128)S(1)} %copy-done.3), channel_id=1, source_target_pairs={{0,32},{32,64},{64,96},{96,128},{128,160},{160,192},{192,224},{224... | collective-permute-start | bytes 98312 | tf_op jit(solution)/shard_map/ppermute | solution.py:388
  77.8 5.5 %collective-permute-start.7 = (f32[64,128]{1,0:T(8,128)S(1)}, f32[64,128]{1,0:T(8,128)S(1)}, u32[]{:S(2)}, u32[]{:S(2)}) collective-permute-start(f32[64,128]{1,0:T(8,128)S(1)} %copy-done.3), channel_id=1, source_target_pairs={{0,224},{32,0},{64,32},{96,64},{128,96},{160,128},{192,160},{224,1... | collective-permute-start | bytes 98312 | tf_op jit(solution)/shard_map/ppermute | solution.py:388
  79.1 4.2 %copy-start.10 = (f32[64,128]{1,0:T(8,128)}, f32[64,128]{1,0:T(8,128)S(1)}, u32[]{:S(2)}) copy-start(f32[64,128]{1,0:T(8,128)S(1)} %collective-permute-done.8.down_ref) | copy-start | bytes 98308
  83.2 0.6 copy-start.11
  86.0 6.9 %copy-start = (f32[128,1,768]{2,1,0:T(1,128)}, f32[128,1,768]{2,1,0:T(1,128)S(1)}, u32[]{:S(2)}) copy-start(f32[128,1,768]{2,1,0:T(1,128)S(1)} %all-to-all-done.1) | copy-start | bytes 1179652
  86.0 6.9 %collective-permute-start.9 = (f32[768,128]{1,0:T(8,128)S(1)}, f32[768,128]{1,0:T(8,128)S(1)}, u32[]{:S(2)}, u32[]{:S(2)}) collective-permute-start(f32[768,128]{1,0:T(8,128)S(1)} %bitcast.4), channel_id=1, source_target_pairs={{0,32},{32,0},{1,33},{33,1},{2,34},{34,2},{3,35},{35,3},{4,36},{36... | collective-permute-start | bytes 1179656 | tf_op jit(solution)/shard_map/ppermute | solution.py:392
  92.9 0.7 copy-start.1

commit v5 on v3

--- a/solution.py
+++ b/solution.py
@@ -201,10 +201,10 @@
 def edge_kernel(
     count_ref,
     features_ref,
+    up_ref,
+    down_ref,
     right_ref,
     left_ref,
-    up_ref,
-    down_ref,
     cotangent_ref,
     length_ref,
     neighbor_ref,
@@ -219,6 +219,10 @@
     selector_ref,
     gathered_ref,
     weight_ref,
+    grads_ref,
+    upstream_ref,
+    ratio_ref,
+    envelope_ref,
     *,
     factor,
 ):
@@ -240,14 +244,14 @@
     reach = jnp.where(jnp.logical_or(targets >= atoms, targets < count_ref[0]), live, 0.0)
     ratio = lengths * (1.0 / CUTOFF)
     envelope = 1.0 - ratio * ratio
-    envelope = math.sqrt(2.0 / CUTOFF) * envelope * envelope / lengths * reach
-    order = lax.broadcasted_iota(jnp.int32, (slots, 8, atoms), 1).astype(F32) + 1.0
-    basis = sin_turns(order * (0.5 * ratio)[:, None, :]) * envelope[:, None, :]
-    basis_ref[...] = basis.reshape(slots * 8, atoms)
+    envelope_ref[...] = math.sqrt(2.0 / CUTOFF) * envelope * envelope / lengths * reach
+    ratio_ref[...] = 0.5 * ratio
+    order = lax.broadcasted_iota(jnp.int32, (8, atoms), 0).astype(F32) + 1.0
 
     radial_high, radial_low = split(radial_ref[...])
     radial_wide = jnp.concatenate([radial_high, radial_high, radial_low], axis=0)
-    column = lax.broadcasted_iota(jnp.int32, (columns, wide), 0)
+    column = lax.broadcasted_iota(jnp.int32, (columns, 128), 0).astype(jnp.int16)
+    one, zero = jnp.ones((), BF16), jnp.zeros((), BF16)
 
     def side_by_side(pieces):
         return jnp.concatenate(pieces, axis=1)
@@ -261,11 +265,22 @@
         )
 
     def forward(turn, total):
-        picks = side_by_side([neighbor_ref[pl.ds(turn * group + i, 1), :] for i in range(group)])
-        selector = (column == picks).astype(F32).astype(BF16)
+        tiles = []
+        for i in range(group):
+            picks = neighbor_ref[pl.ds(turn * group + i, 1), :]
+            for lane in range(0, atoms, 128):
+                pick = jnp.broadcast_to(picks[:, lane : lane + 128], (16, 128)).astype(jnp.int16)
+                pick = jnp.concatenate([pick] * (columns // 16), axis=0)
+                tiles.append(jnp.where(column == pick, one, zero))
+        selector = side_by_side(tiles)
         selector_ref[turn] = selector
         found = dot(projected, selector)
         gathered = found[:channels] + found[channels:]
+        for i in range(group):
+            slot = turn * group + i
+            basis_ref[pl.ds(pl.multiple_of(slot * 8, 8), 8), :] = (
+                sin_turns(order * ratio_ref[pl.ds(slot, 1), :]) * envelope_ref[pl.ds(slot, 1), :]
+            )
         basis_high, basis_low = basis_of(turn)
         weight = dot(
             radial_wide, jnp.concatenate([basis_high, basis_low, basis_high], axis=0), ((0,), (0,))
@@ -281,22 +296,23 @@
     short_sum = lax.fori_loop(0, turns, forward, jnp.zeros((channels, atoms), F32))
     gate = jax.nn.sigmoid(short_sum)
     upstream = cotangent_ref[...] * gate * (1.0 + short_sum * (1.0 - gate)) * live
-    upstream = side_by_side([upstream] * group)
-
-    def backward(turn, running):
-        grads, radial = running
-        spread = jnp.concatenate(split(weight_ref[turn] * upstream), axis=0)
-        grads = grads + dot(spread, selector_ref[turn], ((1,), (1,)))
-        pulled = jnp.concatenate(split(gathered_ref[turn] * upstream), axis=0)
+
+    grads_ref[...] = jnp.zeros(grads_ref.shape, F32)
+    upstream_ref[...] = upstream
+
+    def backward(turn, radial):
+        pieces = []
+        pulls = []
+        for i in range(group):
+            lanes = pl.ds(i * atoms, atoms)
+            pieces.append(jnp.concatenate(split(weight_ref[turn, :, lanes] * upstream_ref[...]), axis=0))
+            pulls.append(jnp.concatenate(split(gathered_ref[turn, :, lanes] * upstream_ref[...]), axis=0))
+        grads_ref[...] += dot(selector_ref[turn], side_by_side(pieces), ((1,), (1,)))
         pair = jnp.concatenate(basis_of(turn), axis=0)
-        return grads, radial + dot(pulled, pair, ((1,), (1,)))
-
-    grads, radial = lax.fori_loop(
-        0,
-        turns,
-        backward,
-        (jnp.zeros((2 * channels, columns), F32), jnp.zeros((2 * channels, 16), F32)),
-    )
+        return radial + dot(pair, side_by_side(pulls), ((1,), (1,)))
+
+    radial = lax.fori_loop(0, turns, backward, jnp.zeros((16, 2 * channels), F32)).T
+    grads = grads_ref[...].T
     grads = grads[:channels] + grads[channels:]
     radial = radial[:channels] + radial[channels:]
     radial = radial[:, :8] + radial[:, 8:]
@@ -308,7 +324,7 @@
     )
 
 
-def return_kernel(right_ref, left_ref, up_ref, down_ref, own_ref, map_ref, short_ref, out_ref):
+def return_kernel(left_ref, right_ref, down_ref, up_ref, own_ref, map_ref, short_ref, out_ref):
     back = pick_lanes((up_ref, down_ref, right_ref, left_ref))
     selector = send_selector(map_ref[...], own_ref.shape[1])
     high, low = split(back)
@@ -318,11 +334,53 @@
     out_ref[...] = dot_full(short_ref[...], owned, ((0,), (0,)))
 
 
+def sum_kernel(pieces_ref, out_ref, *, width):
+    rows = pieces_ref.shape[0]
+    block = 4 * width
+    total = jnp.sum(pieces_ref[...].reshape(rows // block, block, 128), axis=0)
+    mine = total[:width]
+    for step in range(1, 4):
+        mine = mine + total[step * width : (step + 1) * width]
+    pattern = jnp.concatenate([mine] * 4, axis=0)
+    out_ref[...] = jnp.broadcast_to(pattern[None], (rows // block, block, 128)).reshape(rows, 128)
+
+
+def table_kernel(positions_ref, high_ref, low_ref):
+    chunk = chunk_waves(positions_ref[...])
+    for number in range(CHUNKS):
+        rows = pl.ds(number * 2 * HALF_ROWS, 2 * HALF_ROWS)
+        high_ref[rows, :], low_ref[rows, :] = split(chunk(number))
+
+
+def half_charge(half_ref, high_ref, low_ref, first):
+    waves = CHUNKS * HALF_ROWS
+    rows = pl.ds(pl.multiple_of(jnp.where(first, 0, waves), HALF_ROWS), waves)
+    block = half_ref[:waves, :]
+    turned_high, turned_low = split(block.T[:64])
+    block_high, block_low = split(block)
+    wave_high = high_ref[rows, :]
+    turned = jnp.concatenate([turned_high, turned_low], axis=0)
+    field = dot(turned, wave_high)
+    field = field[:64] + field[64:] + dot(turned_high, low_ref[rows, :])
+    grad = dot(turned, block_high)
+    grad = grad[:64] + grad[64:] + dot(turned_high, block_low)
+    return field, grad
+
+
+def mine_kernel(mine_ref, high_ref, low_ref, field_ref, grad_ref, small_ref):
+    small_ref[...] = mine_ref[CHUNKS * HALF_ROWS :, :]
+    first = lax.axis_index("core") == 0
+    field_ref[...], grad_ref[...] = half_charge(mine_ref, high_ref, low_ref, first)
+
+
 def charge_kernel(
     count_ref,
-    positions_ref,
+    other_ref,
+    high_ref,
+    low_ref,
+    field_ref,
+    sums_ref,
     mine_ref,
-    other_ref,
     partial_ref,
     charge_ref,
     grad_ref,
@@ -332,35 +390,15 @@
     *,
     factor,
 ):
-    first = lax.axis_index("core") == 0
+    first = lax.axis_index("core") != 0
     waves = CHUNKS * HALF_ROWS
-    small = mine_ref[waves:, :] + other_ref[waves:, :]
+    small = mine_ref[...] + other_ref[waves:, :]
     channels, atoms = partial_ref.shape
     short_ref[...] = small[:, :channels]
     radial_ref[...] = small.T[channels : channels + 8, :]
-
-    def unit(number):
-        rows = pl.ds(number % CHUNKS * HALF_ROWS, HALF_ROWS)
-        mine = first if number < CHUNKS else jnp.logical_not(first)
-        return jnp.where(mine, mine_ref[rows, :], other_ref[rows, :])
-
-    chunk = chunk_waves(positions_ref[...])
-    field = jnp.zeros((2 * channels, atoms), F32)
-    grad = jnp.zeros((2 * channels, 128), F32)
-    for number in range(CHUNKS):
-        block = jnp.concatenate([unit(2 * number), unit(2 * number + 1)], axis=0)
-        turned = block.T[:channels]
-        turned_high, turned_low = split(turned)
-        turned = jnp.concatenate([turned_high, turned_low], axis=0)
-        block_high, block_low = split(block)
-        wave_high, wave_low = split(chunk(number))
-        field = field + dot(turned, wave_high)
-        grad = grad + dot(turned, block_high)
-        extra = dot(turned_high, jnp.concatenate([wave_low, block_low], axis=1))
-        field = field + jnp.concatenate([extra[:, :atoms], jnp.zeros((channels, atoms), F32)], axis=0)
-        grad = grad + jnp.concatenate([extra[:, atoms:], jnp.zeros((channels, 128), F32)], axis=0)
-    field = (field[:channels] + field[channels:]) * live_row(count_ref, atoms)
-    grad = grad[:channels] + grad[channels:]
+    field, grad = half_charge(other_ref, high_ref, low_ref, first)
+    field = (field + field_ref[...]) * live_row(count_ref, atoms)
+    grad = grad + sums_ref[...]
     grad_ref[...] = grad[:, channels : 2 * channels] * factor
     out_ref[...] = partial_ref[...] + dot_full(charge_ref[...], field, ((0,), (0,)))
 
@@ -383,22 +421,25 @@
     return jax.ShapeDtypeStruct(dims, F32)
 
 
+def near(*dims):
+    return pltpu.VMEM(dims, F32)
+
+
 def shifted(value, axis, step):
     size = lax.axis_size(axis)
     return lax.ppermute(value, axis, [(i, (i + step) % size) for i in range(size)])
 
 
+def close(value):
+    return pltpu.with_memory_space_constraint(value, pltpu.VMEM)
+
+
 def swapped(value):
     return lax.ppermute(value, "core", [(0, 1), (1, 0)])
 
 
 def exchange(value, axes):
     return lax.all_to_all(value, axes, 0, 0, tiled=True)
-
-
-def everywhere(value, axes):
-    size = lax.axis_size(axes)
-    return exchange(jnp.broadcast_to(value[None], (size,) + value.shape), axes)
 
 
 def on_device(
@@ -424,20 +465,22 @@
 
     keep, give, outgoing = pl.pallas_call(
         wave_kernel,
-        out_shape=(shape(half, 128), shape(half, 128), shape(channels, 128)),
+        out_shape=(near(half, 128), near(half, 128), near(channels, 128)),
         in_specs=scalar_first(5),
         out_specs=tuple(vmem(3)),
         cost_estimate=work(4.0),
     )(atom_count, positions, cotangent, features, jnp.asarray(weight_table(factor)), send_map)
+    up = shifted(outgoing, SLAB, 1)
+    down = shifted(outgoing, SLAB, -1)
     right = shifted(outgoing, "brick", 1)
     left = shifted(outgoing, "brick", -1)
-    up = shifted(outgoing, SLAB, 1)
-    down = shifted(outgoing, SLAB, -1)
     taken = swapped(give)
 
+    up, down, right, left = (close(x) for x in (up, down, right, left))
+    keep, taken = close(keep), close(taken)
     own, ghost, payload = pl.pallas_call(
         functools.partial(edge_kernel, factor=factor),
-        out_shape=(shape(channels, atoms), shape(channels, 128), shape(rows, 128)),
+        out_shape=(near(channels, atoms), near(channels, 128), near(rows, 128)),
         in_specs=scalar_first(12),
         out_specs=tuple(vmem(3)),
         scratch_shapes=[
@@ -445,15 +488,19 @@
             pltpu.VMEM((slots // 4, atoms + 128, 4 * atoms), BF16),
             pltpu.VMEM((slots // 4, channels, 4 * atoms), F32),
             pltpu.VMEM((slots // 4, channels, 4 * atoms), F32),
+            pltpu.VMEM((atoms + 128, 2 * channels), F32),
+            pltpu.VMEM((channels, atoms), F32),
+            pltpu.VMEM((slots, atoms), F32),
+            pltpu.VMEM((slots, atoms), F32),
         ],
         cost_estimate=work(10.0),
     )(
         atom_count,
         features,
+        up,
+        down,
         right,
         left,
-        up,
-        down,
         cotangent,
         edge_length,
         neighbors,
@@ -463,22 +510,46 @@
         taken,
     )
     pieces = exchange(payload.reshape(chips, 1, width), CHIPS)
-    back = (
-        shifted(ghost, "brick", -1),
-        shifted(ghost, "brick", 1),
-        shifted(ghost, SLAB, -1),
-        shifted(ghost, SLAB, 1),
+    back_right = shifted(ghost, "brick", 1)
+    back_left = shifted(ghost, "brick", -1)
+    back_up = shifted(ghost, SLAB, 1)
+    back_down = shifted(ghost, SLAB, -1)
+    pieces, back_right, back_left = lax.optimization_barrier((pieces, back_right, back_left))
+    summed = pl.pallas_call(
+        functools.partial(sum_kernel, width=rows // chips),
+        out_shape=near(rows, 128),
+        in_specs=vmem(1),
+        out_specs=vmem(1)[0],
+        cost_estimate=work(0.5),
+    )(close(pieces.reshape(rows, 128)))
+    mine = exchange(summed.reshape(chips, 1, width), CHIPS).reshape(rows, 128)
+    back_right, back_left, back_up, back_down = (
+        close(x) for x in (back_right, back_left, back_up, back_down)
     )
     partial = pl.pallas_call(
         return_kernel,
-        out_shape=shape(channels, atoms),
+        out_shape=near(channels, atoms),
         in_specs=vmem(7),
         out_specs=vmem(1)[0],
         cost_estimate=work(2.0),
-    )(*back, own, send_map, short_weight)
-    summed, partial = lax.optimization_barrier((jnp.sum(pieces, axis=0), partial))
-    mine = everywhere(summed, CHIPS).reshape(rows, 128)
-    other = swapped(mine)
+    )(back_right, back_left, back_up, back_down, close(own), send_map, short_weight)
+    high, low = pl.pallas_call(
+        table_kernel,
+        out_shape=(pltpu.VMEM((2 * half, atoms), BF16), pltpu.VMEM((2 * half, atoms), BF16)),
+        in_specs=vmem(1),
+        out_specs=tuple(vmem(2)),
+        cost_estimate=work(2.0),
+    )(positions)
+    mine, partial, high, low = lax.optimization_barrier((mine, partial, high, low))
+    high, low = close(high), close(low)
+    other = close(swapped(mine))
+    field, sums, small = pl.pallas_call(
+        mine_kernel,
+        out_shape=(near(channels, atoms), near(channels, 128), near(channels, 128)),
+        in_specs=vmem(3),
+        out_specs=tuple(vmem(3)),
+        cost_estimate=work(2.0),
+    )(close(mine), high, low)
     charge_grad, feature_grad, short_grad, radial_grad = pl.pallas_call(
         functools.partial(charge_kernel, factor=factor),
         out_shape=(
@@ -487,10 +558,20 @@
             shape(channels, channels),
             shape(radial_weight.shape[1], channels),
         ),
-        in_specs=scalar_first(5),
+        in_specs=scalar_first(8),
         out_specs=tuple(vmem(4)),
         cost_estimate=work(3.0),
-    )(atom_count, positions, mine, other, partial, charge_weight)
+    )(
+        atom_count,
+        other,
+        high,
+        low,
+        close(field),
+        close(sums),
+        close(small),
+        close(partial),
+        charge_weight,
+    )
     return feature_grad, short_grad, charge_grad, radial_grad.T
 
 

time: 103 us -> 91.5 us (0.89)
  starting transfers between devices: 38.8 us -> 60.6 us
  blocking collectives: 21.6 us -> 0 us
  waiting for transfers between devices: 18.3 us -> 11.3 us
  local copies, waits for them, and re-layouts: 2.3 us -> 0 us
  Pallas kernels: 19.9 us -> 17.9 us
    all_to_all x1 -> x0, blocking collectives: 21.6 us -> none  [exchange(): return lax.all_to_all(value, axes, 0, 0, tiled=True)]
    all_to_all x1 -> x2, starting transfers between devices: 7.08 us -> 23.4 us  [exchange(): return lax.all_to_all(value, axes, 0, 0, tiled=True)]
    ppermute x8, waiting for transfers between devices: 16.9 us -> 10.3 us  [shifted(): lax.ppermute(value, axis, [(i, (i + step) % size) for i in range(size)])]
    ppermute x8, starting transfers between devices: 23 us -> 26.9 us  [shifted(): lax.ppermute(value, axis, [(i, (i + step) % size) for i in range(size)])]
    unnamed x24 -> x0, local copies, waits for them, and re-layouts: 2.09 us -> none
    pallas_call x1, Pallas kernels: 10.4 us -> 8.48 us  [on_device(): pl.pallas_call(functools.partial(edge_kernel, factor=factor), out_shape=(...]
    ppermute x2, starting transfers between devices: 8.72 us -> 10.3 us  [swapped(): return lax.ppermute(value, 'core', [(0, 1), (1, 0)])]
    pallas_call x2 -> x5, Pallas kernels: 6.65 us -> 7.45 us  [the longest x1 3.66 us: on_device(): pl.pallas_call(wave_kernel, out_shape=(near(half, 128), near(half, 128),...]
  transfers between devices with their start and end apart: 11 -> 12, of which waited for: 4 -> 6; matrix products, arithmetic and copies ran while one was open for 0% -> 0% of each run, Pallas kernels for 2% -> 3%
where the time goes in v5:
time: 91.5 us; the launch traced here: 91.1 us
  starting transfers between devices  60.6 us (66%)
  Pallas kernels  17.9 us (20%)
  waiting for transfers between devices  11.3 us (12%)
  between operations  1.34 us (1%)
    ppermute x8, starting transfers between devices, shifted(): lax.ppermute(value, axis, [(i, (i + step) % size) for i in range(size)])  26.9 us
    all_to_all x2, starting transfers between devices, exchange(): return lax.all_to_all(value, axes, 0, 0, tiled=True)  23.4 us
    ppermute x8, waiting for transfers between devices, shifted(): lax.ppermute(value, axis, [(i, (i + step) % size) for i in range(size)])  10.3 us
    ppermute x2, starting transfers between devices, swapped(): return lax.ppermute(value, 'core', [(0, 1), (1, 0)])  10.3 us
    pallas_call x1, Pallas kernels, on_device(): pl.pallas_call(functools.partial(edge_kernel, factor=factor), out_shape=(...  8.48 us
    pallas_call x1, Pallas kernels, on_device(): pl.pallas_call(wave_kernel, out_shape=(near(half, 128), near(half, 128),...  3.66 us
    pallas_call x1, Pallas kernels, on_device(): pl.pallas_call(functools.partial(charge_kernel, factor=factor), out_shape...  2 us
  transfers between devices with their start and end apart: 12, of which 6 were waited for; matrix products, arithmetic and copies ran while one was open for 0% of the time, Pallas kernels for 3%

profile of v5, /device:TPU:1, one launch (start us, length us, event | category | flops | bytes accessed | tf_op | source)
XLA Modules:
  0.0 91.1 jit_solution(6164274792832015296)
XLA Ops:
  1.3 3.7 %shard_map.138 = (f32[704,128]{1,0:T(8,128)S(1)}, f32[704,128]{1,0:T(8,128)S(1)}, f32[64,128]{1,0:T(8,128)S(1)}) custom-call(s32[1]{0:T(128)S(6)} %copy.17.count_ref, f32[3,256]{1,0:T(4,128)} %positions_ref.3, f32[64,256]{1,0:T(8,128)} %cotangent_ref.3, f32[64,256]{1,0:T(8,128)} %features_ref.3, f32[704,128]{1,0:T(8,128)} %constant.2.clone.table_ref, ...), custom_call_target="tpu_custom_call" | custom-call | flops 4000000000 | bytes 12000000 | tf_op jit(solution)/shard_map/pallas_call | solution.py:466
  4.9 3.3 %collective-permute-start.4 = (f32[704,128]{1,0:T(8,128)S(1)}, f32[704,128]{1,0:T(8,128)S(1)}, u32[]{:S(2)}, u32[]{:S(2)}) collective-permute-start(f32[704,128]{1,0:T(8,128)S(1)} %get-tuple-element.28), channel_id=1, source_target_pairs={{0,32},{32,0},{1,33},{33,1},{2,34},{34,2},{3,35},{35,3},{4,36},{36... | collective-permute-start | bytes 1081352 | tf_op jit(solution)/shard_map/ppermute | solution.py:438
  8.3 0.0 collective-permute-start
  8.3 0.5 collective-permute-start.1
  8.8 5.4 %collective-permute-start.2 = (f32[64,128]{1,0:T(8,128)S(1)}, f32[64,128]{1,0:T(8,128)S(1)}, u32[]{:S(2)}, u32[]{:S(2)}) collective-permute-start(f32[64,128]{1,0:T(8,128)S(1)} %get-tuple-element.26), channel_id=1, source_target_pairs={{0,1},{1,2},{2,3},{3,4},{4,5},{5,6},{6,7},{7,8},{8,9},{9,10},{10,1... | collective-permute-start | bytes 98312 | tf_op jit(solution)/shard_map/ppermute | solution.py:430
  14.2 4.6 %collective-permute-start.3 = (f32[64,128]{1,0:T(8,128)S(1)}, f32[64,128]{1,0:T(8,128)S(1)}, u32[]{:S(2)}, u32[]{:S(2)}) collective-permute-start(f32[64,128]{1,0:T(8,128)S(1)} %get-tuple-element.26), channel_id=1, source_target_pairs={{0,31},{1,0},{2,1},{3,2},{4,3},{5,4},{6,5},{7,6},{8,7},{9,8},{10,9... | collective-permute-start | bytes 98312 | tf_op jit(solution)/shard_map/ppermute | solution.py:430
  18.8 0.0 collective-permute-done.up_ref
  18.8 0.0 collective-permute-done.1.down_ref
  18.8 1.7 %collective-permute-done.2.right_ref = f32[64,128]{1,0:T(8,128)S(1)} collective-permute-done((f32[64,128]{1,0:T(8,128)S(1)}, f32[64,128]{1,0:T(8,128)S(1)}, u32[]{:S(2)}, u32[]{:S(2)}) %collective-permute-start.2) | collective-permute-done | bytes 32800 | tf_op jit(solution)/shard_map/ppermute | solution.py:430
  20.5 0.4 collective-permute-done.3.left_ref
  20.8 0.0 collective-permute-done.4.taken_ref
  20.8 8.5 %shard_map.139 = (f32[64,256]{1,0:T(8,128)S(1)}, f32[64,128]{1,0:T(8,128)S(1)}, f32[768,128]{1,0:T(8,128)}) custom-call(s32[1]{0:T(128)S(6)} %copy.17.count_ref, f32[64,256]{1,0:T(8,128)} %features_ref.3, f32[64,128]{1,0:T(8,128)S(1)} %collective-permute-done.up_ref, f32[64,128]{1,0:T(8,128)S(1)} %collective-permute-done.1.down_ref, ...), custom_call_target="tpu_custom_call" | custom-call | flops 10000000000 | bytes 30000000 | tf_op jit(solution)/shard_map/pallas_call | solution.py:481
  29.3 12.6 %all-to-all-start = ((f32[128,1,768]{2,1,0:T(1,128)}), f32[128,1,768]{2,1,0:T(1,128)S(1)}, u32[]{:S(2)}, u32[]{:S(2)}) async-start(f32[128,1,768]{2,1,0:T(1,128)} %bitcast.1), calls=%async_computation | async-start | bytes 786432 | tf_op jit(solution)/shard_map/all_to_all | solution.py:442
  41.9 4.6 %collective-permute-start.5 = (f32[64,128]{1,0:T(8,128)S(1)}, f32[64,128]{1,0:T(8,128)S(1)}, u32[]{:S(2)}, u32[]{:S(2)}) collective-permute-start(f32[64,128]{1,0:T(8,128)S(1)} %get-tuple-element.30), channel_id=1, source_target_pairs={{0,1},{1,2},{2,3},{3,4},{4,5},{5,6},{6,7},{7,8},{8,9},{9,10},{10,1... | collective-permute-start | bytes 98312 | tf_op jit(solution)/shard_map/ppermute | solution.py:430
  46.5 5.1 %collective-permute-start.6 = (f32[64,128]{1,0:T(8,128)S(1)}, f32[64,128]{1,0:T(8,128)S(1)}, u32[]{:S(2)}, u32[]{:S(2)}) collective-permute-start(f32[64,128]{1,0:T(8,128)S(1)} %get-tuple-element.30), channel_id=1, source_target_pairs={{0,31},{1,0},{2,1},{3,2},{4,3},{5,4},{6,5},{7,6},{8,7},{9,8},{10,9... | collective-permute-start | bytes 98312 | tf_op jit(solution)/shard_map/ppermute | solution.py:430
  51.6 4.2 %collective-permute-done.5.left_ref = f32[64,128]{1,0:T(8,128)S(1)} collective-permute-done((f32[64,128]{1,0:T(8,128)S(1)}, f32[64,128]{1,0:T(8,128)S(1)}, u32[]{:S(2)}, u32[]{:S(2)}) %collective-permute-start.5) | collective-permute-done | bytes 32800 | tf_op jit(solution)/shard_map/ppermute | solution.py:430
  55.8 0.0 collective-permute-done.6.right_ref
  55.8 0.0 all-to-all-done
  55.8 0.8 shard_map.140
  56.6 10.8 %all-to-all-start.1 = ((f32[128,1,768]{2,1,0:T(1,128)}), f32[128,1,768]{2,1,0:T(1,128)S(1)}, u32[]{:S(2)}, u32[]{:S(2)}) async-start(f32[128,1,768]{2,1,0:T(1,128)} %bitcast.3), calls=%async_computation.1 | async-start | bytes 786432 | tf_op jit(solution)/shard_map/all_to_all | solution.py:442
  67.5 6.7 %collective-permute-start.7 = (f32[64,128]{1,0:T(8,128)S(1)}, f32[64,128]{1,0:T(8,128)S(1)}, u32[]{:S(2)}, u32[]{:S(2)}) collective-permute-start(f32[64,128]{1,0:T(8,128)S(1)} %get-tuple-element.30), channel_id=1, source_target_pairs={{0,32},{32,64},{64,96},{96,128},{128,160},{160,192},{192,224},{224... | collective-permute-start | bytes 98312 | tf_op jit(solution)/shard_map/ppermute | solution.py:430
  74.2 0.0 collective-permute-start.8
  74.2 1.2 %shard_map.142 = (bf16[1408,256]{1,0:T(8,128)(2,1)S(1)}, bf16[1408,256]{1,0:T(8,128)(2,1)S(1)}) custom-call(f32[3,256]{1,0:T(4,128)} %positions_ref.3), custom_call_target="tpu_custom_call" | custom-call | flops 2000000000 | bytes 6000000 | tf_op jit(solution)/shard_map/pallas_call | solution.py:536
  75.4 0.1 collective-permute-done.7.down_ref
  75.4 4.0 %collective-permute-done.8.up_ref = f32[64,128]{1,0:T(8,128)S(1)} collective-permute-done((f32[64,128]{1,0:T(8,128)S(1)}, f32[64,128]{1,0:T(8,128)S(1)}, u32[]{:S(2)}, u32[]{:S(2)}) %collective-permute-start.8) | collective-permute-done | bytes 32800 | tf_op jit(solution)/shard_map/ppermute | solution.py:430
  79.4 1.3 %shard_map.141.partial_ref = f32[64,256]{1,0:T(8,128)S(1)} custom-call(f32[64,128]{1,0:T(8,128)S(1)} %collective-permute-done.5.left_ref, f32[64,128]{1,0:T(8,128)S(1)} %collective-permute-done.6.right_ref, f32[64,128]{1,0:T(8,128)S(1)} %collective-permute-done.7.down_ref, f32[64,128]{1,0:T(8,128)S(1)} %collective-permute-done.8.up_ref, ...), custom_call_target="tpu_custom_call" | custom-call | flops 2000000000 | bytes 6000000 | tf_op jit(solution)/shard_map/pallas_call | solution.py:529
  80.8 0.0 all-to-all-done.1
  80.8 6.9 %collective-permute-start.9 = (f32[768,128]{1,0:T(8,128)S(1)}, f32[768,128]{1,0:T(8,128)S(1)}, u32[]{:S(2)}, u32[]{:S(2)}) collective-permute-start(f32[768,128]{1,0:T(8,128)S(1)} %bitcast.6), channel_id=1, source_target_pairs={{0,32},{32,0},{1,33},{33,1},{2,34},{34,2},{3,35},{35,3},{4,36},{36... | collective-permute-start | bytes 1179656 | tf_op jit(solution)/shard_map/ppermute | solution.py:438
  87.7 0.4 shard_map.143
  88.1 0.9 %collective-permute-done.9.other_ref = f32[768,128]{1,0:T(8,128)S(1)} collective-permute-done((f32[768,128]{1,0:T(8,128)S(1)}, f32[768,128]{1,0:T(8,128)S(1)}, u32[]{:S(2)}, u32[]{:S(2)}) %collective-permute-start.9) | collective-permute-done | bytes 393248 | tf_op jit(solution)/shard_map/ppermute | solution.py:438
  89.1 2.0 %shard_map.144 = (f32[64,64]{1,0:T(8,128)}, f32[64,256]{1,0:T(8,128)}, f32[64,64]{1,0:T(8,128)}, f32[8,64]{1,0:T(8,128)}) custom-call(s32[1]{0:T(128)S(6)} %copy.17.count_ref, f32[768,128]{1,0:T(8,128)S(1)} %collective-permute-done.9.other_ref, bf16[1408,256]{1,0:T(8,128)(2,1)S(1)} %get-tuple-element.38.high_ref, ...), custom_call_target="tpu_custom_call" | custom-call | flops 3000000000 | bytes 9000000 | tf_op jit(solution)/shard_map/pallas_call | solution.py:553
Async XLA Ops:
  4.9 15.9 %collective-permute-start.4 = (f32[704,128]{1,0:T(8,128)S(1)}, f32[704,128]{1,0:T(8,128)S(1)}, u32[]{:S(2)}, u32[]{:S(2)}) collective-permute-start(f32[704,128]{1,0:T(8,128)S(1)} %get-tuple-element.28), channel_id=1, source_target_pairs={{0,32},{32,0},{1,33},{33,1},{2,34},{34,2},{3,35},{35,3},{4,36},{36... | collective-permute-start | bytes 1081352 | tf_op jit(solution)/shard_map/ppermute | solution.py:438
  8.3 10.5 %collective-permute-start = (f32[64,128]{1,0:T(8,128)S(1)}, f32[64,128]{1,0:T(8,128)S(1)}, u32[]{:S(2)}, u32[]{:S(2)}) collective-permute-start(f32[64,128]{1,0:T(8,128)S(1)} %get-tuple-element.26), channel_id=1, source_target_pairs={{0,32},{32,64},{64,96},{96,128},{128,160},{160,192},{192,224},{224... | collective-permute-start | bytes 98312 | tf_op jit(solution)/shard_map/ppermute | solution.py:430
  8.3 10.5 %collective-permute-start.1 = (f32[64,128]{1,0:T(8,128)S(1)}, f32[64,128]{1,0:T(8,128)S(1)}, u32[]{:S(2)}, u32[]{:S(2)}) collective-permute-start(f32[64,128]{1,0:T(8,128)S(1)} %get-tuple-element.26), channel_id=1, source_target_pairs={{0,224},{32,0},{64,32},{96,64},{128,96},{160,128},{192,160},{224,1... | collective-permute-start | bytes 98312 | tf_op jit(solution)/shard_map/ppermute | solution.py:430
  8.8 11.7 %collective-permute-start.2 = (f32[64,128]{1,0:T(8,128)S(1)}, f32[64,128]{1,0:T(8,128)S(1)}, u32[]{:S(2)}, u32[]{:S(2)}) collective-permute-start(f32[64,128]{1,0:T(8,128)S(1)} %get-tuple-element.26), channel_id=1, source_target_pairs={{0,1},{1,2},{2,3},{3,4},{4,5},{5,6},{6,7},{7,8},{8,9},{9,10},{10,1... | collective-permute-start | bytes 98312 | tf_op jit(solution)/shard_map/ppermute | solution.py:430
  14.2 6.7 %collective-permute-start.3 = (f32[64,128]{1,0:T(8,128)S(1)}, f32[64,128]{1,0:T(8,128)S(1)}, u32[]{:S(2)}, u32[]{:S(2)}) collective-permute-start(f32[64,128]{1,0:T(8,128)S(1)} %get-tuple-element.26), channel_id=1, source_target_pairs={{0,31},{1,0},{2,1},{3,2},{4,3},{5,4},{6,5},{7,6},{8,7},{9,8},{10,9... | collective-permute-start | bytes 98312 | tf_op jit(solution)/shard_map/ppermute | solution.py:430
  29.3 26.5 %all-to-all-start = ((f32[128,1,768]{2,1,0:T(1,128)}), f32[128,1,768]{2,1,0:T(1,128)S(1)}, u32[]{:S(2)}, u32[]{:S(2)}) async-start(f32[128,1,768]{2,1,0:T(1,128)} %bitcast.1), calls=%async_computation | async-start | bytes 786432 | tf_op jit(solution)/shard_map/all_to_all | solution.py:442
  41.9 13.9 %collective-permute-start.5 = (f32[64,128]{1,0:T(8,128)S(1)}, f32[64,128]{1,0:T(8,128)S(1)}, u32[]{:S(2)}, u32[]{:S(2)}) collective-permute-start(f32[64,128]{1,0:T(8,128)S(1)} %get-tuple-element.30), channel_id=1, source_target_pairs={{0,1},{1,2},{2,3},{3,4},{4,5},{5,6},{6,7},{7,8},{8,9},{9,10},{10,1... | collective-permute-start | bytes 98312 | tf_op jit(solution)/shard_map/ppermute | solution.py:430
  46.5 9.4 %collective-permute-start.6 = (f32[64,128]{1,0:T(8,128)S(1)}, f32[64,128]{1,0:T(8,128)S(1)}, u32[]{:S(2)}, u32[]{:S(2)}) collective-permute-start(f32[64,128]{1,0:T(8,128)S(1)} %get-tuple-element.30), channel_id=1, source_target_pairs={{0,31},{1,0},{2,1},{3,2},{4,3},{5,4},{6,5},{7,6},{8,7},{9,8},{10,9... | collective-permute-start | bytes 98312 | tf_op jit(solution)/shard_map/ppermute | solution.py:430
  56.6 24.1 %all-to-all-start.1 = ((f32[128,1,768]{2,1,0:T(1,128)}), f32[128,1,768]{2,1,0:T(1,128)S(1)}, u32[]{:S(2)}, u32[]{:S(2)}) async-start(f32[128,1,768]{2,1,0:T(1,128)} %bitcast.3), calls=%async_computation.1 | async-start | bytes 786432 | tf_op jit(solution)/shard_map/all_to_all | solution.py:442
  67.5 8.0 %collective-permute-start.7 = (f32[64,128]{1,0:T(8,128)S(1)}, f32[64,128]{1,0:T(8,128)S(1)}, u32[]{:S(2)}, u32[]{:S(2)}) collective-permute-start(f32[64,128]{1,0:T(8,128)S(1)} %get-tuple-element.30), channel_id=1, source_target_pairs={{0,32},{32,64},{64,96},{96,128},{128,160},{160,192},{192,224},{224... | collective-permute-start | bytes 98312 | tf_op jit(solution)/shard_map/ppermute | solution.py:430
  74.2 5.3 %collective-permute-start.8 = (f32[64,128]{1,0:T(8,128)S(1)}, f32[64,128]{1,0:T(8,128)S(1)}, u32[]{:S(2)}, u32[]{:S(2)}) collective-permute-start(f32[64,128]{1,0:T(8,128)S(1)} %get-tuple-element.30), channel_id=1, source_target_pairs={{0,224},{32,0},{64,32},{96,64},{128,96},{160,128},{192,160},{224,1... | collective-permute-start | bytes 98312 | tf_op jit(solution)/shard_map/ppermute | solution.py:430
  80.8 8.3 %collective-permute-start.9 = (f32[768,128]{1,0:T(8,128)S(1)}, f32[768,128]{1,0:T(8,128)S(1)}, u32[]{:S(2)}, u32[]{:S(2)}) collective-permute-start(f32[768,128]{1,0:T(8,128)S(1)} %bitcast.6), channel_id=1, source_target_pairs={{0,32},{32,0},{1,33},{33,1},{2,34},{34,2},{3,35},{35,3},{4,36},{36... | collective-permute-start | bytes 1179656 | tf_op jit(solution)/shard_map/ppermute | solution.py:438

commit v6 on v5

--- a/solution.py
+++ b/solution.py
@@ -164,6 +164,7 @@
     keep_ref,
     give_ref,
     outgoing_ref,
+    parts_ref,
 ):
     features = features_ref[...]
     selector = send_selector(map_ref[...], features.shape[1])
@@ -175,27 +176,19 @@
     both = jnp.concatenate([cotangent_ref[...] * live, features * live], axis=0)
     high, low = split(both)
     stacked = jnp.concatenate([high, low], axis=0)
-    first = lax.axis_index("core") == 0
-
-    def store(unit, value):
-        rows = pl.ds(unit % CHUNKS * HALF_ROWS, HALF_ROWS)
-        mine = first if unit < CHUNKS else jnp.logical_not(first)
-
-        @pl.when(mine)
-        def _():
-            keep_ref[rows, :] = value
-
-        @pl.when(jnp.logical_not(mine))
-        def _():
-            give_ref[rows, :] = value
-
     for number in range(CHUNKS):
         wave_high, wave_low = split(chunk(number))
         part = dot(wave_high, stacked, ((1,), (1,)))
         part = part[:, :128] + part[:, 128:] + dot(wave_low, high, ((1,), (1,)))
         weight = table_ref[number * HALF_ROWS : (number + 1) * HALF_ROWS, :]
-        store(2 * number, part[:HALF_ROWS] * weight)
-        store(2 * number + 1, part[HALF_ROWS:] * weight)
+        base = number * 2 * HALF_ROWS
+        parts_ref[base : base + HALF_ROWS, :] = part[:HALF_ROWS] * weight
+        parts_ref[base + HALF_ROWS : base + 2 * HALF_ROWS, :] = part[HALF_ROWS:] * weight
+    half = keep_ref.shape[0]
+    first = lax.axis_index("core") == 0
+    lower, upper = parts_ref[:half, :], parts_ref[half:, :]
+    keep_ref[...] = jnp.where(first, lower, upper)
+    give_ref[...] = jnp.where(first, upper, lower)
 
 
 def edge_kernel(
@@ -293,7 +286,9 @@
         return total
 
     turns = slots // group
-    short_sum = lax.fori_loop(0, turns, forward, jnp.zeros((channels, atoms), F32))
+    short_sum = lax.fori_loop(
+        0, turns, forward, jnp.zeros((channels, atoms), F32), unroll=8
+    )
     gate = jax.nn.sigmoid(short_sum)
     upstream = cotangent_ref[...] * gate * (1.0 + short_sum * (1.0 - gate)) * live
 
@@ -311,7 +306,9 @@
         pair = jnp.concatenate(basis_of(turn), axis=0)
         return radial + dot(pair, side_by_side(pulls), ((1,), (1,)))
 
-    radial = lax.fori_loop(0, turns, backward, jnp.zeros((16, 2 * channels), F32)).T
+    radial = lax.fori_loop(
+        0, turns, backward, jnp.zeros((16, 2 * channels), F32), unroll=8
+    ).T
     grads = grads_ref[...].T
     grads = grads[:channels] + grads[channels:]
     radial = radial[:channels] + radial[channels:]
@@ -468,6 +465,7 @@
         out_shape=(near(half, 128), near(half, 128), near(channels, 128)),
         in_specs=scalar_first(5),
         out_specs=tuple(vmem(3)),
+        scratch_shapes=[pltpu.VMEM((2 * half, 128), F32)],
         cost_estimate=work(4.0),
     )(atom_count, positions, cotangent, features, jnp.asarray(weight_table(factor)), send_map)
     up = shifted(outgoing, SLAB, 1)

time: 91.5 us -> 88.2 us (0.964)
  Pallas kernels: 17.9 us -> 14.4 us
    pallas_call x1, Pallas kernels: 8.48 us -> 6.56 us  [on_device(): pl.pallas_call(functools.partial(edge_kernel, factor=factor), out_shape=(...]
    pallas_call x1, Pallas kernels: 3.66 us -> 2.03 us  [on_device(): pl.pallas_call(wave_kernel, out_shape=(near(half, 128), near(half, 128),...]
  transfers between devices with their start and end apart: 12 -> 12, of which waited for: 6 -> 5; matrix products, arithmetic and copies ran while one was open for 0% -> 0% of each run, Pallas kernels for 3% -> 3%
where the time goes in v6:
time: 88.2 us; the launch traced here: 87.7 us
  starting transfers between devices  60.6 us (69%)
  Pallas kernels  14.4 us (16%)
  waiting for transfers between devices  11.4 us (13%)
  between operations  1.34 us (2%)
    ppermute x8, starting transfers between devices, shifted(): lax.ppermute(value, axis, [(i, (i + step) % size) for i in range(size)])  26.7 us
    all_to_all x2, starting transfers between devices, exchange(): return lax.all_to_all(value, axes, 0, 0, tiled=True)  23.6 us
    ppermute x8, waiting for transfers between devices, shifted(): lax.ppermute(value, axis, [(i, (i + step) % size) for i in range(size)])  10.5 us
    ppermute x2, starting transfers between devices, swapped(): return lax.ppermute(value, 'core', [(0, 1), (1, 0)])  10.3 us
    pallas_call x1, Pallas kernels, on_device(): pl.pallas_call(functools.partial(edge_kernel, factor=factor), out_shape=(...  6.56 us
    pallas_call x1, Pallas kernels, on_device(): pl.pallas_call(wave_kernel, out_shape=(near(half, 128), near(half, 128),...  2.03 us
    pallas_call x1, Pallas kernels, on_device(): pl.pallas_call(functools.partial(charge_kernel, factor=factor), out_shape...  2 us
  transfers between devices with their start and end apart: 12, of which 5 were waited for; matrix products, arithmetic and copies ran while one was open for 0% of the time, Pallas kernels for 3%

profile of v6, /device:TPU:1, one launch (start us, length us, event | category | flops | bytes accessed | tf_op | source)
XLA Modules:
  0.0 87.7 jit_solution(16764394769966348837)
XLA Ops:
  1.3 2.0 %shard_map.138 = (f32[704,128]{1,0:T(8,128)S(1)}, f32[704,128]{1,0:T(8,128)S(1)}, f32[64,128]{1,0:T(8,128)S(1)}) custom-call(s32[1]{0:T(128)S(6)} %copy.17.count_ref, f32[3,256]{1,0:T(4,128)} %positions_ref.3, f32[64,256]{1,0:T(8,128)} %cotangent_ref.3, f32[64,256]{1,0:T(8,128)} %features_ref.3, f32[704,128]{1,0:T(8,128)} %constant.2.clone.table_ref, ...), custom_call_target="tpu_custom_call" | custom-call | flops 4000000000 | bytes 12000000 | tf_op jit(solution)/shard_map/pallas_call | solution.py:463
  3.3 3.3 %collective-permute-start.4 = (f32[704,128]{1,0:T(8,128)S(1)}, f32[704,128]{1,0:T(8,128)S(1)}, u32[]{:S(2)}, u32[]{:S(2)}) collective-permute-start(f32[704,128]{1,0:T(8,128)S(1)} %get-tuple-element.28), channel_id=1, source_target_pairs={{0,32},{32,0},{1,33},{33,1},{2,34},{34,2},{3,35},{35,3},{4,36},{36... | collective-permute-start | bytes 1081352 | tf_op jit(solution)/shard_map/ppermute | solution.py:435
  6.6 0.0 collective-permute-start
  6.6 0.5 collective-permute-start.1
  7.2 5.4 %collective-permute-start.2 = (f32[64,128]{1,0:T(8,128)S(1)}, f32[64,128]{1,0:T(8,128)S(1)}, u32[]{:S(2)}, u32[]{:S(2)}) collective-permute-start(f32[64,128]{1,0:T(8,128)S(1)} %get-tuple-element.26), channel_id=1, source_target_pairs={{0,1},{1,2},{2,3},{3,4},{4,5},{5,6},{6,7},{7,8},{8,9},{9,10},{10,1... | collective-permute-start | bytes 98312 | tf_op jit(solution)/shard_map/ppermute | solution.py:427
  12.5 4.6 %collective-permute-start.3 = (f32[64,128]{1,0:T(8,128)S(1)}, f32[64,128]{1,0:T(8,128)S(1)}, u32[]{:S(2)}, u32[]{:S(2)}) collective-permute-start(f32[64,128]{1,0:T(8,128)S(1)} %get-tuple-element.26), channel_id=1, source_target_pairs={{0,31},{1,0},{2,1},{3,2},{4,3},{5,4},{6,5},{7,6},{8,7},{9,8},{10,9... | collective-permute-start | bytes 98312 | tf_op jit(solution)/shard_map/ppermute | solution.py:427
  17.2 0.0 collective-permute-done.up_ref
  17.2 0.0 collective-permute-done.1.down_ref
  17.2 1.7 %collective-permute-done.2.right_ref = f32[64,128]{1,0:T(8,128)S(1)} collective-permute-done((f32[64,128]{1,0:T(8,128)S(1)}, f32[64,128]{1,0:T(8,128)S(1)}, u32[]{:S(2)}, u32[]{:S(2)}) %collective-permute-start.2) | collective-permute-done | bytes 32800 | tf_op jit(solution)/shard_map/ppermute | solution.py:427
  18.8 0.4 collective-permute-done.3.left_ref
  19.2 0.0 collective-permute-done.4.taken_ref
  19.2 6.6 %shard_map.139 = (f32[64,256]{1,0:T(8,128)S(1)}, f32[64,128]{1,0:T(8,128)S(1)}, f32[768,128]{1,0:T(8,128)}) custom-call(s32[1]{0:T(128)S(6)} %copy.17.count_ref, f32[64,256]{1,0:T(8,128)} %features_ref.3, f32[64,128]{1,0:T(8,128)S(1)} %collective-permute-done.up_ref, f32[64,128]{1,0:T(8,128)S(1)} %collective-permute-done.1.down_ref, ...), custom_call_target="tpu_custom_call" | custom-call | flops 10000000000 | bytes 30000000 | tf_op jit(solution)/shard_map/pallas_call | solution.py:479
  25.8 12.6 %all-to-all-start = ((f32[128,1,768]{2,1,0:T(1,128)}), f32[128,1,768]{2,1,0:T(1,128)S(1)}, u32[]{:S(2)}, u32[]{:S(2)}) async-start(f32[128,1,768]{2,1,0:T(1,128)} %bitcast.1), calls=%async_computation | async-start | bytes 786432 | tf_op jit(solution)/shard_map/all_to_all | solution.py:439
  38.3 4.6 %collective-permute-start.5 = (f32[64,128]{1,0:T(8,128)S(1)}, f32[64,128]{1,0:T(8,128)S(1)}, u32[]{:S(2)}, u32[]{:S(2)}) collective-permute-start(f32[64,128]{1,0:T(8,128)S(1)} %get-tuple-element.30), channel_id=1, source_target_pairs={{0,1},{1,2},{2,3},{3,4},{4,5},{5,6},{6,7},{7,8},{8,9},{9,10},{10,1... | collective-permute-start | bytes 98312 | tf_op jit(solution)/shard_map/ppermute | solution.py:427
  42.9 5.1 %collective-permute-start.6 = (f32[64,128]{1,0:T(8,128)S(1)}, f32[64,128]{1,0:T(8,128)S(1)}, u32[]{:S(2)}, u32[]{:S(2)}) collective-permute-start(f32[64,128]{1,0:T(8,128)S(1)} %get-tuple-element.30), channel_id=1, source_target_pairs={{0,31},{1,0},{2,1},{3,2},{4,3},{5,4},{6,5},{7,6},{8,7},{9,8},{10,9... | collective-permute-start | bytes 98312 | tf_op jit(solution)/shard_map/ppermute | solution.py:427
  48.0 4.2 %collective-permute-done.5.left_ref = f32[64,128]{1,0:T(8,128)S(1)} collective-permute-done((f32[64,128]{1,0:T(8,128)S(1)}, f32[64,128]{1,0:T(8,128)S(1)}, u32[]{:S(2)}, u32[]{:S(2)}) %collective-permute-start.5) | collective-permute-done | bytes 32800 | tf_op jit(solution)/shard_map/ppermute | solution.py:427
  52.3 0.0 collective-permute-done.6.right_ref
  52.3 0.0 all-to-all-done
  52.3 0.8 shard_map.140
  53.1 11.0 %all-to-all-start.1 = ((f32[128,1,768]{2,1,0:T(1,128)}), f32[128,1,768]{2,1,0:T(1,128)S(1)}, u32[]{:S(2)}, u32[]{:S(2)}) async-start(f32[128,1,768]{2,1,0:T(1,128)} %bitcast.3), calls=%async_computation.1 | async-start | bytes 786432 | tf_op jit(solution)/shard_map/all_to_all | solution.py:439
  64.1 6.5 %collective-permute-start.7 = (f32[64,128]{1,0:T(8,128)S(1)}, f32[64,128]{1,0:T(8,128)S(1)}, u32[]{:S(2)}, u32[]{:S(2)}) collective-permute-start(f32[64,128]{1,0:T(8,128)S(1)} %get-tuple-element.30), channel_id=1, source_target_pairs={{0,32},{32,64},{64,96},{96,128},{128,160},{160,192},{192,224},{224... | collective-permute-start | bytes 98312 | tf_op jit(solution)/shard_map/ppermute | solution.py:427
  70.6 0.0 collective-permute-start.8
  70.6 1.2 %shard_map.142 = (bf16[1408,256]{1,0:T(8,128)(2,1)S(1)}, bf16[1408,256]{1,0:T(8,128)(2,1)S(1)}) custom-call(f32[3,256]{1,0:T(4,128)} %positions_ref.3), custom_call_target="tpu_custom_call" | custom-call | flops 2000000000 | bytes 6000000 | tf_op jit(solution)/shard_map/pallas_call | solution.py:534
  71.8 0.0 collective-permute-done.7.down_ref
  71.9 4.2 %collective-permute-done.8.up_ref = f32[64,128]{1,0:T(8,128)S(1)} collective-permute-done((f32[64,128]{1,0:T(8,128)S(1)}, f32[64,128]{1,0:T(8,128)S(1)}, u32[]{:S(2)}, u32[]{:S(2)}) %collective-permute-start.8) | collective-permute-done | bytes 32800 | tf_op jit(solution)/shard_map/ppermute | solution.py:427
  76.1 1.3 %shard_map.141.partial_ref = f32[64,256]{1,0:T(8,128)S(1)} custom-call(f32[64,128]{1,0:T(8,128)S(1)} %collective-permute-done.5.left_ref, f32[64,128]{1,0:T(8,128)S(1)} %collective-permute-done.6.right_ref, f32[64,128]{1,0:T(8,128)S(1)} %collective-permute-done.7.down_ref, f32[64,128]{1,0:T(8,128)S(1)} %collective-permute-done.8.up_ref, ...), custom_call_target="tpu_custom_call" | custom-call | flops 2000000000 | bytes 6000000 | tf_op jit(solution)/shard_map/pallas_call | solution.py:527
  77.4 0.0 all-to-all-done.1
  77.4 7.0 %collective-permute-start.9 = (f32[768,128]{1,0:T(8,128)S(1)}, f32[768,128]{1,0:T(8,128)S(1)}, u32[]{:S(2)}, u32[]{:S(2)}) collective-permute-start(f32[768,128]{1,0:T(8,128)S(1)} %bitcast.6), channel_id=1, source_target_pairs={{0,32},{32,0},{1,33},{33,1},{2,34},{34,2},{3,35},{35,3},{4,36},{36... | collective-permute-start | bytes 1179656 | tf_op jit(solution)/shard_map/ppermute | solution.py:435
  84.4 0.4 shard_map.143
  84.8 0.9 %collective-permute-done.9.other_ref = f32[768,128]{1,0:T(8,128)S(1)} collective-permute-done((f32[768,128]{1,0:T(8,128)S(1)}, f32[768,128]{1,0:T(8,128)S(1)}, u32[]{:S(2)}, u32[]{:S(2)}) %collective-permute-start.9) | collective-permute-done | bytes 393248 | tf_op jit(solution)/shard_map/ppermute | solution.py:435
  85.7 2.0 %shard_map.144 = (f32[64,64]{1,0:T(8,128)}, f32[64,256]{1,0:T(8,128)}, f32[64,64]{1,0:T(8,128)}, f32[8,64]{1,0:T(8,128)}) custom-call(s32[1]{0:T(128)S(6)} %copy.17.count_ref, f32[768,128]{1,0:T(8,128)S(1)} %collective-permute-done.9.other_ref, bf16[1408,256]{1,0:T(8,128)(2,1)S(1)} %get-tuple-element.38.high_ref, ...), custom_call_target="tpu_custom_call" | custom-call | flops 3000000000 | bytes 9000000 | tf_op jit(solution)/shard_map/pallas_call | solution.py:551
Async XLA Ops:
  3.3 15.9 %collective-permute-start.4 = (f32[704,128]{1,0:T(8,128)S(1)}, f32[704,128]{1,0:T(8,128)S(1)}, u32[]{:S(2)}, u32[]{:S(2)}) collective-permute-start(f32[704,128]{1,0:T(8,128)S(1)} %get-tuple-element.28), channel_id=1, source_target_pairs={{0,32},{32,0},{1,33},{33,1},{2,34},{34,2},{3,35},{35,3},{4,36},{36... | collective-permute-start | bytes 1081352 | tf_op jit(solution)/shard_map/ppermute | solution.py:435
  6.6 10.5 %collective-permute-start = (f32[64,128]{1,0:T(8,128)S(1)}, f32[64,128]{1,0:T(8,128)S(1)}, u32[]{:S(2)}, u32[]{:S(2)}) collective-permute-start(f32[64,128]{1,0:T(8,128)S(1)} %get-tuple-element.26), channel_id=1, source_target_pairs={{0,32},{32,64},{64,96},{96,128},{128,160},{160,192},{192,224},{224... | collective-permute-start | bytes 98312 | tf_op jit(solution)/shard_map/ppermute | solution.py:427
  6.6 10.5 %collective-permute-start.1 = (f32[64,128]{1,0:T(8,128)S(1)}, f32[64,128]{1,0:T(8,128)S(1)}, u32[]{:S(2)}, u32[]{:S(2)}) collective-permute-start(f32[64,128]{1,0:T(8,128)S(1)} %get-tuple-element.26), channel_id=1, source_target_pairs={{0,224},{32,0},{64,32},{96,64},{128,96},{160,128},{192,160},{224,1... | collective-permute-start | bytes 98312 | tf_op jit(solution)/shard_map/ppermute | solution.py:427
  7.2 11.7 %collective-permute-start.2 = (f32[64,128]{1,0:T(8,128)S(1)}, f32[64,128]{1,0:T(8,128)S(1)}, u32[]{:S(2)}, u32[]{:S(2)}) collective-permute-start(f32[64,128]{1,0:T(8,128)S(1)} %get-tuple-element.26), channel_id=1, source_target_pairs={{0,1},{1,2},{2,3},{3,4},{4,5},{5,6},{6,7},{7,8},{8,9},{9,10},{10,1... | collective-permute-start | bytes 98312 | tf_op jit(solution)/shard_map/ppermute | solution.py:427
  12.5 6.7 %collective-permute-start.3 = (f32[64,128]{1,0:T(8,128)S(1)}, f32[64,128]{1,0:T(8,128)S(1)}, u32[]{:S(2)}, u32[]{:S(2)}) collective-permute-start(f32[64,128]{1,0:T(8,128)S(1)} %get-tuple-element.26), channel_id=1, source_target_pairs={{0,31},{1,0},{2,1},{3,2},{4,3},{5,4},{6,5},{7,6},{8,7},{9,8},{10,9... | collective-permute-start | bytes 98312 | tf_op jit(solution)/shard_map/ppermute | solution.py:427
  25.8 26.5 %all-to-all-start = ((f32[128,1,768]{2,1,0:T(1,128)}), f32[128,1,768]{2,1,0:T(1,128)S(1)}, u32[]{:S(2)}, u32[]{:S(2)}) async-start(f32[128,1,768]{2,1,0:T(1,128)} %bitcast.1), calls=%async_computation | async-start | bytes 786432 | tf_op jit(solution)/shard_map/all_to_all | solution.py:439
  38.3 13.9 %collective-permute-start.5 = (f32[64,128]{1,0:T(8,128)S(1)}, f32[64,128]{1,0:T(8,128)S(1)}, u32[]{:S(2)}, u32[]{:S(2)}) collective-permute-start(f32[64,128]{1,0:T(8,128)S(1)} %get-tuple-element.30), channel_id=1, source_target_pairs={{0,1},{1,2},{2,3},{3,4},{4,5},{5,6},{6,7},{7,8},{8,9},{9,10},{10,1... | collective-permute-start | bytes 98312 | tf_op jit(solution)/shard_map/ppermute | solution.py:427
  42.9 9.4 %collective-permute-start.6 = (f32[64,128]{1,0:T(8,128)S(1)}, f32[64,128]{1,0:T(8,128)S(1)}, u32[]{:S(2)}, u32[]{:S(2)}) collective-permute-start(f32[64,128]{1,0:T(8,128)S(1)} %get-tuple-element.30), channel_id=1, source_target_pairs={{0,31},{1,0},{2,1},{3,2},{4,3},{5,4},{6,5},{7,6},{8,7},{9,8},{10,9... | collective-permute-start | bytes 98312 | tf_op jit(solution)/shard_map/ppermute | solution.py:427
  53.1 24.3 %all-to-all-start.1 = ((f32[128,1,768]{2,1,0:T(1,128)}), f32[128,1,768]{2,1,0:T(1,128)S(1)}, u32[]{:S(2)}, u32[]{:S(2)}) async-start(f32[128,1,768]{2,1,0:T(1,128)} %bitcast.3), calls=%async_computation.1 | async-start | bytes 786432 | tf_op jit(solution)/shard_map/all_to_all | solution.py:439
  64.1 7.8 %collective-permute-start.7 = (f32[64,128]{1,0:T(8,128)S(1)}, f32[64,128]{1,0:T(8,128)S(1)}, u32[]{:S(2)}, u32[]{:S(2)}) collective-permute-start(f32[64,128]{1,0:T(8,128)S(1)} %get-tuple-element.30), channel_id=1, source_target_pairs={{0,32},{32,64},{64,96},{96,128},{128,160},{160,192},{192,224},{224... | collective-permute-start | bytes 98312 | tf_op jit(solution)/shard_map/ppermute | solution.py:427
  70.6 5.5 %collective-permute-start.8 = (f32[64,128]{1,0:T(8,128)S(1)}, f32[64,128]{1,0:T(8,128)S(1)}, u32[]{:S(2)}, u32[]{:S(2)}) collective-permute-start(f32[64,128]{1,0:T(8,128)S(1)} %get-tuple-element.30), channel_id=1, source_target_pairs={{0,224},{32,0},{64,32},{96,64},{128,96},{160,128},{192,160},{224,1... | collective-permute-start | bytes 98312 | tf_op jit(solution)/shard_map/ppermute | solution.py:427
  77.4 8.3 %collective-permute-start.9 = (f32[768,128]{1,0:T(8,128)S(1)}, f32[768,128]{1,0:T(8,128)S(1)}, u32[]{:S(2)}, u32[]{:S(2)}) collective-permute-start(f32[768,128]{1,0:T(8,128)S(1)} %bitcast.6), channel_id=1, source_target_pairs={{0,32},{32,0},{1,33},{33,1},{2,34},{34,2},{3,35},{35,3},{4,36},{36... | collective-permute-start | bytes 1179656 | tf_op jit(solution)/shard_map/ppermute | solution.py:435

commit v7 on v6

--- a/solution.py
+++ b/solution.py
@@ -512,7 +512,6 @@
     back_left = shifted(ghost, "brick", -1)
     back_up = shifted(ghost, SLAB, 1)
     back_down = shifted(ghost, SLAB, -1)
-    pieces, back_right, back_left = lax.optimization_barrier((pieces, back_right, back_left))
     summed = pl.pallas_call(
         functools.partial(sum_kernel, width=rows // chips),
         out_shape=near(rows, 128),

time: 88.2 us -> 84 us (0.952)
  blocking collectives: 0 us -> 25.1 us
  starting transfers between devices: 60.6 us -> 38.1 us
  waiting for transfers between devices: 11.4 us -> 5.36 us
    all_to_all x0 -> x1, blocking collectives: none -> 25.1 us  [exchange(): return lax.all_to_all(value, axes, 0, 0, tiled=True)]
    all_to_all x2 -> x1, starting transfers between devices: 23.6 us -> 6.84 us  [exchange(): return lax.all_to_all(value, axes, 0, 0, tiled=True)]
    ppermute x8, waiting for transfers between devices: 10.5 us -> 4.42 us  [shifted(): lax.ppermute(value, axis, [(i, (i + step) % size) for i in range(size)])]
    ppermute x2, starting transfers between devices: 10.3 us -> 4.29 us  [swapped(): return lax.ppermute(value, 'core', [(0, 1), (1, 0)])]
  transfers between devices with their start and end apart: 12 -> 11, of which waited for: 5 -> 4; matrix products, arithmetic and copies ran while one was open for 0% -> 0% of each run, Pallas kernels for 3% -> 4%
where the time goes in v7:
time: 84 us; the launch traced here: 83.5 us
  starting transfers between devices  38.1 us (45%)
  blocking collectives  25.1 us (30%)
  Pallas kernels  13.7 us (16%)
  waiting for transfers between devices  5.36 us (6%)
  between operations  1.36 us (2%)
    ppermute x8, starting transfers between devices, shifted(): lax.ppermute(value, axis, [(i, (i + step) % size) for i in range(size)])  27 us
    all_to_all x1, blocking collectives, exchange(): return lax.all_to_all(value, axes, 0, 0, tiled=True)  25.1 us
    all_to_all x1, starting transfers between devices, exchange(): return lax.all_to_all(value, axes, 0, 0, tiled=True)  6.84 us
    pallas_call x1, Pallas kernels, on_device(): pl.pallas_call(functools.partial(edge_kernel, factor=factor), out_shape=(...  5.83 us
    ppermute x8, waiting for transfers between devices, shifted(): lax.ppermute(value, axis, [(i, (i + step) % size) for i in range(size)])  4.42 us
    ppermute x2, starting transfers between devices, swapped(): return lax.ppermute(value, 'core', [(0, 1), (1, 0)])  4.29 us
    pallas_call x1, Pallas kernels, on_device(): pl.pallas_call(wave_kernel, out_shape=(near(half, 128), near(half, 128),...  2.03 us
    pallas_call x1, Pallas kernels, on_device(): pl.pallas_call(functools.partial(charge_kernel, factor=factor), out_shape...  2 us
  transfers between devices with their start and end apart: 11, of which 4 were waited for; matrix products, arithmetic and copies ran while one was open for 0% of the time, Pallas kernels for 4%

profile of v7, /device:TPU:1, one launch (start us, length us, event | category | flops | bytes accessed | tf_op | source)
XLA Modules:
  0.0 83.5 jit_solution(13584134360219520827)
XLA Ops:
  1.3 2.0 %shard_map.138 = (f32[704,128]{1,0:T(8,128)S(1)}, f32[704,128]{1,0:T(8,128)S(1)}, f32[64,128]{1,0:T(8,128)S(1)}) custom-call(s32[1]{0:T(128)S(6)} %copy.17.count_ref, f32[3,256]{1,0:T(4,128)} %positions_ref.3, f32[64,256]{1,0:T(8,128)} %cotangent_ref.3, f32[64,256]{1,0:T(8,128)} %features_ref.3, f32[704,128]{1,0:T(8,128)} %constant.2.clone.table_ref, ...), custom_call_target="tpu_custom_call" | custom-call | flops 4000000000 | bytes 12000000 | tf_op jit(solution)/shard_map/pallas_call | solution.py:463
  3.3 3.3 %collective-permute-start.4 = (f32[704,128]{1,0:T(8,128)S(1)}, f32[704,128]{1,0:T(8,128)S(1)}, u32[]{:S(2)}, u32[]{:S(2)}) collective-permute-start(f32[704,128]{1,0:T(8,128)S(1)} %get-tuple-element.25), channel_id=1, source_target_pairs={{0,32},{32,0},{1,33},{33,1},{2,34},{34,2},{3,35},{35,3},{4,36},{36... | collective-permute-start | bytes 1081352 | tf_op jit(solution)/shard_map/ppermute | solution.py:435
  6.6 0.0 collective-permute-start
  6.6 0.5 collective-permute-start.1
  7.2 5.4 %collective-permute-start.2 = (f32[64,128]{1,0:T(8,128)S(1)}, f32[64,128]{1,0:T(8,128)S(1)}, u32[]{:S(2)}, u32[]{:S(2)}) collective-permute-start(f32[64,128]{1,0:T(8,128)S(1)} %get-tuple-element.23), channel_id=1, source_target_pairs={{0,1},{1,2},{2,3},{3,4},{4,5},{5,6},{6,7},{7,8},{8,9},{9,10},{10,1... | collective-permute-start | bytes 98312 | tf_op jit(solution)/shard_map/ppermute | solution.py:427
  12.5 4.6 %collective-permute-start.3 = (f32[64,128]{1,0:T(8,128)S(1)}, f32[64,128]{1,0:T(8,128)S(1)}, u32[]{:S(2)}, u32[]{:S(2)}) collective-permute-start(f32[64,128]{1,0:T(8,128)S(1)} %get-tuple-element.23), channel_id=1, source_target_pairs={{0,31},{1,0},{2,1},{3,2},{4,3},{5,4},{6,5},{7,6},{8,7},{9,8},{10,9... | collective-permute-start | bytes 98312 | tf_op jit(solution)/shard_map/ppermute | solution.py:427
  17.2 0.0 collective-permute-done.up_ref
  17.2 0.0 collective-permute-done.1.down_ref
  17.2 1.7 %collective-permute-done.2.right_ref = f32[64,128]{1,0:T(8,128)S(1)} collective-permute-done((f32[64,128]{1,0:T(8,128)S(1)}, f32[64,128]{1,0:T(8,128)S(1)}, u32[]{:S(2)}, u32[]{:S(2)}) %collective-permute-start.2) | collective-permute-done | bytes 32800 | tf_op jit(solution)/shard_map/ppermute | solution.py:427
  18.8 0.4 collective-permute-done.3.left_ref
  19.2 0.0 collective-permute-done.4.taken_ref
  19.2 5.8 %shard_map.139 = (f32[64,256]{1,0:T(8,128)S(1)}, f32[64,128]{1,0:T(8,128)S(1)}, f32[768,128]{1,0:T(8,128)S(1)}) custom-call(s32[1]{0:T(128)S(6)} %copy.17.count_ref, f32[64,256]{1,0:T(8,128)} %features_ref.3, f32[64,128]{1,0:T(8,128)S(1)} %collective-permute-done.up_ref, f32[64,128]{1,0:T(8,128)S(1)} %collective-permute-done.1.down_ref, ...), custom_call_target="tpu_custom_call" | custom-call | flops 10000000000 | bytes 30000000 | tf_op jit(solution)/shard_map/pallas_call | solution.py:479
  25.1 25.1 %all_to_all.10 = f32[128,1,768]{2,1,0:T(1,128)S(1)} all-to-all(f32[128,1,768]{2,1,0:T(1,128)S(1)} %bitcast.8), channel_id=1, replica_groups=mesh['chip'=4,'core'=2,'brick'=32] {'chip','brick'}, dimensions={0} | all-to-all | bytes 786432 | tf_op jit(solution)/shard_map/all_to_all | solution.py:439
  50.1 0.8 shard_map.140
  50.9 6.8 %all-to-all-start.1 = ((f32[128,1,768]{2,1,0:T(1,128)}), f32[128,1,768]{2,1,0:T(1,128)S(1)}, u32[]{:S(2)}, u32[]{:S(2)}) async-start(f32[128,1,768]{2,1,0:T(1,128)} %bitcast.3), calls=%async_computation.1 | async-start | bytes 786432 | tf_op jit(solution)/shard_map/all_to_all | solution.py:439
  57.8 4.6 %collective-permute-start.5 = (f32[64,128]{1,0:T(8,128)S(1)}, f32[64,128]{1,0:T(8,128)S(1)}, u32[]{:S(2)}, u32[]{:S(2)}) collective-permute-start(f32[64,128]{1,0:T(8,128)S(1)} %get-tuple-element.27), channel_id=1, source_target_pairs={{0,1},{1,2},{2,3},{3,4},{4,5},{5,6},{6,7},{7,8},{8,9},{9,10},{10,1... | collective-permute-start | bytes 98312 | tf_op jit(solution)/shard_map/ppermute | solution.py:427
  62.3 5.1 %collective-permute-start.6 = (f32[64,128]{1,0:T(8,128)S(1)}, f32[64,128]{1,0:T(8,128)S(1)}, u32[]{:S(2)}, u32[]{:S(2)}) collective-permute-start(f32[64,128]{1,0:T(8,128)S(1)} %get-tuple-element.27), channel_id=1, source_target_pairs={{0,31},{1,0},{2,1},{3,2},{4,3},{5,4},{6,5},{7,6},{8,7},{9,8},{10,9... | collective-permute-start | bytes 98312 | tf_op jit(solution)/shard_map/ppermute | solution.py:427
  67.5 6.8 %collective-permute-start.7 = (f32[64,128]{1,0:T(8,128)S(1)}, f32[64,128]{1,0:T(8,128)S(1)}, u32[]{:S(2)}, u32[]{:S(2)}) collective-permute-start(f32[64,128]{1,0:T(8,128)S(1)} %get-tuple-element.27), channel_id=1, source_target_pairs={{0,32},{32,64},{64,96},{96,128},{128,160},{160,192},{192,224},{224... | collective-permute-start | bytes 98312 | tf_op jit(solution)/shard_map/ppermute | solution.py:427
  74.2 0.0 collective-permute-start.8
  74.2 1.2 %shard_map.142 = (bf16[1408,256]{1,0:T(8,128)(2,1)S(1)}, bf16[1408,256]{1,0:T(8,128)(2,1)S(1)}) custom-call(f32[3,256]{1,0:T(4,128)} %positions_ref.3), custom_call_target="tpu_custom_call" | custom-call | flops 2000000000 | bytes 6000000 | tf_op jit(solution)/shard_map/pallas_call | solution.py:533
  75.4 0.0 collective-permute-done.5.left_ref
  75.4 0.0 collective-permute-done.6.right_ref
  75.5 0.0 collective-permute-done.7.down_ref
  75.5 2.4 %collective-permute-done.8.up_ref = f32[64,128]{1,0:T(8,128)S(1)} collective-permute-done((f32[64,128]{1,0:T(8,128)S(1)}, f32[64,128]{1,0:T(8,128)S(1)}, u32[]{:S(2)}, u32[]{:S(2)}) %collective-permute-start.8) | collective-permute-done | bytes 32800 | tf_op jit(solution)/shard_map/ppermute | solution.py:427
  77.9 1.3 %shard_map.141.partial_ref = f32[64,256]{1,0:T(8,128)S(1)} custom-call(f32[64,128]{1,0:T(8,128)S(1)} %collective-permute-done.5.left_ref, f32[64,128]{1,0:T(8,128)S(1)} %collective-permute-done.6.right_ref, f32[64,128]{1,0:T(8,128)S(1)} %collective-permute-done.7.down_ref, f32[64,128]{1,0:T(8,128)S(1)} %collective-permute-done.8.up_ref, ...), custom_call_target="tpu_custom_call" | custom-call | flops 2000000000 | bytes 6000000 | tf_op jit(solution)/shard_map/pallas_call | solution.py:526
  79.2 0.0 all-to-all-done.1
  79.2 1.0 %collective-permute-start.9 = (f32[768,128]{1,0:T(8,128)S(1)}, f32[768,128]{1,0:T(8,128)S(1)}, u32[]{:S(2)}, u32[]{:S(2)}) collective-permute-start(f32[768,128]{1,0:T(8,128)S(1)} %bitcast.6), channel_id=1, source_target_pairs={{0,32},{32,0},{1,33},{33,1},{2,34},{34,2},{3,35},{35,3},{4,36},{36... | collective-permute-start | bytes 1179656 | tf_op jit(solution)/shard_map/ppermute | solution.py:435
  80.2 0.4 shard_map.143
  80.6 0.9 %collective-permute-done.9.other_ref = f32[768,128]{1,0:T(8,128)S(1)} collective-permute-done((f32[768,128]{1,0:T(8,128)S(1)}, f32[768,128]{1,0:T(8,128)S(1)}, u32[]{:S(2)}, u32[]{:S(2)}) %collective-permute-start.9) | collective-permute-done | bytes 393248 | tf_op jit(solution)/shard_map/ppermute | solution.py:435
  81.5 2.0 %shard_map.144 = (f32[64,64]{1,0:T(8,128)}, f32[64,256]{1,0:T(8,128)}, f32[64,64]{1,0:T(8,128)}, f32[8,64]{1,0:T(8,128)}) custom-call(s32[1]{0:T(128)S(6)} %copy.17.count_ref, f32[768,128]{1,0:T(8,128)S(1)} %collective-permute-done.9.other_ref, bf16[1408,256]{1,0:T(8,128)(2,1)S(1)} %get-tuple-element.32.high_ref, ...), custom_call_target="tpu_custom_call" | custom-call | flops 3000000000 | bytes 9000000 | tf_op jit(solution)/shard_map/pallas_call | solution.py:550
Async XLA Ops:
  3.3 15.9 %collective-permute-start.4 = (f32[704,128]{1,0:T(8,128)S(1)}, f32[704,128]{1,0:T(8,128)S(1)}, u32[]{:S(2)}, u32[]{:S(2)}) collective-permute-start(f32[704,128]{1,0:T(8,128)S(1)} %get-tuple-element.25), channel_id=1, source_target_pairs={{0,32},{32,0},{1,33},{33,1},{2,34},{34,2},{3,35},{35,3},{4,36},{36... | collective-permute-start | bytes 1081352 | tf_op jit(solution)/shard_map/ppermute | solution.py:435
  6.6 10.5 %collective-permute-start = (f32[64,128]{1,0:T(8,128)S(1)}, f32[64,128]{1,0:T(8,128)S(1)}, u32[]{:S(2)}, u32[]{:S(2)}) collective-permute-start(f32[64,128]{1,0:T(8,128)S(1)} %get-tuple-element.23), channel_id=1, source_target_pairs={{0,32},{32,64},{64,96},{96,128},{128,160},{160,192},{192,224},{224... | collective-permute-start | bytes 98312 | tf_op jit(solution)/shard_map/ppermute | solution.py:427
  6.6 10.5 %collective-permute-start.1 = (f32[64,128]{1,0:T(8,128)S(1)}, f32[64,128]{1,0:T(8,128)S(1)}, u32[]{:S(2)}, u32[]{:S(2)}) collective-permute-start(f32[64,128]{1,0:T(8,128)S(1)} %get-tuple-element.23), channel_id=1, source_target_pairs={{0,224},{32,0},{64,32},{96,64},{128,96},{160,128},{192,160},{224,1... | collective-permute-start | bytes 98312 | tf_op jit(solution)/shard_map/ppermute | solution.py:427
  7.2 11.7 %collective-permute-start.2 = (f32[64,128]{1,0:T(8,128)S(1)}, f32[64,128]{1,0:T(8,128)S(1)}, u32[]{:S(2)}, u32[]{:S(2)}) collective-permute-start(f32[64,128]{1,0:T(8,128)S(1)} %get-tuple-element.23), channel_id=1, source_target_pairs={{0,1},{1,2},{2,3},{3,4},{4,5},{5,6},{6,7},{7,8},{8,9},{9,10},{10,1... | collective-permute-start | bytes 98312 | tf_op jit(solution)/shard_map/ppermute | solution.py:427
  12.5 6.7 %collective-permute-start.3 = (f32[64,128]{1,0:T(8,128)S(1)}, f32[64,128]{1,0:T(8,128)S(1)}, u32[]{:S(2)}, u32[]{:S(2)}) collective-permute-start(f32[64,128]{1,0:T(8,128)S(1)} %get-tuple-element.23), channel_id=1, source_target_pairs={{0,31},{1,0},{2,1},{3,2},{4,3},{5,4},{6,5},{7,6},{8,7},{9,8},{10,9... | collective-permute-start | bytes 98312 | tf_op jit(solution)/shard_map/ppermute | solution.py:427
  50.9 28.3 %all-to-all-start.1 = ((f32[128,1,768]{2,1,0:T(1,128)}), f32[128,1,768]{2,1,0:T(1,128)S(1)}, u32[]{:S(2)}, u32[]{:S(2)}) async-start(f32[128,1,768]{2,1,0:T(1,128)} %bitcast.3), calls=%async_computation.1 | async-start | bytes 786432 | tf_op jit(solution)/shard_map/all_to_all | solution.py:439
  57.8 17.7 %collective-permute-start.5 = (f32[64,128]{1,0:T(8,128)S(1)}, f32[64,128]{1,0:T(8,128)S(1)}, u32[]{:S(2)}, u32[]{:S(2)}) collective-permute-start(f32[64,128]{1,0:T(8,128)S(1)} %get-tuple-element.27), channel_id=1, source_target_pairs={{0,1},{1,2},{2,3},{3,4},{4,5},{5,6},{6,7},{7,8},{8,9},{9,10},{10,1... | collective-permute-start | bytes 98312 | tf_op jit(solution)/shard_map/ppermute | solution.py:427
  62.3 13.1 %collective-permute-start.6 = (f32[64,128]{1,0:T(8,128)S(1)}, f32[64,128]{1,0:T(8,128)S(1)}, u32[]{:S(2)}, u32[]{:S(2)}) collective-permute-start(f32[64,128]{1,0:T(8,128)S(1)} %get-tuple-element.27), channel_id=1, source_target_pairs={{0,31},{1,0},{2,1},{3,2},{4,3},{5,4},{6,5},{7,6},{8,7},{9,8},{10,9... | collective-permute-start | bytes 98312 | tf_op jit(solution)/shard_map/ppermute | solution.py:427
  67.5 8.0 %collective-permute-start.7 = (f32[64,128]{1,0:T(8,128)S(1)}, f32[64,128]{1,0:T(8,128)S(1)}, u32[]{:S(2)}, u32[]{:S(2)}) collective-permute-start(f32[64,128]{1,0:T(8,128)S(1)} %get-tuple-element.27), channel_id=1, source_target_pairs={{0,32},{32,64},{64,96},{96,128},{128,160},{160,192},{192,224},{224... | collective-permute-start | bytes 98312 | tf_op jit(solution)/shard_map/ppermute | solution.py:427
  74.2 3.6 %collective-permute-start.8 = (f32[64,128]{1,0:T(8,128)S(1)}, f32[64,128]{1,0:T(8,128)S(1)}, u32[]{:S(2)}, u32[]{:S(2)}) collective-permute-start(f32[64,128]{1,0:T(8,128)S(1)} %get-tuple-element.27), channel_id=1, source_target_pairs={{0,224},{32,0},{64,32},{96,64},{128,96},{160,128},{192,160},{224,1... | collective-permute-start | bytes 98312 | tf_op jit(solution)/shard_map/ppermute | solution.py:427
  79.2 2.3 %collective-permute-start.9 = (f32[768,128]{1,0:T(8,128)S(1)}, f32[768,128]{1,0:T(8,128)S(1)}, u32[]{:S(2)}, u32[]{:S(2)}) collective-permute-start(f32[768,128]{1,0:T(8,128)S(1)} %bitcast.6), channel_id=1, source_target_pairs={{0,32},{32,0},{1,33},{33,1},{2,34},{34,2},{3,35},{35,3},{4,36},{36... | collective-permute-start | bytes 1179656 | tf_op jit(solution)/shard_map/ppermute | solution.py:435

commit v8 on v7

--- a/solution.py
+++ b/solution.py
@@ -146,12 +146,20 @@
     return (atom == jnp.round(wanted)).astype(F32).astype(BF16)
 
 
-def pick_lanes(refs):
-    place = lax.broadcasted_iota(jnp.int32, (64, 128), 1) // 32
-    value = refs[3][...]
-    for slot in range(3):
-        value = jnp.where(place == slot, refs[slot][...], value)
-    return value
+def packed(value, place):
+    lanes = slice(32 * place, 32 * place + 32)
+    return jnp.concatenate([value[16 * q : 16 * q + 16, lanes] for q in range(4)], axis=1)
+
+
+def unpacked(refs):
+    values = [ref[...] for ref in refs]
+    return jnp.concatenate(
+        [
+            jnp.concatenate([value[:, 32 * q : 32 * q + 32] for value in values], axis=1)
+            for q in range(4)
+        ],
+        axis=0,
+    )
 
 
 def wave_kernel(
@@ -163,14 +171,19 @@
     map_ref,
     keep_ref,
     give_ref,
-    outgoing_ref,
+    up_ref,
+    down_ref,
+    right_ref,
+    left_ref,
     parts_ref,
 ):
     features = features_ref[...]
     selector = send_selector(map_ref[...], features.shape[1])
     top, rest = split(features)
     middle, bottom = split(features - top.astype(F32))
-    outgoing_ref[...] = dot(top, selector) + (dot(middle, selector) + dot(bottom, selector))
+    outgoing = dot(top, selector) + (dot(middle, selector) + dot(bottom, selector))
+    for place, ref in enumerate((up_ref, down_ref, right_ref, left_ref)):
+        ref[...] = packed(outgoing, place)
     chunk = chunk_waves(positions_ref[...])
     live = live_row(count_ref, positions_ref.shape[1])
     both = jnp.concatenate([cotangent_ref[...] * live, features * live], axis=0)
@@ -206,7 +219,10 @@
     keep_ref,
     taken_ref,
     own_ref,
-    ghost_ref,
+    ghost_up_ref,
+    ghost_down_ref,
+    ghost_right_ref,
+    ghost_left_ref,
     payload_ref,
     basis_ref,
     selector_ref,
@@ -227,7 +243,7 @@
     waves = keep_ref.shape[0]
     payload_ref[:waves, :] = keep_ref[...] + taken_ref[...]
     extended = jnp.concatenate(
-        [features_ref[...], pick_lanes((up_ref, down_ref, right_ref, left_ref))], axis=1
+        [features_ref[...], unpacked((up_ref, down_ref, right_ref, left_ref))], axis=1
     )
     projected = jnp.concatenate(split(dot_full(short_ref[...], extended)), axis=0)
     live = live_row(count_ref, atoms)
@@ -314,7 +330,8 @@
     radial = radial[:channels] + radial[channels:]
     radial = radial[:, :8] + radial[:, 8:]
     own_ref[...] = grads[:, :atoms]
-    ghost_ref[...] = grads[:, atoms:]
+    for place, ref in enumerate((ghost_up_ref, ghost_down_ref, ghost_right_ref, ghost_left_ref)):
+        ref[...] = packed(grads[:, atoms:], place)
     short_part = dot_full(grads, extended, ((1,), (1,))) * factor
     payload_ref[waves:, :] = jnp.concatenate(
         [short_part, radial * factor, jnp.zeros((channels, 128 - channels - 8), F32)], axis=1
@@ -322,7 +339,7 @@
 
 
 def return_kernel(left_ref, right_ref, down_ref, up_ref, own_ref, map_ref, short_ref, out_ref):
-    back = pick_lanes((up_ref, down_ref, right_ref, left_ref))
+    back = unpacked((up_ref, down_ref, right_ref, left_ref))
     selector = send_selector(map_ref[...], own_ref.shape[1])
     high, low = split(back)
     owned = own_ref[...] + (
@@ -460,27 +477,28 @@
     rows = half + channels
     width = rows // chips * 128
 
-    keep, give, outgoing = pl.pallas_call(
+    message = near(channels // 4, 128)
+    keep, give, *outgoing = pl.pallas_call(
         wave_kernel,
-        out_shape=(near(half, 128), near(half, 128), near(channels, 128)),
+        out_shape=(near(half, 128), near(half, 128)) + (message,) * 4,
         in_specs=scalar_first(5),
-        out_specs=tuple(vmem(3)),
+        out_specs=tuple(vmem(6)),
         scratch_shapes=[pltpu.VMEM((2 * half, 128), F32)],
         cost_estimate=work(4.0),
     )(atom_count, positions, cotangent, features, jnp.asarray(weight_table(factor)), send_map)
-    up = shifted(outgoing, SLAB, 1)
-    down = shifted(outgoing, SLAB, -1)
-    right = shifted(outgoing, "brick", 1)
-    left = shifted(outgoing, "brick", -1)
+    up = shifted(outgoing[0], SLAB, 1)
+    down = shifted(outgoing[1], SLAB, -1)
+    right = shifted(outgoing[2], "brick", 1)
+    left = shifted(outgoing[3], "brick", -1)
     taken = swapped(give)
 
     up, down, right, left = (close(x) for x in (up, down, right, left))
     keep, taken = close(keep), close(taken)
-    own, ghost, payload = pl.pallas_call(
+    own, *ghost, payload = pl.pallas_call(
         functools.partial(edge_kernel, factor=factor),
-        out_shape=(near(channels, atoms), near(channels, 128), near(rows, 128)),
+        out_shape=(near(channels, atoms),) + (message,) * 4 + (near(rows, 128),),
         in_specs=scalar_first(12),
-        out_specs=tuple(vmem(3)),
+        out_specs=tuple(vmem(6)),
         scratch_shapes=[
             pltpu.VMEM((slots * 8, atoms), F32),
             pltpu.VMEM((slots // 4, atoms + 128, 4 * atoms), BF16),
@@ -508,10 +526,10 @@
         taken,
     )
     pieces = exchange(payload.reshape(chips, 1, width), CHIPS)
-    back_right = shifted(ghost, "brick", 1)
-    back_left = shifted(ghost, "brick", -1)
-    back_up = shifted(ghost, SLAB, 1)
-    back_down = shifted(ghost, SLAB, -1)
+    back_right = shifted(ghost[3], "brick", 1)
+    back_left = shifted(ghost[2], "brick", -1)
+    back_up = shifted(ghost[1], SLAB, 1)
+    back_down = shifted(ghost[0], SLAB, -1)
     summed = pl.pallas_call(
         functools.partial(sum_kernel, width=rows // chips),
         out_shape=near(rows, 128),

time: 84 us -> 83.3 us (level)
  no operation moved by 1% of the time
where the time goes in v8:
time: 83.3 us; the launch traced here: 82.8 us
  starting transfers between devices  38.1 us (46%)
  blocking collectives  24.9 us (30%)
  Pallas kernels  13.7 us (16%)
  waiting for transfers between devices  4.81 us (6%)
  between operations  1.36 us (2%)
    ppermute x8, starting transfers between devices, shifted(): lax.ppermute(value, axis, [(i, (i + step) % size) for i in range(size)])  27.2 us
    all_to_all x1, blocking collectives, exchange(): return lax.all_to_all(value, axes, 0, 0, tiled=True)  24.9 us
    all_to_all x1, starting transfers between devices, exchange(): return lax.all_to_all(value, axes, 0, 0, tiled=True)  6.85 us
    pallas_call x1, Pallas kernels, on_device(): pl.pallas_call(functools.partial(edge_kernel, factor=factor), out_shape=(...  5.86 us
    ppermute x2, starting transfers between devices, swapped(): return lax.ppermute(value, 'core', [(0, 1), (1, 0)])  4.12 us
    ppermute x8, waiting for transfers between devices, shifted(): lax.ppermute(value, axis, [(i, (i + step) % size) for i in range(size)])  3.88 us
    pallas_call x1, Pallas kernels, on_device(): pl.pallas_call(wave_kernel, out_shape=(near(half, 128), near(half, 128))...  2.03 us
    pallas_call x1, Pallas kernels, on_device(): pl.pallas_call(functools.partial(charge_kernel, factor=factor), out_shape...  2 us
  transfers between devices with their start and end apart: 11, of which 4 were waited for; matrix products, arithmetic and copies ran while one was open for 0% of the time, Pallas kernels for 4%

profile of v8, /device:TPU:1, one launch (start us, length us, event | category | flops | bytes accessed | tf_op | source)
XLA Modules:
  0.0 82.8 jit_solution(10790872105347153140)
XLA Ops:
  1.3 2.0 %shard_map.138 = (f32[704,128]{1,0:T(8,128)S(1)}, f32[704,128]{1,0:T(8,128)S(1)}, f32[16,128]{1,0:T(8,128)S(1)}, f32[16,128]{1,0:T(8,128)S(1)}, f32[16,128]{1,0:T(8,128)S(1)}, /*index=5*/f32[16,128]{1,0:T(8,128)S(1)}) custom-call(s32[1]{0:T(128)S(6)} %copy.17.count_ref, f32[3,256]{1,0:T(4,128)} %positions_ref.3, f32[64,256]{1,0:T(8,128)} %cotangent_ref.3, ...), custom_call_target="tpu_custom_call" | custom-call | flops 4000000000 | bytes 12000000 | tf_op jit(solution)/shard_map/pallas_call | solution.py:481
  3.3 3.3 %collective-permute-start.4 = (f32[704,128]{1,0:T(8,128)S(1)}, f32[704,128]{1,0:T(8,128)S(1)}, u32[]{:S(2)}, u32[]{:S(2)}) collective-permute-start(f32[704,128]{1,0:T(8,128)S(1)} %get-tuple-element.34), channel_id=1, source_target_pairs={{0,32},{32,0},{1,33},{33,1},{2,34},{34,2},{3,35},{35,3},{4,36},{36... | collective-permute-start | bytes 1081352 | tf_op jit(solution)/shard_map/ppermute | solution.py:452
  6.6 0.0 collective-permute-start
  6.6 0.5 collective-permute-start.1
  7.2 5.4 %collective-permute-start.2 = (f32[16,128]{1,0:T(8,128)S(1)}, f32[16,128]{1,0:T(8,128)S(1)}, u32[]{:S(2)}, u32[]{:S(2)}) collective-permute-start(f32[16,128]{1,0:T(8,128)S(1)} %get-tuple-element.31), channel_id=1, source_target_pairs={{0,1},{1,2},{2,3},{3,4},{4,5},{5,6},{6,7},{7,8},{8,9},{9,10},{10,1... | collective-permute-start | bytes 24584 | tf_op jit(solution)/shard_map/ppermute | solution.py:444
  12.5 4.7 %collective-permute-start.3 = (f32[16,128]{1,0:T(8,128)S(1)}, f32[16,128]{1,0:T(8,128)S(1)}, u32[]{:S(2)}, u32[]{:S(2)}) collective-permute-start(f32[16,128]{1,0:T(8,128)S(1)} %get-tuple-element.32), channel_id=1, source_target_pairs={{0,31},{1,0},{2,1},{3,2},{4,3},{5,4},{6,5},{7,6},{8,7},{9,8},{10,9... | collective-permute-start | bytes 24584 | tf_op jit(solution)/shard_map/ppermute | solution.py:444
  17.2 0.0 collective-permute-done.up_ref
  17.2 0.0 collective-permute-done.1.down_ref
  17.2 1.1 %collective-permute-done.2.right_ref = f32[16,128]{1,0:T(8,128)S(1)} collective-permute-done((f32[16,128]{1,0:T(8,128)S(1)}, f32[16,128]{1,0:T(8,128)S(1)}, u32[]{:S(2)}, u32[]{:S(2)}) %collective-permute-start.2) | collective-permute-done | bytes 8224 | tf_op jit(solution)/shard_map/ppermute | solution.py:444
  18.3 0.6 collective-permute-done.3.left_ref
  18.9 0.0 collective-permute-done.4.taken_ref
  18.9 5.9 %shard_map.139 = (f32[64,256]{1,0:T(8,128)S(1)}, f32[16,128]{1,0:T(8,128)S(1)}, f32[16,128]{1,0:T(8,128)S(1)}, f32[16,128]{1,0:T(8,128)S(1)}, f32[16,128]{1,0:T(8,128)S(1)}, /*index=5*/f32[768,128]{1,0:T(8,128)S(1)}) custom-call(s32[1]{0:T(128)S(6)} %copy.17.count_ref, f32[64,256]{1,0:T(8,128)} %features_ref.3, f32[16,128]{1,0:T(8,128)S(1)} %collective-permute-done.up_ref, ...), custom_call_target="tpu_custom_call" | custom-call | flops 10000000000 | bytes 30000000 | tf_op jit(solution)/shard_map/pallas_call | solution.py:497
  24.8 24.9 %all_to_all.10 = f32[128,1,768]{2,1,0:T(1,128)S(1)} all-to-all(f32[128,1,768]{2,1,0:T(1,128)S(1)} %bitcast.8), channel_id=1, replica_groups=mesh['chip'=4,'core'=2,'brick'=32] {'chip','brick'}, dimensions={0} | all-to-all | bytes 786432 | tf_op jit(solution)/shard_map/all_to_all | solution.py:456
  49.7 0.8 shard_map.140
  50.5 6.9 %all-to-all-start.1 = ((f32[128,1,768]{2,1,0:T(1,128)}), f32[128,1,768]{2,1,0:T(1,128)S(1)}, u32[]{:S(2)}, u32[]{:S(2)}) async-start(f32[128,1,768]{2,1,0:T(1,128)} %bitcast.3), calls=%async_computation.1 | async-start | bytes 786432 | tf_op jit(solution)/shard_map/all_to_all | solution.py:456
  57.4 4.6 %collective-permute-start.5 = (f32[16,128]{1,0:T(8,128)S(1)}, f32[16,128]{1,0:T(8,128)S(1)}, u32[]{:S(2)}, u32[]{:S(2)}) collective-permute-start(f32[16,128]{1,0:T(8,128)S(1)} %get-tuple-element.36), channel_id=1, source_target_pairs={{0,1},{1,2},{2,3},{3,4},{4,5},{5,6},{6,7},{7,8},{8,9},{9,10},{10,1... | collective-permute-start | bytes 24584 | tf_op jit(solution)/shard_map/ppermute | solution.py:444
  61.9 5.1 %collective-permute-start.6 = (f32[16,128]{1,0:T(8,128)S(1)}, f32[16,128]{1,0:T(8,128)S(1)}, u32[]{:S(2)}, u32[]{:S(2)}) collective-permute-start(f32[16,128]{1,0:T(8,128)S(1)} %get-tuple-element.37), channel_id=1, source_target_pairs={{0,31},{1,0},{2,1},{3,2},{4,3},{5,4},{6,5},{7,6},{8,7},{9,8},{10,9... | collective-permute-start | bytes 24584 | tf_op jit(solution)/shard_map/ppermute | solution.py:444
  67.0 6.9 %collective-permute-start.7 = (f32[16,128]{1,0:T(8,128)S(1)}, f32[16,128]{1,0:T(8,128)S(1)}, u32[]{:S(2)}, u32[]{:S(2)}) collective-permute-start(f32[16,128]{1,0:T(8,128)S(1)} %get-tuple-element.38), channel_id=1, source_target_pairs={{0,32},{32,64},{64,96},{96,128},{128,160},{160,192},{192,224},{224... | collective-permute-start | bytes 24584 | tf_op jit(solution)/shard_map/ppermute | solution.py:444
  74.0 0.0 collective-permute-start.8
  74.0 1.2 %shard_map.142 = (bf16[1408,256]{1,0:T(8,128)(2,1)S(1)}, bf16[1408,256]{1,0:T(8,128)(2,1)S(1)}) custom-call(f32[3,256]{1,0:T(4,128)} %positions_ref.3), custom_call_target="tpu_custom_call" | custom-call | flops 2000000000 | bytes 6000000 | tf_op jit(solution)/shard_map/pallas_call | solution.py:551
  75.2 0.0 collective-permute-done.5.left_ref
  75.2 0.0 collective-permute-done.6.right_ref
  75.2 0.0 collective-permute-done.7.down_ref
  75.2 2.1 %collective-permute-done.8.up_ref = f32[16,128]{1,0:T(8,128)S(1)} collective-permute-done((f32[16,128]{1,0:T(8,128)S(1)}, f32[16,128]{1,0:T(8,128)S(1)}, u32[]{:S(2)}, u32[]{:S(2)}) %collective-permute-start.8) | collective-permute-done | bytes 8224 | tf_op jit(solution)/shard_map/ppermute | solution.py:444
  77.3 1.3 %shard_map.141.partial_ref = f32[64,256]{1,0:T(8,128)S(1)} custom-call(f32[16,128]{1,0:T(8,128)S(1)} %collective-permute-done.5.left_ref, f32[16,128]{1,0:T(8,128)S(1)} %collective-permute-done.6.right_ref, f32[16,128]{1,0:T(8,128)S(1)} %collective-permute-done.7.down_ref, f32[16,128]{1,0:T(8,128)S(1)} %collective-permute-done.8.up_ref, ...), custom_call_target="tpu_custom_call" | custom-call | flops 2000000000 | bytes 6000000 | tf_op jit(solution)/shard_map/pallas_call | solution.py:544
  78.7 0.0 all-to-all-done.1
  78.7 0.8 collective-permute-start.9
  79.5 0.4 shard_map.143
  79.9 0.9 %collective-permute-done.9.other_ref = f32[768,128]{1,0:T(8,128)S(1)} collective-permute-done((f32[768,128]{1,0:T(8,128)S(1)}, f32[768,128]{1,0:T(8,128)S(1)}, u32[]{:S(2)}, u32[]{:S(2)}) %collective-permute-start.9) | collective-permute-done | bytes 393248 | tf_op jit(solution)/shard_map/ppermute | solution.py:452
  80.8 2.0 %shard_map.144 = (f32[64,64]{1,0:T(8,128)}, f32[64,256]{1,0:T(8,128)}, f32[64,64]{1,0:T(8,128)}, f32[8,64]{1,0:T(8,128)}) custom-call(s32[1]{0:T(128)S(6)} %copy.17.count_ref, f32[768,128]{1,0:T(8,128)S(1)} %collective-permute-done.9.other_ref, bf16[1408,256]{1,0:T(8,128)(2,1)S(1)} %get-tuple-element.44.high_ref, ...), custom_call_target="tpu_custom_call" | custom-call | flops 3000000000 | bytes 9000000 | tf_op jit(solution)/shard_map/pallas_call | solution.py:568
Async XLA Ops:
  3.3 15.6 %collective-permute-start.4 = (f32[704,128]{1,0:T(8,128)S(1)}, f32[704,128]{1,0:T(8,128)S(1)}, u32[]{:S(2)}, u32[]{:S(2)}) collective-permute-start(f32[704,128]{1,0:T(8,128)S(1)} %get-tuple-element.34), channel_id=1, source_target_pairs={{0,32},{32,0},{1,33},{33,1},{2,34},{34,2},{3,35},{35,3},{4,36},{36... | collective-permute-start | bytes 1081352 | tf_op jit(solution)/shard_map/ppermute | solution.py:452
  6.6 10.5 %collective-permute-start = (f32[16,128]{1,0:T(8,128)S(1)}, f32[16,128]{1,0:T(8,128)S(1)}, u32[]{:S(2)}, u32[]{:S(2)}) collective-permute-start(f32[16,128]{1,0:T(8,128)S(1)} %get-tuple-element.29), channel_id=1, source_target_pairs={{0,32},{32,64},{64,96},{96,128},{128,160},{160,192},{192,224},{224... | collective-permute-start | bytes 24584 | tf_op jit(solution)/shard_map/ppermute | solution.py:444
  6.6 10.5 %collective-permute-start.1 = (f32[16,128]{1,0:T(8,128)S(1)}, f32[16,128]{1,0:T(8,128)S(1)}, u32[]{:S(2)}, u32[]{:S(2)}) collective-permute-start(f32[16,128]{1,0:T(8,128)S(1)} %get-tuple-element.30), channel_id=1, source_target_pairs={{0,224},{32,0},{64,32},{96,64},{128,96},{160,128},{192,160},{224,1... | collective-permute-start | bytes 24584 | tf_op jit(solution)/shard_map/ppermute | solution.py:444
  7.2 11.1 %collective-permute-start.2 = (f32[16,128]{1,0:T(8,128)S(1)}, f32[16,128]{1,0:T(8,128)S(1)}, u32[]{:S(2)}, u32[]{:S(2)}) collective-permute-start(f32[16,128]{1,0:T(8,128)S(1)} %get-tuple-element.31), channel_id=1, source_target_pairs={{0,1},{1,2},{2,3},{3,4},{4,5},{5,6},{6,7},{7,8},{8,9},{9,10},{10,1... | collective-permute-start | bytes 24584 | tf_op jit(solution)/shard_map/ppermute | solution.py:444
  12.5 6.4 %collective-permute-start.3 = (f32[16,128]{1,0:T(8,128)S(1)}, f32[16,128]{1,0:T(8,128)S(1)}, u32[]{:S(2)}, u32[]{:S(2)}) collective-permute-start(f32[16,128]{1,0:T(8,128)S(1)} %get-tuple-element.32), channel_id=1, source_target_pairs={{0,31},{1,0},{2,1},{3,2},{4,3},{5,4},{6,5},{7,6},{8,7},{9,8},{10,9... | collective-permute-start | bytes 24584 | tf_op jit(solution)/shard_map/ppermute | solution.py:444
  50.5 28.2 %all-to-all-start.1 = ((f32[128,1,768]{2,1,0:T(1,128)}), f32[128,1,768]{2,1,0:T(1,128)S(1)}, u32[]{:S(2)}, u32[]{:S(2)}) async-start(f32[128,1,768]{2,1,0:T(1,128)} %bitcast.3), calls=%async_computation.1 | async-start | bytes 786432 | tf_op jit(solution)/shard_map/all_to_all | solution.py:456
  57.4 17.8 %collective-permute-start.5 = (f32[16,128]{1,0:T(8,128)S(1)}, f32[16,128]{1,0:T(8,128)S(1)}, u32[]{:S(2)}, u32[]{:S(2)}) collective-permute-start(f32[16,128]{1,0:T(8,128)S(1)} %get-tuple-element.36), channel_id=1, source_target_pairs={{0,1},{1,2},{2,3},{3,4},{4,5},{5,6},{6,7},{7,8},{8,9},{9,10},{10,1... | collective-permute-start | bytes 24584 | tf_op jit(solution)/shard_map/ppermute | solution.py:444
  61.9 13.3 %collective-permute-start.6 = (f32[16,128]{1,0:T(8,128)S(1)}, f32[16,128]{1,0:T(8,128)S(1)}, u32[]{:S(2)}, u32[]{:S(2)}) collective-permute-start(f32[16,128]{1,0:T(8,128)S(1)} %get-tuple-element.37), channel_id=1, source_target_pairs={{0,31},{1,0},{2,1},{3,2},{4,3},{5,4},{6,5},{7,6},{8,7},{9,8},{10,9... | collective-permute-start | bytes 24584 | tf_op jit(solution)/shard_map/ppermute | solution.py:444
  67.0 8.2 %collective-permute-start.7 = (f32[16,128]{1,0:T(8,128)S(1)}, f32[16,128]{1,0:T(8,128)S(1)}, u32[]{:S(2)}, u32[]{:S(2)}) collective-permute-start(f32[16,128]{1,0:T(8,128)S(1)} %get-tuple-element.38), channel_id=1, source_target_pairs={{0,32},{32,64},{64,96},{96,128},{128,160},{160,192},{192,224},{224... | collective-permute-start | bytes 24584 | tf_op jit(solution)/shard_map/ppermute | solution.py:444
  74.0 3.4 %collective-permute-start.8 = (f32[16,128]{1,0:T(8,128)S(1)}, f32[16,128]{1,0:T(8,128)S(1)}, u32[]{:S(2)}, u32[]{:S(2)}) collective-permute-start(f32[16,128]{1,0:T(8,128)S(1)} %get-tuple-element.39), channel_id=1, source_target_pairs={{0,224},{32,0},{64,32},{96,64},{128,96},{160,128},{192,160},{224,1... | collective-permute-start | bytes 24584 | tf_op jit(solution)/shard_map/ppermute | solution.py:444
  78.7 2.1 %collective-permute-start.9 = (f32[768,128]{1,0:T(8,128)S(1)}, f32[768,128]{1,0:T(8,128)S(1)}, u32[]{:S(2)}, u32[]{:S(2)}) collective-permute-start(f32[768,128]{1,0:T(8,128)S(1)} %bitcast.6), channel_id=1, source_target_pairs={{0,32},{32,0},{1,33},{33,1},{2,34},{34,2},{3,35},{35,3},{4,36},{36... | collective-permute-start | bytes 1179656 | tf_op jit(solution)/shard_map/ppermute | solution.py:452

commit v9 on v8

--- a/solution.py
+++ b/solution.py
@@ -18,7 +18,6 @@
 CHUNKS = 11
 F32 = jnp.float32
 BF16 = jnp.bfloat16
-FULL_PRECISION = lax.Precision.HIGHEST
 SLAB = ("chip", "core")
 CHIPS = ("chip", "brick")
 ALL = ("chip", "core", "brick")
@@ -65,8 +64,10 @@
 
 
 def dot_full(left, right, contract=((1,), (0,))):
-    return lax.dot_general(
-        left, right, (contract, ((), ())), precision=FULL_PRECISION, preferred_element_type=F32
+    left_high, left_low = split(left)
+    right_high, right_low = split(right)
+    return dot(left_high, right_high, contract) + (
+        dot(left_high, right_low, contract) + dot(left_low, right_high, contract)
     )
 
 
@@ -493,7 +494,17 @@
     taken = swapped(give)
 
     up, down, right, left = (close(x) for x in (up, down, right, left))
-    keep, taken = close(keep), close(taken)
+    taken = close(taken)
+    table = jax.ShapeDtypeStruct((2 * half, atoms), BF16)
+    high, low = pl.pallas_call(
+        table_kernel,
+        out_shape=(table, table),
+        in_specs=vmem(1),
+        out_specs=tuple(vmem(2)),
+        cost_estimate=work(2.0),
+    )(positions)
+    keep, high, low = lax.optimization_barrier((keep, high, low))
+    keep = close(keep)
     own, *ghost, payload = pl.pallas_call(
         functools.partial(edge_kernel, factor=factor),
         out_shape=(near(channels, atoms),) + (message,) * 4 + (near(rows, 128),),
@@ -548,14 +559,7 @@
         out_specs=vmem(1)[0],
         cost_estimate=work(2.0),
     )(back_right, back_left, back_up, back_down, close(own), send_map, short_weight)
-    high, low = pl.pallas_call(
-        table_kernel,
-        out_shape=(pltpu.VMEM((2 * half, atoms), BF16), pltpu.VMEM((2 * half, atoms), BF16)),
-        in_specs=vmem(1),
-        out_specs=tuple(vmem(2)),
-        cost_estimate=work(2.0),
-    )(positions)
-    mine, partial, high, low = lax.optimization_barrier((mine, partial, high, low))
+    mine, partial = lax.optimization_barrier((mine, partial))
     high, low = close(high), close(low)
     other = close(swapped(mine))
     field, sums, small = pl.pallas_call(

time: 83.3 us -> 83.1 us (level)
  Pallas kernels: 13.7 us -> 14.7 us
    pallas_call x1, Pallas kernels: 1.22 us -> 2.32 us  [on_device(): pl.pallas_call(table_kernel, out_shape=(table, table), in_specs=vmem(1),...]
  transfers between devices with their start and end apart: 11 -> 11, of which waited for: 4 -> 3; matrix products, arithmetic and copies ran while one was open for 0% -> 0% of each run, Pallas kernels for 4% -> 5%
where the time goes in v9:
time: 83.1 us; the launch traced here: 82.7 us
  starting transfers between devices  38.1 us (46%)
  blocking collectives  24.2 us (29%)
  Pallas kernels  14.7 us (18%)
  waiting for transfers between devices  4.3 us (5%)
  between operations  1.36 us (2%)
    ppermute x8, starting transfers between devices, shifted(): lax.ppermute(value, axis, [(i, (i + step) % size) for i in range(size)])  27.2 us
    all_to_all x1, blocking collectives, exchange(): return lax.all_to_all(value, axes, 0, 0, tiled=True)  24.2 us
    all_to_all x1, starting transfers between devices, exchange(): return lax.all_to_all(value, axes, 0, 0, tiled=True)  6.85 us
    pallas_call x1, Pallas kernels, on_device(): pl.pallas_call(functools.partial(edge_kernel, factor=factor), out_shape=(...  5.8 us
    ppermute x2, starting transfers between devices, swapped(): return lax.ppermute(value, 'core', [(0, 1), (1, 0)])  4.12 us
    ppermute x8, waiting for transfers between devices, shifted(): lax.ppermute(value, axis, [(i, (i + step) % size) for i in range(size)])  3.37 us
    pallas_call x1, Pallas kernels, on_device(): pl.pallas_call(table_kernel, out_shape=(table, table), in_specs=vmem(1),...  2.32 us
    pallas_call x1, Pallas kernels, on_device(): pl.pallas_call(wave_kernel, out_shape=(near(half, 128), near(half, 128))...  2.02 us
  transfers between devices with their start and end apart: 11, of which 3 were waited for; matrix products, arithmetic and copies ran while one was open for 0% of the time, Pallas kernels for 5%

profile of v9, /device:TPU:1, one launch (start us, length us, event | category | flops | bytes accessed | tf_op | source)
XLA Modules:
  0.0 82.7 jit_solution(722018364202870429)
XLA Ops:
  1.3 2.0 %shard_map.138 = (f32[704,128]{1,0:T(8,128)S(1)}, f32[704,128]{1,0:T(8,128)S(1)}, f32[16,128]{1,0:T(8,128)S(1)}, f32[16,128]{1,0:T(8,128)S(1)}, f32[16,128]{1,0:T(8,128)S(1)}, /*index=5*/f32[16,128]{1,0:T(8,128)S(1)}) custom-call(s32[1]{0:T(128)S(6)} %copy.17.count_ref, f32[3,256]{1,0:T(4,128)} %positions_ref.3, f32[64,256]{1,0:T(8,128)} %cotangent_ref.3, ...), custom_call_target="tpu_custom_call" | custom-call | flops 4000000000 | bytes 12000000 | tf_op jit(solution)/shard_map/pallas_call | solution.py:482
  3.3 3.3 %collective-permute-start.4 = (f32[704,128]{1,0:T(8,128)S(1)}, f32[704,128]{1,0:T(8,128)S(1)}, u32[]{:S(2)}, u32[]{:S(2)}) collective-permute-start(f32[704,128]{1,0:T(8,128)S(1)} %get-tuple-element.38), channel_id=1, source_target_pairs={{0,32},{32,0},{1,33},{33,1},{2,34},{34,2},{3,35},{35,3},{4,36},{36... | collective-permute-start | bytes 1081352 | tf_op jit(solution)/shard_map/ppermute | solution.py:453
  6.6 0.0 collective-permute-start
  6.6 0.5 collective-permute-start.1
  7.1 5.4 %collective-permute-start.2 = (f32[16,128]{1,0:T(8,128)S(1)}, f32[16,128]{1,0:T(8,128)S(1)}, u32[]{:S(2)}, u32[]{:S(2)}) collective-permute-start(f32[16,128]{1,0:T(8,128)S(1)} %get-tuple-element.32), channel_id=1, source_target_pairs={{0,1},{1,2},{2,3},{3,4},{4,5},{5,6},{6,7},{7,8},{8,9},{9,10},{10,1... | collective-permute-start | bytes 24584 | tf_op jit(solution)/shard_map/ppermute | solution.py:445
  12.5 4.6 %collective-permute-start.3 = (f32[16,128]{1,0:T(8,128)S(1)}, f32[16,128]{1,0:T(8,128)S(1)}, u32[]{:S(2)}, u32[]{:S(2)}) collective-permute-start(f32[16,128]{1,0:T(8,128)S(1)} %get-tuple-element.33), channel_id=1, source_target_pairs={{0,31},{1,0},{2,1},{3,2},{4,3},{5,4},{6,5},{7,6},{8,7},{9,8},{10,9... | collective-permute-start | bytes 24584 | tf_op jit(solution)/shard_map/ppermute | solution.py:445
  17.2 2.3 %shard_map.139 = (bf16[1408,256]{1,0:T(8,128)(2,1)}, bf16[1408,256]{1,0:T(8,128)(2,1)}) custom-call(f32[3,256]{1,0:T(4,128)} %positions_ref.3), custom_call_target="tpu_custom_call" | custom-call | flops 2000000000 | bytes 6000000 | tf_op jit(solution)/shard_map/pallas_call | solution.py:499
  19.5 0.0 collective-permute-done.up_ref
  19.5 0.0 collective-permute-done.1.down_ref
  19.5 0.0 collective-permute-done.2.right_ref
  19.5 0.0 collective-permute-done.3.left_ref
  19.5 0.0 collective-permute-done.4.taken_ref
  19.5 5.8 %shard_map.140 = (f32[64,256]{1,0:T(8,128)S(1)}, f32[16,128]{1,0:T(8,128)S(1)}, f32[16,128]{1,0:T(8,128)S(1)}, f32[16,128]{1,0:T(8,128)S(1)}, f32[16,128]{1,0:T(8,128)S(1)}, /*index=5*/f32[768,128]{1,0:T(8,128)S(1)}) custom-call(s32[1]{0:T(128)S(6)} %copy.17.count_ref, f32[64,256]{1,0:T(8,128)} %features_ref.3, f32[16,128]{1,0:T(8,128)S(1)} %collective-permute-done.up_ref, ...), custom_call_target="tpu_custom_call" | custom-call | flops 10000000000 | bytes 30000000 | tf_op jit(solution)/shard_map/pallas_call | solution.py:508
  25.3 24.2 %all_to_all.10 = f32[128,1,768]{2,1,0:T(1,128)S(1)} all-to-all(f32[128,1,768]{2,1,0:T(1,128)S(1)} %bitcast.8), channel_id=1, replica_groups=mesh['chip'=4,'core'=2,'brick'=32] {'chip','brick'}, dimensions={0} | all-to-all | bytes 786432 | tf_op jit(solution)/shard_map/all_to_all | solution.py:457
  49.6 0.8 shard_map.141
  50.4 6.9 %all-to-all-start.1 = ((f32[128,1,768]{2,1,0:T(1,128)}), f32[128,1,768]{2,1,0:T(1,128)S(1)}, u32[]{:S(2)}, u32[]{:S(2)}) async-start(f32[128,1,768]{2,1,0:T(1,128)} %bitcast.3), calls=%async_computation.1 | async-start | bytes 786432 | tf_op jit(solution)/shard_map/all_to_all | solution.py:457
  57.2 4.6 %collective-permute-start.5 = (f32[16,128]{1,0:T(8,128)S(1)}, f32[16,128]{1,0:T(8,128)S(1)}, u32[]{:S(2)}, u32[]{:S(2)}) collective-permute-start(f32[16,128]{1,0:T(8,128)S(1)} %get-tuple-element.40), channel_id=1, source_target_pairs={{0,1},{1,2},{2,3},{3,4},{4,5},{5,6},{6,7},{7,8},{8,9},{9,10},{10,1... | collective-permute-start | bytes 24584 | tf_op jit(solution)/shard_map/ppermute | solution.py:445
  61.8 5.1 %collective-permute-start.6 = (f32[16,128]{1,0:T(8,128)S(1)}, f32[16,128]{1,0:T(8,128)S(1)}, u32[]{:S(2)}, u32[]{:S(2)}) collective-permute-start(f32[16,128]{1,0:T(8,128)S(1)} %get-tuple-element.41), channel_id=1, source_target_pairs={{0,31},{1,0},{2,1},{3,2},{4,3},{5,4},{6,5},{7,6},{8,7},{9,8},{10,9... | collective-permute-start | bytes 24584 | tf_op jit(solution)/shard_map/ppermute | solution.py:445
  66.9 6.9 %collective-permute-start.7 = (f32[16,128]{1,0:T(8,128)S(1)}, f32[16,128]{1,0:T(8,128)S(1)}, u32[]{:S(2)}, u32[]{:S(2)}) collective-permute-start(f32[16,128]{1,0:T(8,128)S(1)} %get-tuple-element.42), channel_id=1, source_target_pairs={{0,32},{32,64},{64,96},{96,128},{128,160},{160,192},{192,224},{224... | collective-permute-start | bytes 24584 | tf_op jit(solution)/shard_map/ppermute | solution.py:445
  73.8 0.0 collective-permute-start.8
  73.9 0.0 collective-permute-done.5.left_ref
  73.9 0.0 collective-permute-done.6.right_ref
  73.9 0.8 collective-permute-done.7.down_ref
  74.6 2.6 %collective-permute-done.8.up_ref = f32[16,128]{1,0:T(8,128)S(1)} collective-permute-done((f32[16,128]{1,0:T(8,128)S(1)}, f32[16,128]{1,0:T(8,128)S(1)}, u32[]{:S(2)}, u32[]{:S(2)}) %collective-permute-start.8) | collective-permute-done | bytes 8224 | tf_op jit(solution)/shard_map/ppermute | solution.py:445
  77.2 0.0 copy-start
  77.2 0.0 copy-start.1
  77.2 1.4 %shard_map.142.partial_ref = f32[64,256]{1,0:T(8,128)S(1)} custom-call(f32[16,128]{1,0:T(8,128)S(1)} %collective-permute-done.5.left_ref, f32[16,128]{1,0:T(8,128)S(1)} %collective-permute-done.6.right_ref, f32[16,128]{1,0:T(8,128)S(1)} %collective-permute-done.7.down_ref, f32[16,128]{1,0:T(8,128)S(1)} %collective-permute-done.8.up_ref, ...), custom_call_target="tpu_custom_call" | custom-call | flops 2000000000 | bytes 6000000 | tf_op jit(solution)/shard_map/pallas_call | solution.py:555
  78.6 0.0 all-to-all-done.1
  78.6 0.8 collective-permute-start.9
  79.4 0.0 copy-done
  79.4 0.0 copy-done.1
  79.4 0.4 shard_map.143
  79.9 0.9 %collective-permute-done.9.other_ref = f32[768,128]{1,0:T(8,128)S(1)} collective-permute-done((f32[768,128]{1,0:T(8,128)S(1)}, f32[768,128]{1,0:T(8,128)S(1)}, u32[]{:S(2)}, u32[]{:S(2)}) %collective-permute-start.9) | collective-permute-done | bytes 393248 | tf_op jit(solution)/shard_map/ppermute | solution.py:453
  80.8 2.0 %shard_map.144 = (f32[64,64]{1,0:T(8,128)}, f32[64,256]{1,0:T(8,128)}, f32[64,64]{1,0:T(8,128)}, f32[8,64]{1,0:T(8,128)}) custom-call(s32[1]{0:T(128)S(6)} %copy.17.count_ref, f32[768,128]{1,0:T(8,128)S(1)} %collective-permute-done.9.other_ref, bf16[1408,256]{1,0:T(8,128)(2,1)S(1)} %copy-done, bf16[1408,256]{1,0:T(8,128)(2,1)S(1)} %copy-done.1, ...), custom_call_target="tpu_custom_call" | custom-call | flops 3000000000 | bytes 9000000 | tf_op jit(solution)/shard_map/pallas_call | solution.py:572
Async XLA Ops:
  3.3 16.2 %collective-permute-start.4 = (f32[704,128]{1,0:T(8,128)S(1)}, f32[704,128]{1,0:T(8,128)S(1)}, u32[]{:S(2)}, u32[]{:S(2)}) collective-permute-start(f32[704,128]{1,0:T(8,128)S(1)} %get-tuple-element.38), channel_id=1, source_target_pairs={{0,32},{32,0},{1,33},{33,1},{2,34},{34,2},{3,35},{35,3},{4,36},{36... | collective-permute-start | bytes 1081352 | tf_op jit(solution)/shard_map/ppermute | solution.py:453
  6.6 12.9 %collective-permute-start = (f32[16,128]{1,0:T(8,128)S(1)}, f32[16,128]{1,0:T(8,128)S(1)}, u32[]{:S(2)}, u32[]{:S(2)}) collective-permute-start(f32[16,128]{1,0:T(8,128)S(1)} %get-tuple-element.30), channel_id=1, source_target_pairs={{0,32},{32,64},{64,96},{96,128},{128,160},{160,192},{192,224},{224... | collective-permute-start | bytes 24584 | tf_op jit(solution)/shard_map/ppermute | solution.py:445
  6.6 12.9 %collective-permute-start.1 = (f32[16,128]{1,0:T(8,128)S(1)}, f32[16,128]{1,0:T(8,128)S(1)}, u32[]{:S(2)}, u32[]{:S(2)}) collective-permute-start(f32[16,128]{1,0:T(8,128)S(1)} %get-tuple-element.31), channel_id=1, source_target_pairs={{0,224},{32,0},{64,32},{96,64},{128,96},{160,128},{192,160},{224,1... | collective-permute-start | bytes 24584 | tf_op jit(solution)/shard_map/ppermute | solution.py:445
  7.1 12.4 %collective-permute-start.2 = (f32[16,128]{1,0:T(8,128)S(1)}, f32[16,128]{1,0:T(8,128)S(1)}, u32[]{:S(2)}, u32[]{:S(2)}) collective-permute-start(f32[16,128]{1,0:T(8,128)S(1)} %get-tuple-element.32), channel_id=1, source_target_pairs={{0,1},{1,2},{2,3},{3,4},{4,5},{5,6},{6,7},{7,8},{8,9},{9,10},{10,1... | collective-permute-start | bytes 24584 | tf_op jit(solution)/shard_map/ppermute | solution.py:445
  12.5 7.0 %collective-permute-start.3 = (f32[16,128]{1,0:T(8,128)S(1)}, f32[16,128]{1,0:T(8,128)S(1)}, u32[]{:S(2)}, u32[]{:S(2)}) collective-permute-start(f32[16,128]{1,0:T(8,128)S(1)} %get-tuple-element.33), channel_id=1, source_target_pairs={{0,31},{1,0},{2,1},{3,2},{4,3},{5,4},{6,5},{7,6},{8,7},{9,8},{10,9... | collective-permute-start | bytes 24584 | tf_op jit(solution)/shard_map/ppermute | solution.py:445
  50.4 28.2 %all-to-all-start.1 = ((f32[128,1,768]{2,1,0:T(1,128)}), f32[128,1,768]{2,1,0:T(1,128)S(1)}, u32[]{:S(2)}, u32[]{:S(2)}) async-start(f32[128,1,768]{2,1,0:T(1,128)} %bitcast.3), calls=%async_computation.1 | async-start | bytes 786432 | tf_op jit(solution)/shard_map/all_to_all | solution.py:457
  57.2 16.6 %collective-permute-start.5 = (f32[16,128]{1,0:T(8,128)S(1)}, f32[16,128]{1,0:T(8,128)S(1)}, u32[]{:S(2)}, u32[]{:S(2)}) collective-permute-start(f32[16,128]{1,0:T(8,128)S(1)} %get-tuple-element.40), channel_id=1, source_target_pairs={{0,1},{1,2},{2,3},{3,4},{4,5},{5,6},{6,7},{7,8},{8,9},{9,10},{10,1... | collective-permute-start | bytes 24584 | tf_op jit(solution)/shard_map/ppermute | solution.py:445
  61.8 12.1 %collective-permute-start.6 = (f32[16,128]{1,0:T(8,128)S(1)}, f32[16,128]{1,0:T(8,128)S(1)}, u32[]{:S(2)}, u32[]{:S(2)}) collective-permute-start(f32[16,128]{1,0:T(8,128)S(1)} %get-tuple-element.41), channel_id=1, source_target_pairs={{0,31},{1,0},{2,1},{3,2},{4,3},{5,4},{6,5},{7,6},{8,7},{9,8},{10,9... | collective-permute-start | bytes 24584 | tf_op jit(solution)/shard_map/ppermute | solution.py:445
  66.9 7.7 %collective-permute-start.7 = (f32[16,128]{1,0:T(8,128)S(1)}, f32[16,128]{1,0:T(8,128)S(1)}, u32[]{:S(2)}, u32[]{:S(2)}) collective-permute-start(f32[16,128]{1,0:T(8,128)S(1)} %get-tuple-element.42), channel_id=1, source_target_pairs={{0,32},{32,64},{64,96},{96,128},{128,160},{160,192},{192,224},{224... | collective-permute-start | bytes 24584 | tf_op jit(solution)/shard_map/ppermute | solution.py:445
  73.8 3.4 %collective-permute-start.8 = (f32[16,128]{1,0:T(8,128)S(1)}, f32[16,128]{1,0:T(8,128)S(1)}, u32[]{:S(2)}, u32[]{:S(2)}) collective-permute-start(f32[16,128]{1,0:T(8,128)S(1)} %get-tuple-element.43), channel_id=1, source_target_pairs={{0,224},{32,0},{64,32},{96,64},{128,96},{160,128},{192,160},{224,1... | collective-permute-start | bytes 24584 | tf_op jit(solution)/shard_map/ppermute | solution.py:445
  77.2 2.2 %copy-start = (bf16[1408,256]{1,0:T(8,128)(2,1)S(1)}, bf16[1408,256]{1,0:T(8,128)(2,1)}, u32[]{:S(2)}) copy-start(bf16[1408,256]{1,0:T(8,128)(2,1)} %get-tuple-element.46.high_ref) | copy-start | bytes 2162692
  77.2 2.2 %copy-start.1 = (bf16[1408,256]{1,0:T(8,128)(2,1)S(1)}, bf16[1408,256]{1,0:T(8,128)(2,1)}, u32[]{:S(2)}) copy-start(bf16[1408,256]{1,0:T(8,128)(2,1)} %get-tuple-element.47.low_ref) | copy-start | bytes 2162692
  78.6 2.1 %collective-permute-start.9 = (f32[768,128]{1,0:T(8,128)S(1)}, f32[768,128]{1,0:T(8,128)S(1)}, u32[]{:S(2)}, u32[]{:S(2)}) collective-permute-start(f32[768,128]{1,0:T(8,128)S(1)} %bitcast.6), channel_id=1, source_target_pairs={{0,32},{32,0},{1,33},{33,1},{2,34},{34,2},{3,35},{35,3},{4,36},{36... | collective-permute-start | bytes 1179656 | tf_op jit(solution)/shard_map/ppermute | solution.py:453

commit v10 on v9

--- a/solution.py
+++ b/solution.py
@@ -239,7 +239,7 @@
     channels, atoms = features_ref.shape
     slots = length_ref.shape[0]
     columns = atoms + 128
-    group = 4
+    group = 8
     wide = group * atoms
     waves = keep_ref.shape[0]
     payload_ref[:waves, :] = keep_ref[...] + taken_ref[...]
@@ -304,7 +304,7 @@
 
     turns = slots // group
     short_sum = lax.fori_loop(
-        0, turns, forward, jnp.zeros((channels, atoms), F32), unroll=8
+        0, turns, forward, jnp.zeros((channels, atoms), F32), unroll=4
     )
     gate = jax.nn.sigmoid(short_sum)
     upstream = cotangent_ref[...] * gate * (1.0 + short_sum * (1.0 - gate)) * live
@@ -324,7 +324,7 @@
         return radial + dot(pair, side_by_side(pulls), ((1,), (1,)))
 
     radial = lax.fori_loop(
-        0, turns, backward, jnp.zeros((16, 2 * channels), F32), unroll=8
+        0, turns, backward, jnp.zeros((16, 2 * channels), F32), unroll=4
     ).T
     grads = grads_ref[...].T
     grads = grads[:channels] + grads[channels:]
@@ -512,9 +512,9 @@
         out_specs=tuple(vmem(6)),
         scratch_shapes=[
             pltpu.VMEM((slots * 8, atoms), F32),
-            pltpu.VMEM((slots // 4, atoms + 128, 4 * atoms), BF16),
-            pltpu.VMEM((slots // 4, channels, 4 * atoms), F32),
-            pltpu.VMEM((slots // 4, channels, 4 * atoms), F32),
+            pltpu.VMEM((slots // 8, atoms + 128, 8 * atoms), BF16),
+            pltpu.VMEM((slots // 8, channels, 8 * atoms), F32),
+            pltpu.VMEM((slots // 8, channels, 8 * atoms), F32),
             pltpu.VMEM((atoms + 128, 2 * channels), F32),
             pltpu.VMEM((channels, atoms), F32),
             pltpu.VMEM((slots, atoms), F32),

time: 83.1 us -> 83 us (level)
  no operation moved by 1% of the time
where the time goes in v10:
time: 83 us; the launch traced here: 82.7 us
  starting transfers between devices  38.1 us (46%)
  blocking collectives  24.2 us (29%)
  Pallas kernels  14.6 us (18%)
  waiting for transfers between devices  4.3 us (5%)
  between operations  1.36 us (2%)
    ppermute x8, starting transfers between devices, shifted(): lax.ppermute(value, axis, [(i, (i + step) % size) for i in range(size)])  27.1 us
    all_to_all x1, blocking collectives, exchange(): return lax.all_to_all(value, axes, 0, 0, tiled=True)  24.2 us
    all_to_all x1, starting transfers between devices, exchange(): return lax.all_to_all(value, axes, 0, 0, tiled=True)  6.85 us
    pallas_call x1, Pallas kernels, on_device(): pl.pallas_call(functools.partial(edge_kernel, factor=factor), out_shape=(...  5.7 us
    ppermute x2, starting transfers between devices, swapped(): return lax.ppermute(value, 'core', [(0, 1), (1, 0)])  4.12 us
    ppermute x8, waiting for transfers between devices, shifted(): lax.ppermute(value, axis, [(i, (i + step) % size) for i in range(size)])  3.37 us
    pallas_call x1, Pallas kernels, on_device(): pl.pallas_call(table_kernel, out_shape=(table, table), in_specs=vmem(1),...  2.32 us
    pallas_call x1, Pallas kernels, on_device(): pl.pallas_call(wave_kernel, out_shape=(near(half, 128), near(half, 128))...  2.02 us
  transfers between devices with their start and end apart: 11, of which 3 were waited for; matrix products, arithmetic and copies ran while one was open for 0% of the time, Pallas kernels for 5%

profile of v10, /device:TPU:1, one launch (start us, length us, event | category | flops | bytes accessed | tf_op | source)
XLA Modules:
  0.0 82.7 jit_solution(14871424349551740299)
XLA Ops:
  1.3 2.0 %shard_map.138 = (f32[704,128]{1,0:T(8,128)S(1)}, f32[704,128]{1,0:T(8,128)S(1)}, f32[16,128]{1,0:T(8,128)S(1)}, f32[16,128]{1,0:T(8,128)S(1)}, f32[16,128]{1,0:T(8,128)S(1)}, /*index=5*/f32[16,128]{1,0:T(8,128)S(1)}) custom-call(s32[1]{0:T(128)S(6)} %copy.17.count_ref, f32[3,256]{1,0:T(4,128)} %positions_ref.3, f32[64,256]{1,0:T(8,128)} %cotangent_ref.3, ...), custom_call_target="tpu_custom_call" | custom-call | flops 4000000000 | bytes 12000000 | tf_op jit(solution)/shard_map/pallas_call | solution.py:482
  3.3 3.3 %collective-permute-start.4 = (f32[704,128]{1,0:T(8,128)S(1)}, f32[704,128]{1,0:T(8,128)S(1)}, u32[]{:S(2)}, u32[]{:S(2)}) collective-permute-start(f32[704,128]{1,0:T(8,128)S(1)} %get-tuple-element.38), channel_id=1, source_target_pairs={{0,32},{32,0},{1,33},{33,1},{2,34},{34,2},{3,35},{35,3},{4,36},{36... | collective-permute-start | bytes 1081352 | tf_op jit(solution)/shard_map/ppermute | solution.py:453
  6.6 0.0 collective-permute-start
  6.6 0.5 collective-permute-start.1
  7.1 5.4 %collective-permute-start.2 = (f32[16,128]{1,0:T(8,128)S(1)}, f32[16,128]{1,0:T(8,128)S(1)}, u32[]{:S(2)}, u32[]{:S(2)}) collective-permute-start(f32[16,128]{1,0:T(8,128)S(1)} %get-tuple-element.32), channel_id=1, source_target_pairs={{0,1},{1,2},{2,3},{3,4},{4,5},{5,6},{6,7},{7,8},{8,9},{9,10},{10,1... | collective-permute-start | bytes 24584 | tf_op jit(solution)/shard_map/ppermute | solution.py:445
  12.5 4.6 %collective-permute-start.3 = (f32[16,128]{1,0:T(8,128)S(1)}, f32[16,128]{1,0:T(8,128)S(1)}, u32[]{:S(2)}, u32[]{:S(2)}) collective-permute-start(f32[16,128]{1,0:T(8,128)S(1)} %get-tuple-element.33), channel_id=1, source_target_pairs={{0,31},{1,0},{2,1},{3,2},{4,3},{5,4},{6,5},{7,6},{8,7},{9,8},{10,9... | collective-permute-start | bytes 24584 | tf_op jit(solution)/shard_map/ppermute | solution.py:445
  17.2 2.3 %shard_map.139 = (bf16[1408,256]{1,0:T(8,128)(2,1)}, bf16[1408,256]{1,0:T(8,128)(2,1)}) custom-call(f32[3,256]{1,0:T(4,128)} %positions_ref.3), custom_call_target="tpu_custom_call" | custom-call | flops 2000000000 | bytes 6000000 | tf_op jit(solution)/shard_map/pallas_call | solution.py:499
  19.5 0.0 collective-permute-done.up_ref
  19.5 0.0 collective-permute-done.1.down_ref
  19.5 0.0 collective-permute-done.2.right_ref
  19.5 0.0 collective-permute-done.3.left_ref
  19.5 0.0 collective-permute-done.4.taken_ref
  19.5 5.7 %shard_map.140 = (f32[64,256]{1,0:T(8,128)S(1)}, f32[16,128]{1,0:T(8,128)S(1)}, f32[16,128]{1,0:T(8,128)S(1)}, f32[16,128]{1,0:T(8,128)S(1)}, f32[16,128]{1,0:T(8,128)S(1)}, /*index=5*/f32[768,128]{1,0:T(8,128)S(1)}) custom-call(s32[1]{0:T(128)S(6)} %copy.17.count_ref, f32[64,256]{1,0:T(8,128)} %features_ref.3, f32[16,128]{1,0:T(8,128)S(1)} %collective-permute-done.up_ref, ...), custom_call_target="tpu_custom_call" | custom-call | flops 10000000000 | bytes 30000000 | tf_op jit(solution)/shard_map/pallas_call | solution.py:508
  25.2 24.2 %all_to_all.10 = f32[128,1,768]{2,1,0:T(1,128)S(1)} all-to-all(f32[128,1,768]{2,1,0:T(1,128)S(1)} %bitcast.8), channel_id=1, replica_groups=mesh['chip'=4,'core'=2,'brick'=32] {'chip','brick'}, dimensions={0} | all-to-all | bytes 786432 | tf_op jit(solution)/shard_map/all_to_all | solution.py:457
  49.5 0.8 shard_map.141
  50.3 6.9 %all-to-all-start.1 = ((f32[128,1,768]{2,1,0:T(1,128)}), f32[128,1,768]{2,1,0:T(1,128)S(1)}, u32[]{:S(2)}, u32[]{:S(2)}) async-start(f32[128,1,768]{2,1,0:T(1,128)} %bitcast.3), calls=%async_computation.1 | async-start | bytes 786432 | tf_op jit(solution)/shard_map/all_to_all | solution.py:457
  57.2 4.6 %collective-permute-start.5 = (f32[16,128]{1,0:T(8,128)S(1)}, f32[16,128]{1,0:T(8,128)S(1)}, u32[]{:S(2)}, u32[]{:S(2)}) collective-permute-start(f32[16,128]{1,0:T(8,128)S(1)} %get-tuple-element.40), channel_id=1, source_target_pairs={{0,1},{1,2},{2,3},{3,4},{4,5},{5,6},{6,7},{7,8},{8,9},{9,10},{10,1... | collective-permute-start | bytes 24584 | tf_op jit(solution)/shard_map/ppermute | solution.py:445
  61.7 5.1 %collective-permute-start.6 = (f32[16,128]{1,0:T(8,128)S(1)}, f32[16,128]{1,0:T(8,128)S(1)}, u32[]{:S(2)}, u32[]{:S(2)}) collective-permute-start(f32[16,128]{1,0:T(8,128)S(1)} %get-tuple-element.41), channel_id=1, source_target_pairs={{0,31},{1,0},{2,1},{3,2},{4,3},{5,4},{6,5},{7,6},{8,7},{9,8},{10,9... | collective-permute-start | bytes 24584 | tf_op jit(solution)/shard_map/ppermute | solution.py:445
  66.8 6.9 %collective-permute-start.7 = (f32[16,128]{1,0:T(8,128)S(1)}, f32[16,128]{1,0:T(8,128)S(1)}, u32[]{:S(2)}, u32[]{:S(2)}) collective-permute-start(f32[16,128]{1,0:T(8,128)S(1)} %get-tuple-element.42), channel_id=1, source_target_pairs={{0,32},{32,64},{64,96},{96,128},{128,160},{160,192},{192,224},{224... | collective-permute-start | bytes 24584 | tf_op jit(solution)/shard_map/ppermute | solution.py:445
  73.8 0.0 collective-permute-start.8
  73.8 0.0 collective-permute-done.5.left_ref
  73.8 0.0 collective-permute-done.6.right_ref
  73.8 0.8 collective-permute-done.7.down_ref
  74.5 2.6 %collective-permute-done.8.up_ref = f32[16,128]{1,0:T(8,128)S(1)} collective-permute-done((f32[16,128]{1,0:T(8,128)S(1)}, f32[16,128]{1,0:T(8,128)S(1)}, u32[]{:S(2)}, u32[]{:S(2)}) %collective-permute-start.8) | collective-permute-done | bytes 8224 | tf_op jit(solution)/shard_map/ppermute | solution.py:445
  77.1 0.0 copy-start
  77.1 0.0 copy-start.1
  77.1 1.4 %shard_map.142.partial_ref = f32[64,256]{1,0:T(8,128)S(1)} custom-call(f32[16,128]{1,0:T(8,128)S(1)} %collective-permute-done.5.left_ref, f32[16,128]{1,0:T(8,128)S(1)} %collective-permute-done.6.right_ref, f32[16,128]{1,0:T(8,128)S(1)} %collective-permute-done.7.down_ref, f32[16,128]{1,0:T(8,128)S(1)} %collective-permute-done.8.up_ref, ...), custom_call_target="tpu_custom_call" | custom-call | flops 2000000000 | bytes 6000000 | tf_op jit(solution)/shard_map/pallas_call | solution.py:555
  78.5 0.0 all-to-all-done.1
  78.5 0.8 collective-permute-start.9
  79.3 0.0 copy-done
  79.3 0.0 copy-done.1
  79.3 0.4 shard_map.143
  79.8 0.9 %collective-permute-done.9.other_ref = f32[768,128]{1,0:T(8,128)S(1)} collective-permute-done((f32[768,128]{1,0:T(8,128)S(1)}, f32[768,128]{1,0:T(8,128)S(1)}, u32[]{:S(2)}, u32[]{:S(2)}) %collective-permute-start.9) | collective-permute-done | bytes 393248 | tf_op jit(solution)/shard_map/ppermute | solution.py:453
  80.7 2.0 %shard_map.144 = (f32[64,64]{1,0:T(8,128)}, f32[64,256]{1,0:T(8,128)}, f32[64,64]{1,0:T(8,128)}, f32[8,64]{1,0:T(8,128)}) custom-call(s32[1]{0:T(128)S(6)} %copy.17.count_ref, f32[768,128]{1,0:T(8,128)S(1)} %collective-permute-done.9.other_ref, bf16[1408,256]{1,0:T(8,128)(2,1)S(1)} %copy-done, bf16[1408,256]{1,0:T(8,128)(2,1)S(1)} %copy-done.1, ...), custom_call_target="tpu_custom_call" | custom-call | flops 3000000000 | bytes 9000000 | tf_op jit(solution)/shard_map/pallas_call | solution.py:572
Async XLA Ops:
  3.3 16.2 %collective-permute-start.4 = (f32[704,128]{1,0:T(8,128)S(1)}, f32[704,128]{1,0:T(8,128)S(1)}, u32[]{:S(2)}, u32[]{:S(2)}) collective-permute-start(f32[704,128]{1,0:T(8,128)S(1)} %get-tuple-element.38), channel_id=1, source_target_pairs={{0,32},{32,0},{1,33},{33,1},{2,34},{34,2},{3,35},{35,3},{4,36},{36... | collective-permute-start | bytes 1081352 | tf_op jit(solution)/shard_map/ppermute | solution.py:453
  6.6 12.9 %collective-permute-start = (f32[16,128]{1,0:T(8,128)S(1)}, f32[16,128]{1,0:T(8,128)S(1)}, u32[]{:S(2)}, u32[]{:S(2)}) collective-permute-start(f32[16,128]{1,0:T(8,128)S(1)} %get-tuple-element.30), channel_id=1, source_target_pairs={{0,32},{32,64},{64,96},{96,128},{128,160},{160,192},{192,224},{224... | collective-permute-start | bytes 24584 | tf_op jit(solution)/shard_map/ppermute | solution.py:445
  6.6 12.9 %collective-permute-start.1 = (f32[16,128]{1,0:T(8,128)S(1)}, f32[16,128]{1,0:T(8,128)S(1)}, u32[]{:S(2)}, u32[]{:S(2)}) collective-permute-start(f32[16,128]{1,0:T(8,128)S(1)} %get-tuple-element.31), channel_id=1, source_target_pairs={{0,224},{32,0},{64,32},{96,64},{128,96},{160,128},{192,160},{224,1... | collective-permute-start | bytes 24584 | tf_op jit(solution)/shard_map/ppermute | solution.py:445
  7.1 12.4 %collective-permute-start.2 = (f32[16,128]{1,0:T(8,128)S(1)}, f32[16,128]{1,0:T(8,128)S(1)}, u32[]{:S(2)}, u32[]{:S(2)}) collective-permute-start(f32[16,128]{1,0:T(8,128)S(1)} %get-tuple-element.32), channel_id=1, source_target_pairs={{0,1},{1,2},{2,3},{3,4},{4,5},{5,6},{6,7},{7,8},{8,9},{9,10},{10,1... | collective-permute-start | bytes 24584 | tf_op jit(solution)/shard_map/ppermute | solution.py:445
  12.5 7.0 %collective-permute-start.3 = (f32[16,128]{1,0:T(8,128)S(1)}, f32[16,128]{1,0:T(8,128)S(1)}, u32[]{:S(2)}, u32[]{:S(2)}) collective-permute-start(f32[16,128]{1,0:T(8,128)S(1)} %get-tuple-element.33), channel_id=1, source_target_pairs={{0,31},{1,0},{2,1},{3,2},{4,3},{5,4},{6,5},{7,6},{8,7},{9,8},{10,9... | collective-permute-start | bytes 24584 | tf_op jit(solution)/shard_map/ppermute | solution.py:445
  50.3 28.2 %all-to-all-start.1 = ((f32[128,1,768]{2,1,0:T(1,128)}), f32[128,1,768]{2,1,0:T(1,128)S(1)}, u32[]{:S(2)}, u32[]{:S(2)}) async-start(f32[128,1,768]{2,1,0:T(1,128)} %bitcast.3), calls=%async_computation.1 | async-start | bytes 786432 | tf_op jit(solution)/shard_map/all_to_all | solution.py:457
  57.2 16.6 %collective-permute-start.5 = (f32[16,128]{1,0:T(8,128)S(1)}, f32[16,128]{1,0:T(8,128)S(1)}, u32[]{:S(2)}, u32[]{:S(2)}) collective-permute-start(f32[16,128]{1,0:T(8,128)S(1)} %get-tuple-element.40), channel_id=1, source_target_pairs={{0,1},{1,2},{2,3},{3,4},{4,5},{5,6},{6,7},{7,8},{8,9},{9,10},{10,1... | collective-permute-start | bytes 24584 | tf_op jit(solution)/shard_map/ppermute | solution.py:445
  61.7 12.1 %collective-permute-start.6 = (f32[16,128]{1,0:T(8,128)S(1)}, f32[16,128]{1,0:T(8,128)S(1)}, u32[]{:S(2)}, u32[]{:S(2)}) collective-permute-start(f32[16,128]{1,0:T(8,128)S(1)} %get-tuple-element.41), channel_id=1, source_target_pairs={{0,31},{1,0},{2,1},{3,2},{4,3},{5,4},{6,5},{7,6},{8,7},{9,8},{10,9... | collective-permute-start | bytes 24584 | tf_op jit(solution)/shard_map/ppermute | solution.py:445
  66.8 7.7 %collective-permute-start.7 = (f32[16,128]{1,0:T(8,128)S(1)}, f32[16,128]{1,0:T(8,128)S(1)}, u32[]{:S(2)}, u32[]{:S(2)}) collective-permute-start(f32[16,128]{1,0:T(8,128)S(1)} %get-tuple-element.42), channel_id=1, source_target_pairs={{0,32},{32,64},{64,96},{96,128},{128,160},{160,192},{192,224},{224... | collective-permute-start | bytes 24584 | tf_op jit(solution)/shard_map/ppermute | solution.py:445
  73.8 3.4 %collective-permute-start.8 = (f32[16,128]{1,0:T(8,128)S(1)}, f32[16,128]{1,0:T(8,128)S(1)}, u32[]{:S(2)}, u32[]{:S(2)}) collective-permute-start(f32[16,128]{1,0:T(8,128)S(1)} %get-tuple-element.43), channel_id=1, source_target_pairs={{0,224},{32,0},{64,32},{96,64},{128,96},{160,128},{192,160},{224,1... | collective-permute-start | bytes 24584 | tf_op jit(solution)/shard_map/ppermute | solution.py:445
  77.1 2.2 %copy-start = (bf16[1408,256]{1,0:T(8,128)(2,1)S(1)}, bf16[1408,256]{1,0:T(8,128)(2,1)}, u32[]{:S(2)}) copy-start(bf16[1408,256]{1,0:T(8,128)(2,1)} %get-tuple-element.46.high_ref) | copy-start | bytes 2162692
  77.1 2.2 %copy-start.1 = (bf16[1408,256]{1,0:T(8,128)(2,1)S(1)}, bf16[1408,256]{1,0:T(8,128)(2,1)}, u32[]{:S(2)}) copy-start(bf16[1408,256]{1,0:T(8,128)(2,1)} %get-tuple-element.47.low_ref) | copy-start | bytes 2162692
  78.5 2.1 %collective-permute-start.9 = (f32[768,128]{1,0:T(8,128)S(1)}, f32[768,128]{1,0:T(8,128)S(1)}, u32[]{:S(2)}, u32[]{:S(2)}) collective-permute-start(f32[768,128]{1,0:T(8,128)S(1)} %bitcast.6), channel_id=1, source_target_pairs={{0,32},{32,0},{1,33},{33,1},{2,34},{34,2},{3,35},{35,3},{4,36},{36... | collective-permute-start | bytes 1179656 | tf_op jit(solution)/shard_map/ppermute | solution.py:453
